TPU v7x, 32 devices: a whole 2x2x4 slice. The times are simulated.
32 devices in a mesh: seq: 16 (over z, y, x), dp: 2 (over core).
Axes of the slice: x: 2, y: 2, z: 4, core: 2. Of those that a mesh axis runs over, the one named last changes fastest.
Arguments:
- inputs: bfloat16 [8, 1536, 896], P('dp', 'seq'), may hold values from -6 to 6
- lengths: int32 [8, 9], P('dp'), may hold values from 0 to 1536, as said below
- w_qkv: bfloat16 [896, 1152], replicated, may hold values from -0.1875 to 0.1875
- b_qkv: bfloat16 [1152], replicated, may hold values from -3 to 3
- g_attn: bfloat16 [896], replicated, may hold values from 0.25 to 1.75
- w_out: bfloat16 [896, 896], replicated, may hold values from -1.5 to 1.5
- g_mlp: bfloat16 [896], replicated, may hold values from 0.25 to 1.75
- w_gate_up: bfloat16 [896, 9728], replicated, may hold values from -0.1875 to 0.1875
- w_down: bfloat16 [4864, 896], replicated, may hold values from -0.078125 to 0.078125
- cotangent: bfloat16 [8, 1536, 896], P('dp', 'seq'), may hold values from -6 to 6
Outputs:
- output: bfloat16 [8, 1536, 896], P('dp', 'seq')
- grad_input: float32 [8, 1536, 896], P('dp', 'seq')
- grad_qkv: float32 [896, 1152], P('seq')
- grad_bias_qkv: float32 [1152], replicated
- grad_norm_attn: float32 [896], replicated
- grad_out: float32 [896, 896], P('seq')
- grad_norm_mlp: float32 [896], replicated
- grad_gate_up: float32 [896, 9728], P('seq')
- grad_down: float32 [4864, 896], P('seq')
Inputs may be any that keep to these rules, and one draw needn't show every extreme that they name: Each row lists the lengths of the documents packed one after another from the start of a stream; nonzero entries come first, and the tokens after their sum, fewer than 96, are padding. In every group of 4 consecutive rows one row is a single document of 1536 tokens; any other document has at most 4096 tokens.
All inputs are finite; a program needn't handle non-finite values.
Results may differ from a plain program's by a relative error of at most 0.014.
Values may be sent and summed in bfloat16 or wider, within the bound.
No kernel may reach another device: no remote copies, remote signals or barrier semaphores. Data moves between devices by JAX's collectives and lax.ppermute only.
A program may use at most 576 MiB of HBM per device.

v0:
```python
import functools

import jax
import jax.numpy as jnp
import numpy as np
from jax import lax
from jax.experimental import pallas as pl
from jax.experimental.pallas import tpu as pltpu
from jax.sharding import Mesh
from jax.sharding import PartitionSpec as P

HEADS = 14
KVH = 2
HD = 64
FF = 4864
QW = HEADS * HD
KW = KVH * HD
LANES = 128
GROUP = 8
CHUNK = 256
NEG = -1e30
epsilon = 1e-06
rope_base = 1000000.0
BF = jnp.bfloat16
F32 = jnp.float32
SEQ = ("az", "ay", "ax")

SAME = [h for h in range(HEADS) if h % 2 == h // (HEADS // KVH)]
OTHER = [h for h in range(HEADS) if h % 2 != h // (HEADS // KVH)]


def nt(a, b):
    return lax.dot_general(a, b, (((1,), (1,)), ((), ())), preferred_element_type=F32)


def tn(a, b):
    return lax.dot_general(a, b, (((0,), (0,)), ((), ())), preferred_element_type=F32)


def nn(a, b):
    return lax.dot_general(a, b, (((1,), (0,)), ((), ())), preferred_element_type=F32)


def lane_iota(shape):
    return lax.broadcasted_iota(jnp.int32, shape, len(shape) - 1)


def half_swap(tile):
    low = lane_iota(tile.shape) % HD < HD // 2
    return jnp.where(low, pltpu.roll(tile, LANES - HD // 2, 1), pltpu.roll(tile, HD // 2, 1))


def cost(us):
    return pl.CostEstimate(flops=int(us * 1e6 * 90), bytes_accessed=1 << 16, transcendentals=0)


def params(limit=56):
    return pltpu.CompilerParams(vmem_limit_bytes=limit << 20)


def turn(part, cos, sin):
    return part * cos + half_swap(part) * sin


def project_kv_kernel(x_ref, w_ref, b_ref, g_ref, cos_ref, sin_ref, normed_ref, k_ref, v_ref):
    step = pl.program_id(0)

    @pl.when(step == 0)
    def _():
        x = x_ref[...].astype(F32)
        inv = lax.rsqrt(jnp.mean(x * x, axis=-1, keepdims=True) + epsilon)
        normed_ref[...] = (x * inv * g_ref[...].astype(F32)).astype(BF)

    part = nn(normed_ref[...], w_ref[...]) + b_ref[...].astype(F32)

    @pl.when(step == 0)
    def _():
        k_ref[...] = turn(part, cos_ref[...], sin_ref[...]).astype(BF)

    @pl.when(step == 1)
    def _():
        v_ref[...] = part.astype(BF)


def project_kv(x, w, b, g, cos, sin):
    tokens, width = x.shape
    fixed = lambda *shape: pl.BlockSpec(shape, lambda i: (0, 0))
    return pl.pallas_call(
        project_kv_kernel,
        grid=(2,),
        in_specs=[
            fixed(tokens, width),
            pl.BlockSpec((width, KW), lambda i: (0, QW // KW + i)),
            pl.BlockSpec((1, KW), lambda i: (0, QW // KW + i)),
            fixed(1, width),
            fixed(tokens, LANES),
            fixed(tokens, LANES),
        ],
        out_specs=[fixed(tokens, width), fixed(tokens, KW), fixed(tokens, KW)],
        out_shape=(
            jax.ShapeDtypeStruct((tokens, width), BF),
            jax.ShapeDtypeStruct((tokens, KW), BF),
            jax.ShapeDtypeStruct((tokens, KW), BF),
        ),
        compiler_params=params(),
        cost_estimate=cost(3),
        name="project_kv",
    )(x, w, b, g, cos, sin)


def project_q_kernel(normed_ref, w_ref, b_ref, cos_ref, sin_ref, q_ref):
    normed = normed_ref[...]
    cos = cos_ref[...]
    sin = sin_ref[...]
    for first in range(0, QW, 2 * LANES):
        cols = slice(first, min(first + 2 * LANES, QW))
        both = nn(normed, w_ref[:, cols]) + b_ref[:, cols].astype(F32)
        for at in range(0, both.shape[1], LANES):
            part = turn(both[:, at : at + LANES], cos, sin) * HD**-0.5
            q_ref[:, first + at : first + at + LANES] = part.astype(BF)


def project_q(normed, w, b, cos, sin):
    tokens, width = normed.shape
    return pl.pallas_call(
        project_q_kernel,
        out_shape=jax.ShapeDtypeStruct((tokens, QW), BF),
        compiler_params=params(),
        cost_estimate=cost(4),
        name="project_q",
    )(normed, w, b, cos, sin)


def masked_heads(ref, heads, scratch, rows):
    lane = lane_iota((rows, LANES))
    for slot, h in enumerate(heads):
        pair = ref[0, :, h // 2 * LANES : h // 2 * LANES + LANES]
        keep = (lane >= HD) if h % 2 else (lane < HD)
        scratch[slot * rows : (slot + 1) * rows, :LANES] = jnp.where(keep, pair, jnp.zeros_like(pair))


def swapped(a):
    return jnp.concatenate([a[:, HD:], a[:, :HD]], 1)


def chunks(width):
    return [slice(at, min(at + CHUNK, width)) for at in range(0, width, CHUNK)]


def allowed_pairs(start_ref, first, keys, cols):
    index = first + lax.broadcasted_iota(jnp.int32, (keys, cols.stop - cols.start), 0)
    return (index <= start_ref[0, 1:2, cols]) & (index >= start_ref[0, 0:1, cols])


def gathered(ref, spot_ref, which, j):
    return jnp.concatenate([ref[spot_ref[which, j * GROUP + i], 0] for i in range(GROUP)], 0)


def forward_kernel(low_ref, me_ref, spot_ref, q_ref, k_ref, v_ref, start_ref, out_ref, lse_ref, qa, qb, ma, la, oa, mb, lb, ob, weights):
    rows = q_ref.shape[1]
    stream = pl.program_id(0)
    me = me_ref[0]
    masked_heads(q_ref, SAME, qa, rows)
    masked_heads(q_ref, OTHER, qb, rows)
    for m, l, o in ((ma, la, oa), (mb, lb, ob)):
        m[...] = jnp.full_like(m, NEG)
        l[...] = jnp.zeros_like(l)
        o[...] = jnp.zeros_like(o)
    keys = GROUP * rows

    def step(j, carry):
        key = gathered(k_ref, spot_ref, 0, j)
        value = gathered(v_ref, spot_ref, 1, j)
        for swap, q, m, l, o in ((False, qa, ma, la, oa), (True, qb, mb, lb, ob)):
            width = q.shape[0]
            k = swapped(key) if swap else key
            v = swapped(value) if swap else value
            for cols in chunks(width):
                s = jnp.where(allowed_pairs(start_ref, j * keys, keys, cols), nt(k, q[cols]), NEG)
                before = m[:, cols]
                top = jnp.maximum(before, jnp.max(s, axis=0, keepdims=True))
                p = jnp.exp(s - top)
                shrink = jnp.exp(before - top)
                m[:, cols] = top
                l[:, cols] = l[:, cols] * shrink + jnp.sum(p, axis=0, keepdims=True)
                o[:, cols] = o[:, cols] * shrink
                weights[:, cols] = p.astype(BF)
            o[...] += nn(v.T, weights[:, :width])
        return carry

    lax.fori_loop(low_ref[stream], me // GROUP + 1, step, 0)
    lane = lane_iota((rows, LANES))
    parts = {}
    for row, (heads, m, l, o) in enumerate(((SAME, ma, la, oa), (OTHER, mb, lb, ob))):
        total = l[...]
        flat = (o[...] / total).T
        lse_ref[0, row : row + 1, : total.shape[1]] = m[...] + jnp.log(total)
        for slot, h in enumerate(heads):
            parts[h] = flat[slot * rows : (slot + 1) * rows]
    for pair in range(HEADS // 2):
        both = jnp.where(lane < HD, parts[2 * pair], parts[2 * pair + 1])
        out_ref[0, :, pair * LANES : (pair + 1) * LANES] = both.astype(BF)


def attend(q, k_all, v_all, start_rows, low, me, spots):
    streams, rows, width = q.shape
    n = k_all.shape[0]
    a, b = len(SAME) * rows, len(OTHER) * rows
    tok = lambda w: pl.BlockSpec((1, rows, w), lambda s, *_: (s, 0, 0))
    two = pl.BlockSpec((1, 2, a), lambda s, *_: (s, 0, 0))
    return pl.pallas_call(
        forward_kernel,
        grid_spec=pltpu.PrefetchScalarGridSpec(
            num_scalar_prefetch=3,
            grid=(streams,),
            in_specs=[tok(width), *[pl.BlockSpec((n, 1, rows, KW), lambda s, *_: (0, s, 0, 0))] * 2, two],
            out_specs=[tok(width), two],
            scratch_shapes=[
                pltpu.VMEM((a, LANES), BF),
                pltpu.VMEM((b, LANES), BF),
                pltpu.VMEM((1, a), F32),
                pltpu.VMEM((1, a), F32),
                pltpu.VMEM((LANES, a), F32),
                pltpu.VMEM((1, b), F32),
                pltpu.VMEM((1, b), F32),
                pltpu.VMEM((LANES, b), F32),
                pltpu.VMEM((GROUP * rows, a), BF),
            ],
        ),
        out_shape=(
            jax.ShapeDtypeStruct((streams, rows, width), BF),
            jax.ShapeDtypeStruct((streams, 2, a), F32),
        ),
        compiler_params=params(),
        cost_estimate=cost(18),
        name="attend",
    )(low, me, spots, q, k_all, v_all, start_rows)


def three_parts(column):
    high = column.astype(BF)
    rest = column - high.astype(F32)
    middle = rest.astype(BF)
    return high, middle, (rest - middle.astype(F32)).astype(BF)


def put_column(scratch, at, column, rows):
    lane = lane_iota((rows, LANES))
    out = jnp.zeros((rows, LANES), F32)
    for i, piece in enumerate(three_parts(column)):
        out = jnp.where(lane == i, piece.astype(F32), out)
    scratch[at, LANES:] = out.astype(BF)


def backward_kernel(
    first, low_ref, me_ref, spot_ref, q_ref, k_ref, v_ref, start_ref, lse_ref, mixed_ref, grad_ref, cos_ref, sin_ref, dq_ref, dkk_ref,
    dks_ref, dvk_ref, dvs_ref, qa, qb, ga, gb, ta, tb, dk_all, dv_all, weights, grads,
):
    rows = q_ref.shape[1]
    stream = first + pl.program_id(0)
    me = me_ref[0]
    masked_heads(q_ref, SAME, qa, rows)
    masked_heads(q_ref, OTHER, qb, rows)
    masked_heads(grad_ref, SAME, ga, rows)
    masked_heads(grad_ref, OTHER, gb, rows)
    lane = lane_iota((rows, LANES))
    for heads, g in ((SAME, ga), (OTHER, gb)):
        for slot, h in enumerate(heads):
            at = slice(slot * rows, (slot + 1) * rows)
            cols = slice(h // 2 * LANES, h // 2 * LANES + LANES)
            keep = (lane >= HD) if h % 2 else (lane < HD)
            product = grad_ref[0, :, cols].astype(F32) * mixed_ref[0, :, cols].astype(F32)
            delta = jnp.sum(jnp.where(keep, product, 0.0), axis=-1, keepdims=True)
            put_column(g, at, -delta, rows)
    ta[...] = jnp.zeros_like(ta)
    tb[...] = jnp.zeros_like(tb)
    dk_all[...] = jnp.zeros_like(dk_all)
    dv_all[...] = jnp.zeros_like(dv_all)
    keys = GROUP * rows
    ones = (lane_iota((keys, LANES)) < 3).astype(F32).astype(BF)

    def step(j, carry):
        key = gathered(k_ref, spot_ref, 0, j)
        value = gathered(v_ref, spot_ref, 1, j)
        grad_keys = []
        grad_values = []
        for row, (q, g, t) in enumerate(((qa, ga, ta), (qb, gb, tb))):
            width = q.shape[0]
            k = swapped(key) if row else key
            v = jnp.concatenate([swapped(value) if row else value, ones], 1)
            for cols in chunks(width):
                s = nt(k, q[cols]) - lse_ref[0, row : row + 1, cols]
                p = jnp.exp(jnp.where(allowed_pairs(start_ref, j * keys, keys, cols), s, NEG))
                weights[:, cols] = p.astype(BF)
                grads[:, cols] = (p * nt(v, g[cols])).astype(BF)
            grad_values.append(nn(weights[:, :width], g[:, :LANES]))
            grad_keys.append(nn(grads[:, :width], q[...]))
            t[...] += nn(k.T, grads[:, :width])
        for out_ref, (same, other) in ((dk_all, grad_keys), (dv_all, grad_values)):
            total = (same + swapped(other)).astype(BF)
            out_ref[pl.ds(j * GROUP, GROUP)] = total.reshape(GROUP, rows, KW)
        return carry

    lax.fori_loop(low_ref[stream], me // GROUP + 1, step, 0)
    half = dkk_ref.shape[0]
    for which, (keep_ref, send_ref, out_ref) in enumerate(((dkk_ref, dks_ref, dk_all), (dvk_ref, dvs_ref, dv_all))):
        for spot in range(half):
            keep_ref[spot, 0] = out_ref[spot_ref[2 + which, spot]]
            send_ref[spot, 0] = out_ref[spot_ref[2 + which, half + spot]]
    parts = {}
    for heads, t in ((SAME, ta), (OTHER, tb)):
        flat = t[...].T
        for slot, h in enumerate(heads):
            parts[h] = flat[slot * rows : (slot + 1) * rows]
    cos = cos_ref[0]
    sin = sin_ref[0]
    for pair in range(HEADS // 2):
        both = jnp.where(lane < HD, parts[2 * pair], parts[2 * pair + 1]) * HD**-0.5
        dq_ref[0, :, pair * LANES : (pair + 1) * LANES] = (both * cos - half_swap(both) * sin).astype(BF)


def attend_back(first, streams, q, k_all, v_all, start_rows, low, me, spots, lse, mixed, grad, cos, sin):
    rows, width = q.shape[1:]
    n = k_all.shape[0]
    a, b = len(SAME) * rows, len(OTHER) * rows
    tok = lambda w: pl.BlockSpec((1, rows, w), lambda s, *_: (s + first, 0, 0))
    two = pl.BlockSpec((1, 2, a), lambda s, *_: (s + first, 0, 0))
    key_spec = pl.BlockSpec((n // 2, 1, rows, KW), lambda s, *_: (0, s, 0, 0))
    return pl.pallas_call(
        functools.partial(backward_kernel, first),
        grid_spec=pltpu.PrefetchScalarGridSpec(
            num_scalar_prefetch=3,
            grid=(streams,),
            in_specs=[
                tok(width),
                *[pl.BlockSpec((n, 1, rows, KW), lambda s, *_: (0, s + first, 0, 0))] * 2,
                two,
                two,
                tok(width),
                tok(width),
                tok(LANES),
                tok(LANES),
            ],
            out_specs=[pl.BlockSpec((1, rows, width), lambda s, *_: (s, 0, 0)), *[key_spec] * 4],
            scratch_shapes=[
                pltpu.VMEM((a, LANES), BF),
                pltpu.VMEM((b, LANES), BF),
                pltpu.VMEM((a, 2 * LANES), BF),
                pltpu.VMEM((b, 2 * LANES), BF),
                pltpu.VMEM((LANES, a), F32),
                pltpu.VMEM((LANES, b), F32),
                *[pltpu.VMEM((n, rows, KW), BF)] * 2,
                *[pltpu.VMEM((GROUP * rows, a), BF)] * 2,
            ],
        ),
        out_shape=(
            jax.ShapeDtypeStruct((streams, rows, width), BF),
            *[jax.ShapeDtypeStruct((n // 2, streams, rows, KW), BF)] * 4,
        ),
        compiler_params=params(),
        cost_estimate=cost(8 * streams),
        name="attend_back",
    )(low, me, spots, q, k_all, v_all, start_rows, lse, mixed, grad, cos, sin)


TILE = 256


def mlp_kernel(
    valid, mine_ref, theirs_ref, sm_ref, st_ref, og_ref, ou_ref, wg_ref, wu_ref, wd_ref, om_ref, ot_ref, bm_ref, bt_ref,
    td_ref, gk_ref, gs_ref, uk_ref, us_ref, n_ref, s_ref, ng_ref, nu_ref,
):
    rows = mine_ref.shape[0]
    step = pl.program_id(0)
    sums = (om_ref, ot_ref, bm_ref, bt_ref)

    @pl.when(step == 0)
    def _():
        n_ref[:rows] = mine_ref[...]
        n_ref[rows:] = theirs_ref[...]
        s_ref[:rows] = sm_ref[...]
        s_ref[rows:] = st_ref[...]
        ng_ref[...] = nt(og_ref[...], n_ref[...]).astype(BF)
        nu_ref[...] = nt(ou_ref[...], n_ref[...]).astype(BF)
        for ref in sums:
            ref[...] = jnp.zeros_like(ref)

    normed = n_ref[...]
    seed = s_ref[...]
    left = valid - step * TILE
    inside = lambda w, dim: jnp.where(lax.broadcasted_iota(jnp.int32, w.shape, dim) < left, w, jnp.zeros_like(w))
    wg, wu, wd = inside(wg_ref[...], 1), inside(wu_ref[...], 1), inside(wd_ref[...], 0)
    gate = nn(normed, wg)
    up = nn(normed, wu)
    grad = nt(seed, wd)
    sig = 1.0 / (1.0 + jnp.exp(-gate))
    silu = gate * sig
    active = (silu * up).astype(BF)
    grad_up = (grad * silu).astype(BF)
    grad_gate = (grad * up * (sig * (1.0 + gate * (1.0 - sig)))).astype(BF)
    td_ref[...] = tn(active, seed).astype(BF)
    half = gk_ref.shape[0]
    for turned, grad_pre, keep, send in ((ng_ref, grad_gate, gk_ref, gs_ref), (nu_ref, grad_up, uk_ref, us_ref)):
        term = nn(turned[...], grad_pre).astype(BF)
        keep[...] = term[:half]
        send[...] = term[half:]
    out = nn(active, wd)
    back = nt(grad_gate, wg) + nt(grad_up, wu)
    for ref, part in zip(sums, (out[:rows], out[rows:], back[:rows], back[rows:])):
        ref[...] += part


def fixed(*shape):
    return pl.BlockSpec(shape, lambda *_: (0,) * len(shape))


def shaped(dtype, *dims):
    return jax.ShapeDtypeStruct(dims, dtype)


def mlp(mine, theirs, seed_mine, seed_theirs, order_gate, order_up, w_gate, w_up, w_d):
    rows, width = mine.shape
    half = w_gate.shape[1]
    cols = lambda size: pl.BlockSpec((size, TILE), lambda i: (0, i))
    down = pl.BlockSpec((TILE, width), lambda i: (i, 0))
    part = fixed(rows, width)
    return pl.pallas_call(
        functools.partial(mlp_kernel, half),
        grid=(pl.cdiv(half, TILE),),
        in_specs=[part] * 4 + [fixed(width, width)] * 2 + [cols(width)] * 2 + [down],
        out_specs=[part] * 4 + [down] + [cols(width // 2)] * 4,
        out_shape=[shaped(F32, rows, width)] * 4 + [shaped(BF, half, width)] + [shaped(BF, width // 2, half)] * 4,
        scratch_shapes=[pltpu.VMEM((2 * rows, width), BF)] * 2 + [pltpu.VMEM((width, 2 * rows), BF)] * 2,
        compiler_params=params(),
        cost_estimate=cost(40),
        name="mlp",
    )(mine, theirs, seed_mine, seed_theirs, order_gate, order_up, w_gate, w_up, w_d)


def middle_kernel(bm_ref, bt_ref, middle_ref, seed_ref, g_ref, w_ref, gm_ref, gb_ref, gx_ref, gain_ref):
    @pl.when(pl.program_id(0) == 0)
    def _():
        gain_ref[...] = jnp.zeros_like(gain_ref)

    grad = bm_ref[...] + bt_ref[...]
    middle = middle_ref[...]
    inv = lax.rsqrt(jnp.mean(middle * middle, axis=-1, keepdims=True) + epsilon)
    unit = middle * inv
    scaled = grad * g_ref[...].astype(F32)
    grad_middle = seed_ref[...].astype(F32) + inv * (scaled - unit * jnp.mean(scaled * unit, axis=-1, keepdims=True))
    gm_ref[...] = grad_middle
    branch = grad_middle.astype(BF)
    gb_ref[...] = branch
    gx_ref[...] = nt(branch, w_ref[...]).astype(BF)
    gain_ref[...] += jnp.sum(grad * unit, axis=0, keepdims=True)


def middle_back(mine, theirs, middle, seed, gain, w_out):
    tokens, width = middle.shape
    rows = tokens // 4
    part = pl.BlockSpec((rows, width), lambda i: (i, 0))
    return pl.pallas_call(
        middle_kernel,
        grid=(4,),
        in_specs=[part] * 4 + [fixed(1, width), fixed(width, width)],
        out_specs=[part] * 3 + [fixed(1, width)],
        out_shape=[shaped(F32, tokens, width), shaped(BF, tokens, width), shaped(BF, tokens, width), shaped(F32, 1, width)],
        compiler_params=params(),
        cost_estimate=cost(5),
        name="middle_back",
    )(mine, theirs, middle, seed, gain, w_out)


def attention_terms_kernel(core_ref, normed_ref, mixed_ref, gq_ref, gb_ref, order_ref, sent_ref, kept_ref):
    first = core_ref[0] == 0
    order = order_ref[...]
    pick = lambda flag, a, b: jnp.where(jnp.broadcast_to(flag, a.shape), a[...], b[...])
    for out_ref, flag in ((sent_ref, first), (kept_ref, jnp.logical_not(first))):
        left = nt(order, pick(flag, normed_ref, mixed_ref)).astype(BF)
        out_ref[...] = nn(left, pick(flag, gq_ref, gb_ref)).astype(BF)


def attention_terms(core, normed, mixed, grad_q, grad_branch, order):
    width = normed.shape[1]
    whole = pl.BlockSpec(memory_space=pltpu.VMEM)
    return pl.pallas_call(
        attention_terms_kernel,
        in_specs=[pl.BlockSpec(memory_space=pltpu.SMEM)] + [whole] * 5,
        out_specs=[whole] * 2,
        out_shape=[shaped(BF, width, width)] * 2,
        compiler_params=params(),
        cost_estimate=cost(5),
        name="attention_terms",
    )(core, normed, mixed, grad_q, grad_branch, order)


def last_kernel(gkv_ref, gq_ref, w_ref, x_ref, g_ref, cos_ref, sin_ref, nt_ref, gm_ref, gain_ref, gi_ref, term_ref,
                sums_ref):
    grads = gkv_ref[...]
    keys = grads[:, :KW].astype(F32)
    keys = (keys * cos_ref[...] - half_swap(keys) * sin_ref[...]).astype(BF)
    grad_kv = jnp.concatenate([keys, grads[:, KW:]], 1)
    term_ref[...] = nn(nt_ref[...], grad_kv).astype(BF)
    grad = nt(gq_ref[...], w_ref[:, :QW]) + nt(grad_kv, w_ref[:, QW:])
    x = x_ref[...].astype(F32)
    inv = lax.rsqrt(jnp.mean(x * x, axis=-1, keepdims=True) + epsilon)
    unit = x * inv
    scaled = grad * g_ref[...].astype(F32)
    gi_ref[...] = gm_ref[...] + inv * (scaled - unit * jnp.mean(scaled * unit, axis=-1, keepdims=True))
    over = lambda a: jnp.sum(a.astype(F32), axis=0, keepdims=True)
    at = 0
    for row in (over(gq_ref[...]), over(grad_kv), over(grad * unit), gain_ref[...]):
        sums_ref[:, at : at + row.shape[1]] = row
        at += row.shape[1]


def last_back(grads, grad_q, w_qkv, x, gain, cos, sin, normed_t, grad_middle, gain_mlp_part):
    tokens, width = x.shape
    return pl.pallas_call(
        last_kernel,
        out_shape=[
            shaped(F32, tokens, width),
            shaped(BF, width, 2 * KW),
            shaped(F32, 1, QW + 2 * KW + 2 * width),
        ],
        compiler_params=params(),
        cost_estimate=cost(6),
        name="last_back",
    )(grads, grad_q, w_qkv, x, gain, cos, sin, normed_t, grad_middle, gain_mlp_part)


def after(a, *others):
    return lax.optimization_barrier((a, others))[0]


class Order:
    def __init__(self, token):
        self.token = token

    def enter(self, inputs):
        return lax.optimization_barrier((inputs, self.token))[0]

    def __call__(self, step, *inputs):
        self.token = step(*self.enter(inputs))
        return self.token


def other_core(a):
    return lax.ppermute(a, "dp", [(0, 1), (1, 0)])


def pair_up(a, axis, step):
    return lax.ppermute(a, axis, [(i, i ^ step) for i in range(lax.axis_size(axis))])


def total(terms):
    return functools.reduce(lambda a, b: a + b, [a.astype(F32) for a in terms]).astype(BF)


def add(a, b):
    return total((a, b))


Z, Y, X = SEQ
X_FIRST = ((X, 1), (Y, 1), (Z, 1), (Z, 2))
Y_FIRST = ((Y, 1), (X, 1), (Z, 1), (Z, 2))
Z_FIRST = ((Z, 1), (Z, 2), (X, 1), (Y, 1))
KEY_GATHER = ((Y, 1), (X, 1), (Z, 2), (Z, 1))
VALUE_GATHER = X_FIRST


def halving():
    return [lax.axis_size(axis) for axis in SEQ] == [4, 2, 2]


def my_bit(axis, step):
    return (lax.axis_index(axis) // step) % 2


def device_at(order, spot, relative):
    place = 0
    weight = {(X, 1): 1, (Y, 1): 2, (Z, 1): 4, (Z, 2): 8}
    for i, (axis, step) in enumerate(order):
        bit = (spot >> (len(order) - 1 - i)) & 1
        if relative:
            bit = bit ^ my_bit(axis, step)
        place = place + bit * weight[axis, step]
    return place


def spots_of_devices(order):
    n = lax.axis_size(SEQ)
    if not halving():
        return jnp.arange(n)
    spots = jnp.arange(n)
    return jnp.sum(jnp.where(device_at(order, spots, True)[:, None] == spots[None, :], spots[:, None], 0), 0)


def devices_at_spots(order):
    n = lax.axis_size(SEQ)
    return device_at(order, jnp.arange(n), True) if halving() else jnp.arange(n)


def row_order(order, width):
    n = lax.axis_size(SEQ)
    row = jnp.arange(width)
    source = row
    if halving():
        source = device_at(order, row // (width // n), True) * (width // n) + row % (width // n)
    return (source[:, None] == jnp.arange(width)[None, :]).astype(BF)


class Halving:
    def __init__(self, steps, arrays, rows, order=None, send=None):
        self.steps = list(steps)
        self.arrays = list(arrays)
        self.firsts = [0] * len(self.arrays)
        self.rows = rows
        if send is None:
            self.go(order)
        else:
            self.move(send)

    def halves(self):
        return 0, self.rows

    def move(self, send):
        self.arrays.append(pair_up(send, *self.steps.pop(0)))
        self.firsts.append(0)

    def sum(self, offset):
        cut = lambda a, first: lax.dynamic_slice_in_dim(a, first + offset, self.rows, 0)
        return total([cut(a, first) for a, first in zip(self.arrays, self.firsts)])

    def go(self, order):
        self.arrays = list(order.enter(self.arrays))
        if not self.steps:
            order.token = self.sum(0)
            return order.token
        self.rows //= 2
        kept, sent = self.halves()
        send = order.token = self.sum(sent)
        self.firsts = [first + kept for first in self.firsts]
        self.move(send)


class PlacedHalving(Halving):
    def halves(self):
        bit = my_bit(*self.steps[0])
        return bit * self.rows, (1 - bit) * self.rows


class PairHalving:
    def __init__(self, a_keep, a_send, b_keep, b_send, orders=(X_FIRST, Y_FIRST)):
        rows = a_keep.shape[0]
        self.pair = [
            Halving(orders[0][:2], [a_keep], rows, send=a_send),
            Halving(orders[1][:2], [b_keep], rows, send=b_send),
        ]
        self.last = orders[0][2:]
        self.count = 0

    def go(self, order, which=None):
        if which is not None:
            return self.pair[which].go(order)
        self.count += 1
        a, b = self.pair
        if self.count == 1:
            a.arrays, b.arrays = order.enter((list(a.arrays), list(b.arrays)))
            both = order.token = jnp.concatenate([a.sum(0), b.sum(0)], 1)
            half = both.shape[0] // 2
            self.rest = Halving(self.last, [both], half, send=both[half:])
        else:
            return self.rest.go(order)


def reduce_rows(a):
    return lax.psum_scatter(a, SEQ, scatter_dimension=0, tiled=True)


class Doubling:
    def __init__(self, order, a):
        self.steps = list(reversed(order))
        self.all = a[None]
        self.got = pair_up(self.all, *self.steps.pop(0))

    def go(self, order):
        self.all = order(lambda a, b: jnp.concatenate([a, b], 0), self.all, self.got)
        if self.steps:
            self.got = pair_up(self.all, *self.steps.pop(0))
        return self.all


def to_owner(a, order):
    n = lax.axis_size(SEQ)
    holder = [device_at(order, spot, False) for spot in range(n)] if halving() else list(range(n))
    pairs = [(holder[spot] * 2 + core, core * n + spot) for spot in range(n) for core in range(2)]
    return lax.ppermute(a, (*SEQ, "dp"), pairs)


def sum_over_all(a):
    for axis in ("dp", *SEQ[::-1]):
        size = lax.axis_size(axis)
        step = 1
        while step < size:
            a = a + lax.ppermute(a, axis, [(i, i ^ step) for i in range(size)])
            step *= 2
    return a


def layout(lengths, offset, row_count):
    places = offset + jnp.arange(row_count, dtype=jnp.int32)
    slots = jnp.arange(lengths.shape[1])
    ends = jnp.sum(jnp.where(slots[:, None] <= slots[None, :], lengths[:, :, None], 0), axis=1)
    after = (places[None, :, None] >= ends[:, None, :]).astype(jnp.int32)
    begins = jnp.sum(after * lengths[:, None, :], axis=-1, dtype=jnp.int32)
    return (places, begins, places[None, :] < ends[:, -1:])


def shards(inputs, lengths, w_qkv, b_qkv, g_attn, w_out, g_mlp, w_gate_up, w_down, cotangent):
    streams, length, width = inputs.shape
    tokens = streams * length
    n = 1
    for axis in SEQ:
        n *= lax.axis_size(axis)
    me = lax.axis_index(SEQ)
    core = lax.axis_index("dp")
    offset = me * length
    places, begins, valid = layout(lengths, offset, length)
    frequency = rope_base ** (-(jnp.arange(HD // 2, dtype=F32) * (2.0 / HD)))
    lane_frequency = jnp.tile(frequency, LANES // (HD // 2))
    sign = jnp.where(jnp.arange(LANES) % HD < HD // 2, -1.0, 1.0)
    angle = (places[None, :] - begins).astype(F32).reshape(tokens, 1) * lane_frequency
    cos = jnp.cos(angle)
    sin = jnp.sin(angle) * sign

    x = inputs.reshape(tokens, width)
    bias = b_qkv.reshape(1, -1)
    normed, k, v = project_kv(x, w_qkv, bias, g_attn.reshape(1, -1), cos, sin)
    k, v = k.reshape(streams, length, KW), v.reshape(streams, length, KW)
    half = FF // 2

    def small_inputs(begins):
        start_rows = jnp.stack(
            [
                jnp.tile(begins, (1, len(SAME))),
                jnp.tile(jnp.broadcast_to(places[None], begins.shape), (1, len(SAME))),
            ],
            1,
        )
        spots = jnp.stack(
            [*map(spots_of_devices, (KEY_GATHER, VALUE_GATHER)), *map(devices_at_spots, (Y_FIRST, X_FIRST))]
        ).astype(jnp.int32)
        return start_rows, spots, row_order(X_FIRST, width), row_order(Y_FIRST, width)

    cut_cols = lambda w, first: lax.dynamic_slice_in_dim(w, first + core * half, half, 1)
    cut_rows = lambda w: lax.dynamic_slice_in_dim(w, core * half, half, 0)
    fast = halving()
    order = Order(k)
    if fast:
        keys = Doubling(KEY_GATHER, k)
        values = Doubling(VALUE_GATHER, v)
        q = order(project_q, normed, w_qkv, bias, cos, sin)
        keys.go(order), values.go(order)
        seed = order(lambda c: (c * valid[..., None].astype(BF)).reshape(tokens, width), cotangent)
        w_gate = order(functools.partial(cut_cols, first=0), w_gate_up)
        keys.go(order), values.go(order)
        w_up = order(functools.partial(cut_cols, first=FF), w_gate_up)
        w_d = order(cut_rows, w_down)
        keys.go(order), values.go(order)
        seed_theirs = other_core(seed)
        start_rows, spots, order_x, order_y = order(small_inputs, begins)
        normed_t = order(lambda a, b: nt(a, b).astype(BF), order_x, normed)
        k_all, v_all = keys.go(order), values.go(order)
    else:
        k_all, v_all = lax.all_gather(k, SEQ, axis=0), lax.all_gather(v, SEQ, axis=0)
        q = project_q(normed, w_qkv, bias, cos, sin)
        seed = (cotangent * valid[..., None].astype(BF)).reshape(tokens, width)
        seed_theirs = other_core(seed)
        w_gate, w_up, w_d = cut_cols(w_gate_up, 0), cut_cols(w_gate_up, FF), cut_rows(w_down)
        start_rows, spots, order_x, order_y = small_inputs(begins)
        normed_t = nt(order_x, normed).astype(BF)
    low = begins[:, 0] // (GROUP * length)
    me_1 = jnp.reshape(me, (1,)).astype(jnp.int32)
    q = q.reshape(streams, length, QW)
    mixed, lse = attend(q, k_all, v_all, start_rows, low, me_1, spots)
    mixed_flat = mixed.reshape(tokens, QW)
    middle = x.astype(F32) + nn(mixed_flat, w_out)
    inv_mlp = lax.rsqrt(jnp.mean(middle * middle, axis=-1, keepdims=True) + epsilon)
    unit_mlp = middle * inv_mlp
    gain_mlp = g_mlp.astype(F32)
    normed_mlp = (unit_mlp * gain_mlp).astype(BF)
    normed_theirs = other_core(normed_mlp)
    out_mine, out_theirs, back_mine, back_theirs, term_down, keep_gate, send_gate, keep_up, send_up = mlp(
        normed_mlp, normed_theirs, seed, seed_theirs, order_x, order_y, w_gate, w_up, w_d
    )
    order = Order(back_mine)
    back_theirs = other_core(back_theirs)
    out_theirs = other_core(out_theirs)
    if fast:
        gate_up = PairHalving(keep_gate, send_gate, keep_up, send_up)
        down = PlacedHalving(Z_FIRST, [term_down], half, order)

    grad_middle, grad_branch, grad_mixed, gain_mlp_part = order(
        middle_back, back_mine, back_theirs, middle, seed, g_mlp.reshape(1, -1), w_out
    )
    grad_mixed = grad_mixed.reshape(streams, length, QW)

    cos_s = cos.reshape(streams, length, LANES)
    sin_s = sin.reshape(streams, length, LANES)
    back = lambda first, count: attend_back(
        first, count, q, k_all, v_all, start_rows, low, me_1, spots, lse, mixed, grad_mixed, cos_s, sin_s
    )

    core_1 = jnp.reshape(core, (1,)).astype(jnp.int32)
    gain_attn = g_attn.reshape(1, -1)

    def finish(mine, theirs, middle):
        return (middle + mine + theirs).astype(BF)

    def both_cores(mine, dim):
        theirs = other_core(mine)
        first = jnp.where(core == 0, mine, theirs)
        second = jnp.where(core == 0, theirs, mine)
        return jnp.concatenate([first, second], dim).astype(F32)

    if fast:
        per = streams // PARTS
        rows = (n // 2) * per * length
        grads_q = []
        at = {"down": down, "gu": gate_up}
        value = {}

        def back_step(which):
            grad_q, *grads = attend_back(
                per * which, per, q, k_all, v_all, start_rows, low, order.enter(me_1), spots, lse, mixed, grad_mixed, cos_s, sin_s
            )
            order.token = grad_q
            grads_q.append(grad_q.reshape(per * length, QW))
            at["keys", which] = PairHalving(*[g.reshape(rows, KW) for g in grads], orders=(Y_FIRST, X_FIRST))

        def terms_step():
            value["q"] = jnp.concatenate(grads_q, 0)
            sent, kept = order(attention_terms, core_1, normed, mixed_flat, value["q"], grad_branch, order_x)
            value["attn"] = kept, other_core(sent)

        def attn_step():
            value["attn"] = order(add, *value["attn"])
            at["attn"] = Halving(X_FIRST, [value["attn"]], width, order)

        def last_step():
            grads = jnp.concatenate([value[f"keys:{i}"] for i in range(PARTS)], 0)
            value["input"], term, sums = order(
                last_back, grads, value["q"], w_qkv, x, gain_attn, cos, sin, normed_t,
                grad_middle, gain_mlp_part,
            )
            block = width // n
            extra = jnp.pad(sums.astype(BF).reshape(-1, LANES), ((0, block - sums.size // LANES), (0, 0)))
            term = order(lambda t, e: jnp.concatenate([t, jnp.tile(e, (n, 1))], 1), term, extra)
            at["kv"] = Halving(X_FIRST, [term], width, order)

        def finish_step():
            value["output"] = order(finish, out_mine, out_theirs, middle)

        steps = {"ab": back_step, "terms": terms_step, "attn0": attn_step, "last": last_step}
        steps["finish"] = finish_step
        for name in PLAN:
            head, *rest = name.split(":")
            rest = [int(r) for r in rest]
            if head in steps:
                steps[head](*rest)
            elif head == "gu":
                value[name] = gate_up.go(order, *rest)
            elif head == "keys":
                value[name] = at[head, rest[0]].go(order, *rest[1:])
            else:
                value[name] = at[name].go(order)
        output, grad_input = value["output"], value["input"]
        rows_gate, rows_up = value["gu"][:, :half], value["gu"][:, half:]
        rows_down, rows_attn, rows_kv = value["down"], value["attn"], value["kv"]
        rows_kv = add(rows_kv, other_core(rows_kv))
        sums = rows_kv[:, 2 * KW :].astype(F32).reshape(-1)
    else:
        grad_q, *grads = back(0, streams)
        grad_q = grad_q.reshape(tokens, QW)
        sent, kept = attention_terms(core_1, normed, mixed_flat, grad_q, grad_branch, order_x)
        rows_attn = reduce_rows(add(kept, other_core(sent)))
        output = finish(out_mine, out_theirs, middle)
        grad_k, grad_v = [reduce_rows(jnp.concatenate(g, 0).reshape(n * tokens, KW)) for g in (grads[:2], grads[2:])]
        grad_kv = jnp.concatenate([grad_k, grad_v], 1)
        grad_input, term, sums = last_back(
            grad_kv, grad_q, w_qkv, x, gain_attn, cos, sin, normed_t, grad_middle,
            gain_mlp_part,
        )
        rows_kv = reduce_rows(term)
        rows_kv = add(rows_kv, other_core(rows_kv))
        sums = sum_over_all(sums.reshape(-1, LANES)).reshape(-1)
        rows_gate = reduce_rows(jnp.concatenate([keep_gate, send_gate], 0))
        rows_up = reduce_rows(jnp.concatenate([keep_up, send_up], 0))
        rows_down = reduce_rows(term_down)

    rows_down = to_owner(rows_down, Z_FIRST)
    rows_attn = both_cores(rows_attn, 1)
    rows_out, rows_q = rows_attn[:, :width], rows_attn[:, width:]
    small = [QW + 2 * KW, QW + 2 * KW + width, QW + 2 * KW + 2 * width]
    bias_grad, gain_attn_grad, gain_mlp_grad, _ = jnp.split(sums, small)
    return (
        output.reshape(streams, length, width),
        grad_input.reshape(streams, length, width),
        jnp.concatenate([rows_q, rows_kv[:, : 2 * KW].astype(F32)], 1),
        bias_grad,
        gain_attn_grad,
        rows_out,
        gain_mlp_grad,
        jnp.concatenate([both_cores(rows_gate, 1), both_cores(rows_up, 1)], 1),
        both_cores(rows_down, 0),
    )


PARTS = 1
PLAN = (
    "ab:0", "gu:0", "gu:1", "down", "keys:0:0", "keys:0:1", "terms", "attn0", "keys:0", "down", "keys:0",
    "gu", "finish", "attn", "keys:0", "down", "last", "gu", "kv", "attn", "kv", "attn", "kv", "gu", "down",
    "attn", "kv",
)


def solution(mesh):
    n = mesh.shape["seq"]
    sizes = {16: (4, 2, 2), 64: (4, 4, 4)}.get(n, (n, 1, 1))
    fine = Mesh(np.asarray(mesh.devices).reshape(*sizes, mesh.shape["dp"]), (*SEQ, "dp"))
    in_specs = (P("dp", SEQ, None), P("dp", None), P(), P(), P(), P(), P(), P(), P(), P("dp", SEQ, None))
    out_specs = (
        P("dp", SEQ, None), P("dp", SEQ, None), P(SEQ, None), P(), P(), P(SEQ, None), P(), P(SEQ, None), P(SEQ, None),
    )
    return jax.shard_map(shards, mesh=fine, in_specs=in_specs, out_specs=out_specs, check_vma=False)
```

profile of v0, /device:TPU:0, one launch (start us, length us, event | category | flops | bytes accessed | tf_op | source)
XLA Modules:
  0.0 360.6 jit_solution(12069491933259598135)
XLA Ops:
  6.0 3.4 project_kv.1
  9.5 3.1 collective-permute-start
  12.6 2.6 collective-permute-start.2
  18.3 4.0 %project_q.1 = bf16[384,896]{1,0:T(8,128)(2,1)} custom-call(bf16[384,896]{1,0:T(8,128)(2,1)} %get-tuple-element.238.normed_ref, bf16[896,1152]{1,0:T(8,128)(2,1)} %w_ref.4, bf16[1,1152]{1,0:T(2,128)(2,1)} %reshape.385.b_ref, f32[384,128]{1,0:T(8,128)} %get-tuple-element.281.cos_ref, f32[384,128]{1,0:T(8,128)} %get-tuple-element.282.sin_ref), custom_call_target="tpu_custom_call" | custom-call | flops 360000000 | bytes 65536 | tf_op jit(solution)/shard_map/project_q/pallas_call | solution.py:125
  23.3 5.0 %constant_dynamic-slice_fusion.3.wg_ref = bf16[896,2432]{1,0:T(8,128)(2,1)} fusion(bf16[896,9728]{1,0:T(8,128)(2,1)} %param.17, s32[]{:T(128)S(6)} %select_n.282), kind=kLoop, calls=%fused_computation.102 | loop fusion | bytes 8716292 | tf_op jit(solution)/shard_map/dynamic_slice | solution.py:756
  28.3 5.3 %collective-permute-done.1 = bf16[2,4,96,128]{3,2,1,0:T(8,128)(2,1)S(1)} collective-permute-done((bf16[2,4,96,128]{3,2,1,0:T(8,128)(2,1)S(1)}, bf16[2,4,96,128]{3,2,1,0:T(8,128)(2,1)S(1)}, u32[]{:S(2)}, u32[]{:S(2)}) %collective-permute-start.1) | collective-permute-done | bytes 196640 | tf_op jit(solution)/shard_map/ppermute | solution.py:553
  36.8 4.7 %constant_dynamic-slice_fusion.2.wu_ref = bf16[896,2432]{1,0:T(8,128)(2,1)} fusion(bf16[896,9728]{1,0:T(8,128)(2,1)} %param.17, s32[]{:T(128)S(6)} %select_n.283), kind=kLoop, calls=%fused_computation.101 | loop fusion | bytes 8716292 | tf_op jit(solution)/shard_map/dynamic_slice | solution.py:756
  41.5 2.4 constant_dynamic-slice_fusion.1.wd_ref
  55.2 10.1 %collective-permute-done.5 = bf16[8,4,96,128]{3,2,1,0:T(8,128)(2,1)} collective-permute-done((bf16[8,4,96,128]{3,2,1,0:T(8,128)(2,1)}, bf16[8,4,96,128]{3,2,1,0:T(8,128)(2,1)}, u32[]{:S(2)}, u32[]{:S(2)}) %collective-permute-start.5) | collective-permute-done | bytes 786464 | tf_op jit(solution)/shard_map/ppermute | solution.py:553
  72.8 13.3 %attend.1 = (bf16[4,96,896]{2,1,0:T(8,128)(2,1)}, f32[4,2,768]{2,1,0:T(2,128)}) custom-call(s32[4]{0:T(128)} %add_select_fusion.1.low_ref, s32[1]{0:T(128)} %bitcast.1.me_ref, s32[4,16]{1,0:T(4,128)} %pad_add_fusion.1.spot_ref, bf16[4,96,896]{2,1,0:T(8,128)(2,1)} %bitcast.46, bf16[16,4,96,128]{3,2,1,0:T(8,128)(2,1)} %copy-done.23, ...), custom_call_target="tpu_custom_call" | custom-call | flops 1620000000 | bytes 65536 | tf_op jit(solution)/shard_map/attend/pallas_call | solution.py:211
  91.5 47.9 %mlp.1 = (f32[384,896]{1,0:T(8,128)}, f32[384,896]{1,0:T(8,128)}, f32[384,896]{1,0:T(8,128)}, f32[384,896]{1,0:T(8,128)}, bf16[2432,896]{1,0:T(8,128)(2,1)}, /*i...) custom-call(bf16[384,896]{1,0:T(8,128)(2,1)} %copy-done.4, ...), custom_call_target="tpu_custom_call" | custom-call | flops 3600000000 | bytes 65536 | tf_op jit(solution)/shard_map/mlp/pallas_call | solution.py:427
  141.6 3.1 constant_dynamic-slice_fusion
  145.4 2.2 fusion.5
  148.7 6.4 %middle_back.1 = (f32[384,896]{1,0:T(8,128)}, bf16[384,896]{1,0:T(8,128)(2,1)}, bf16[384,896]{1,0:T(8,128)(2,1)}, f32[1,896]{1,0:T(1,128)}) custom-call(f32[384,896]{1,0:T(8,128)} %get-tuple-element.208.bm_ref, f32[384,896]{1,0:T(8,128)} %copy-done.14, f32[384,896]{1,0:T(8,128)} %copy-done.1, bf16[384,896]{1,0:T(8,128)(2,1)} %bitcast.32, ...), custom_call_target="tpu_custom_call" | custom-call | flops 450000000 | bytes 65536 | tf_op jit(solution)/shard_map/middle_back/pallas_call | solution.py:462
  155.2 19.9 %attend_back.1 = (bf16[4,96,896]{2,1,0:T(8,128)(2,1)}, bf16[8,4,96,128]{3,2,1,0:T(8,128)(2,1)}, bf16[8,4,96,128]{3,2,1,0:T(8,128)(2,1)}, bf16[8,4,96,128]{3,2,1,0:T(8,128)(2,1)}, bf16[8,4,96,128]{3,2,1,0:T(8,128)(2,1)}) custom-call(s32[4]{0:T(128)} %add_select_fusion.1.low_ref, s32[1]{0:T(128)} %bitcast.1.me_ref, s32[4,16]{1,0:T(4,128)} %pad_add_fusion.1.spot_ref, ...), custom_call_target="tpu_custom_call" | custom-call | flops 2880000000 | bytes 65536 | tf_op jit(solution)/shard_map/attend_back/pallas_call | solution.py:329
  177.0 13.0 %collective-permute-done.11 = bf16[448,2432]{1,0:T(8,128)(2,1)} collective-permute-done((bf16[448,2432]{1,0:T(8,128)(2,1)}, bf16[448,2432]{1,0:T(8,128)(2,1)}, u32[]{:S(2)}, u32[]{:S(2)}) %collective-permute-start.11) | collective-permute-done | bytes 2179104 | tf_op jit(solution)/shard_map/ppermute | solution.py:553
  192.0 2.5 add_convert_fusion.4
  194.5 3.3 add_convert_fusion.3
  197.8 10.1 %collective-permute-done.16 = bf16[3072,128]{1,0:T(8,128)(2,1)S(1)} collective-permute-done((bf16[3072,128]{1,0:T(8,128)(2,1)}, bf16[3072,128]{1,0:T(8,128)(2,1)S(1)}, u32[]{:S(2)}, u32[]{:S(2)}) %collective-permute-start.16) | collective-permute-done | bytes 786464 | tf_op jit(solution)/shard_map/ppermute | solution.py:553
  208.1 7.2 %attention_terms.1 = (bf16[896,896]{1,0:T(8,128)(2,1)}, bf16[896,896]{1,0:T(8,128)(2,1)}) custom-call(s32[1]{0:T(128)} %bitcast.14.core_ref, bf16[384,896]{1,0:T(8,128)(2,1)} %get-tuple-element.238.normed_ref, bf16[384,896]{1,0:T(8,128)(2,1)} %bitcast.49, bf16[384,896]{1,0:T(8,128)(2,1)} %bitcast.33, bf16[384,896]{1,0:T(8,128)(2,1)} %get-tuple-element.241.gb_ref, ...), custom_call_target="tpu_custom_call" | custom-call | flops 450000000 | bytes 65536 | tf_op jit(solution)/shard_map/attention_terms/pallas_call | solution.py:486
  216.5 9.1 %collective-permute-start.23 = (bf16[608,896]{1,0:T(8,128)(2,1)}, bf16[608,896]{1,0:T(8,128)(2,1)}, u32[]{:S(2)}, u32[]{:S(2)}) collective-permute-start(bf16[608,896]{1,0:T(8,128)(2,1)} %add_convert_fusion.3), channel_id=1, source_target_pairs={{0,16},{8,24},{16,0},{24,8},{1,17},{9,25},{17,1},{25,9},{2,18},{10... | collective-permute-start | bytes 3268616 | tf_op jit(solution)/shard_map/ppermute | solution.py:553
  232.2 39.8 %collective-permute-done.23 = bf16[608,896]{1,0:T(8,128)(2,1)} collective-permute-done((bf16[608,896]{1,0:T(8,128)(2,1)}, bf16[608,896]{1,0:T(8,128)(2,1)}, u32[]{:S(2)}, u32[]{:S(2)}) %collective-permute-start.23) | collective-permute-done | bytes 1089568 | tf_op jit(solution)/shard_map/ppermute | solution.py:553
  276.8 2.2 add_convert_fusion.2
  281.1 3.1 collective-permute-start.29
  285.6 7.4 %collective-permute-done.25 = bf16[448,896]{1,0:T(8,128)(2,1)S(1)} collective-permute-done((bf16[448,896]{1,0:T(8,128)(2,1)}, bf16[448,896]{1,0:T(8,128)(2,1)S(1)}, u32[]{:S(2)}, u32[]{:S(2)}) %collective-permute-start.25) | collective-permute-done | bytes 802848 | tf_op jit(solution)/shard_map/ppermute | solution.py:553
  295.8 7.9 %collective-permute-done.26 = bf16[304,896]{1,0:T(8,128)(2,1)S(1)} collective-permute-done((bf16[304,896]{1,0:T(8,128)(2,1)S(1)}, bf16[304,896]{1,0:T(8,128)(2,1)S(1)}, u32[]{:S(2)}, u32[]{:S(2)}) %collective-permute-start.26) | collective-permute-done | bytes 544800 | tf_op jit(solution)/shard_map/ppermute | solution.py:553
  307.5 5.6 %last_back.1 = (f32[384,896]{1,0:T(8,128)}, bf16[896,256]{1,0:T(8,128)(2,1)}, f32[1,2944]{1,0:T(1,128)}) custom-call(bf16[384,256]{1,0:T(8,128)(2,1)} %add_convert_fusion.18.gkv_ref, bf16[384,896]{1,0:T(8,128)(2,1)} %bitcast.34, bf16[896,1152]{1,0:T(8,128)(2,1)} %w_ref.4, bf16[384,896]{1,0:T(8,128)(2,1)} %bitcast.36, bf16[1,896]{1,0:T(2,128)(2,1)} %reshape.386.g_ref, ...), custom_call_target="tpu_custom_call" | custom-call | flops 540000000 | bytes 65536 | tf_op jit(solution)/shard_map/last_back/pallas_call | solution.py:519
  317.8 6.3 %collective-permute-done.28 = bf16[448,384]{1,0:T(8,128)(2,1)S(1)} collective-permute-done((bf16[448,384]{1,0:T(8,128)(2,1)S(1)}, bf16[448,384]{1,0:T(8,128)(2,1)S(1)}, u32[]{:S(2)}, u32[]{:S(2)}) %collective-permute-start.28) | collective-permute-done | bytes 344096 | tf_op jit(solution)/shard_map/ppermute | solution.py:553
  325.5 4.2 %collective-permute-done.31 = bf16[224,384]{1,0:T(8,128)(2,1)S(1)} collective-permute-done((bf16[224,384]{1,0:T(8,128)(2,1)S(1)}, bf16[224,384]{1,0:T(8,128)(2,1)S(1)}, u32[]{:S(2)}, u32[]{:S(2)}) %collective-permute-start.31) | collective-permute-done | bytes 172064 | tf_op jit(solution)/shard_map/ppermute | solution.py:553
  329.7 8.2 %collective-permute-done.30 = bf16[112,896]{1,0:T(8,128)(2,1)S(1)} collective-permute-done((bf16[112,896]{1,0:T(8,128)(2,1)S(1)}, bf16[112,896]{1,0:T(8,128)(2,1)S(1)}, u32[]{:S(2)}, u32[]{:S(2)}) %collective-permute-start.30) | collective-permute-done | bytes 200736 | tf_op jit(solution)/shard_map/ppermute | solution.py:553
  338.1 4.2 %collective-permute-done.35 = bf16[112,384]{1,0:T(8,128)(2,1)S(1)} collective-permute-done((bf16[112,384]{1,0:T(8,128)(2,1)S(1)}, bf16[112,384]{1,0:T(8,128)(2,1)S(1)}, u32[]{:S(2)}, u32[]{:S(2)}) %collective-permute-start.35) | collective-permute-done | bytes 86048 | tf_op jit(solution)/shard_map/ppermute | solution.py:553
  353.1 3.7 %collective-permute-start.42 = (bf16[152,896]{1,0:T(8,128)(2,1)S(1)}, bf16[152,896]{1,0:T(8,128)(2,1)S(1)}, u32[]{:S(2)}, u32[]{:S(2)}) collective-permute-start(bf16[152,896]{1,0:T(8,128)(2,1)S(1)} %collective-permute-done.41), channel_id=1, source_target_pairs={{0,1},{1,0},{2,3},{3,2},{4,5},{5,4},{6,7},{7,6},{8,9},{9,8},{10,11... | collective-permute-start | bytes 817160 | tf_op jit(solution)/shard_map/ppermute | solution.py:549
  (245 shorter events, 87.8 us)
Async XLA Ops:
  9.5 12.9 %collective-permute-start = (bf16[1,4,96,128]{3,2,1,0:T(8,128)(2,1)}, bf16[1,4,96,128]{3,2,1,0:T(8,128)(2,1)S(1)}, u32[]{:S(2)}, u32[]{:S(2)}) collective-permute-start(bf16[1,4,96,128]{3,2,1,0:T(8,128)(2,1)} %bitcast.52), channel_id=1, source_target_pairs={{0,8},{8,0},{16,24},{24,16},{1,9},{9,1},{17,25},{25,17},{2,10},{10... | collective-permute-start | bytes 294920 | tf_op jit(solution)/shard_map/ppermute | solution.py:553
  12.6 10.3 %collective-permute-start.2 = (bf16[1,4,96,128]{3,2,1,0:T(8,128)(2,1)}, bf16[1,4,96,128]{3,2,1,0:T(8,128)(2,1)S(1)}, u32[]{:S(2)}, u32[]{:S(2)}) collective-permute-start(bf16[1,4,96,128]{3,2,1,0:T(8,128)(2,1)} %bitcast.50), channel_id=1, source_target_pairs={{0,16},{8,24},{16,0},{24,8},{1,17},{9,25},{17,1},{25,9},{2,18},{10... | collective-permute-start | bytes 294920 | tf_op jit(solution)/shard_map/ppermute | solution.py:553
  22.4 11.1 %collective-permute-start.1 = (bf16[2,4,96,128]{3,2,1,0:T(8,128)(2,1)S(1)}, bf16[2,4,96,128]{3,2,1,0:T(8,128)(2,1)S(1)}, u32[]{:S(2)}, u32[]{:S(2)}) collective-permute-start(bf16[2,4,96,128]{3,2,1,0:T(8,128)(2,1)S(1)} %constant_dynamic-update-slice_fusion), channel_id=1, source_target_pairs={{0,16},{8,24},{16,0},{24,8},{1,17},{9,25},{17,1},{25,9},{2,18},{10... | collective-permute-start | bytes 589832 | tf_op jit(solution)/shard_map/ppermute | solution.py:553
  22.9 12.3 %collective-permute-start.4 = (bf16[2,4,96,128]{3,2,1,0:T(8,128)(2,1)S(1)}, bf16[2,4,96,128]{3,2,1,0:T(8,128)(2,1)S(1)}, u32[]{:S(2)}, u32[]{:S(2)}) collective-permute-start(bf16[2,4,96,128]{3,2,1,0:T(8,128)(2,1)S(1)} %constant_dynamic-update-slice_fusion.2), channel_id=1, source_target_pairs={{0,8},{8,0},{16,24},{24,16},{1,9},{9,1},{17,25},{25,17},{2,10},{10... | collective-permute-start | bytes 589832 | tf_op jit(solution)/shard_map/ppermute | solution.py:553
  33.6 11.1 %collective-permute-start.3 = (bf16[4,4,96,128]{3,2,1,0:T(8,128)(2,1)S(1)}, bf16[4,4,96,128]{3,2,1,0:T(8,128)(2,1)S(1)}, u32[]{:S(2)}, u32[]{:S(2)}) collective-permute-start(bf16[4,4,96,128]{3,2,1,0:T(8,128)(2,1)S(1)} %constant_dynamic-update-slice_fusion.4), channel_id=1, source_target_pairs={{0,2},{2,0},{1,3},{3,1},{4,6},{6,4},{5,7},{7,5},{8,10},{10,8},{9,1... | collective-permute-start | bytes 1179656 | tf_op jit(solution)/shard_map/ppermute | solution.py:553
  35.3 12.6 %collective-permute-start.6 = (bf16[4,4,96,128]{3,2,1,0:T(8,128)(2,1)S(1)}, bf16[4,4,96,128]{3,2,1,0:T(8,128)(2,1)}, u32[]{:S(2)}, u32[]{:S(2)}) collective-permute-start(bf16[4,4,96,128]{3,2,1,0:T(8,128)(2,1)S(1)} %constant_dynamic-update-slice_fusion.6), channel_id=1, source_target_pairs={{0,4},{4,0},{1,5},{5,1},{2,6},{6,2},{3,7},{7,3},{8,12},{12,8},{9,1... | collective-permute-start | bytes 1179656 | tf_op jit(solution)/shard_map/ppermute | solution.py:553
  46.3 19.0 %collective-permute-start.5 = (bf16[8,4,96,128]{3,2,1,0:T(8,128)(2,1)}, bf16[8,4,96,128]{3,2,1,0:T(8,128)(2,1)}, u32[]{:S(2)}, u32[]{:S(2)}) collective-permute-start(bf16[8,4,96,128]{3,2,1,0:T(8,128)(2,1)} %constant_dynamic-update-slice_fusion.8), channel_id=1, source_target_pairs={{0,4},{4,0},{1,5},{5,1},{2,6},{6,2},{3,7},{7,3},{8,12},{12,8},{9,1... | collective-permute-start | bytes 2359304 | tf_op jit(solution)/shard_map/ppermute | solution.py:553
  50.4 18.8 %collective-permute-start.7 = (bf16[8,4,96,128]{3,2,1,0:T(8,128)(2,1)}, bf16[8,4,96,128]{3,2,1,0:T(8,128)(2,1)}, u32[]{:S(2)}, u32[]{:S(2)}) collective-permute-start(bf16[8,4,96,128]{3,2,1,0:T(8,128)(2,1)} %constant_dynamic-update-slice_fusion.10), channel_id=1, source_target_pairs={{0,2},{2,0},{1,3},{3,1},{4,6},{6,4},{5,7},{7,5},{8,10},{10,8},{9,1... | collective-permute-start | bytes 2359304 | tf_op jit(solution)/shard_map/ppermute | solution.py:553
  52.5 36.0 %collective-permute-start.9 = (bf16[384,896]{1,0:T(8,128)(2,1)S(1)}, bf16[384,896]{1,0:T(8,128)(2,1)}, u32[]{:S(2)}, u32[]{:S(2)}) collective-permute-start(bf16[384,896]{1,0:T(8,128)(2,1)S(1)} %bitcast.30), channel_id=1, source_target_pairs={{0,1},{1,0},{2,3},{3,2},{4,5},{5,4},{6,7},{7,6},{8,9},{9,8},{10,11... | collective-permute-start | bytes 2064392 | tf_op jit(solution)/shard_map/ppermute | solution.py:549
  139.5 50.6 %collective-permute-start.11 = (bf16[448,2432]{1,0:T(8,128)(2,1)}, bf16[448,2432]{1,0:T(8,128)(2,1)}, u32[]{:S(2)}, u32[]{:S(2)}) collective-permute-start(bf16[448,2432]{1,0:T(8,128)(2,1)} %get-tuple-element.203), channel_id=1, source_target_pairs={{0,2},{2,0},{1,3},{3,1},{4,6},{6,4},{5,7},{7,5},{8,10},{10,8},{9,1... | collective-permute-start | bytes 6537224 | tf_op jit(solution)/shard_map/ppermute | solution.py:553
  141.0 50.7 %collective-permute-start.14 = (bf16[448,2432]{1,0:T(8,128)(2,1)}, bf16[448,2432]{1,0:T(8,128)(2,1)}, u32[]{:S(2)}, u32[]{:S(2)}) collective-permute-start(bf16[448,2432]{1,0:T(8,128)(2,1)} %get-tuple-element.224), channel_id=1, source_target_pairs={{0,4},{4,0},{1,5},{5,1},{2,6},{6,2},{3,7},{7,3},{8,12},{12,8},{9,1... | collective-permute-start | bytes 6537224 | tf_op jit(solution)/shard_map/ppermute | solution.py:553
  144.8 49.7 %collective-permute-start.17 = (bf16[1216,896]{1,0:T(8,128)(2,1)}, bf16[1216,896]{1,0:T(8,128)(2,1)S(1)}, u32[]{:S(2)}, u32[]{:S(2)}) collective-permute-start(bf16[1216,896]{1,0:T(8,128)(2,1)} %constant_dynamic-slice_fusion), channel_id=1, source_target_pairs={{0,8},{8,0},{16,24},{24,16},{1,9},{9,1},{17,25},{25,17},{2,10},{10... | collective-permute-start | bytes 6537224 | tf_op jit(solution)/shard_map/ppermute | solution.py:553
  175.0 32.9 %collective-permute-start.16 = (bf16[3072,128]{1,0:T(8,128)(2,1)}, bf16[3072,128]{1,0:T(8,128)(2,1)S(1)}, u32[]{:S(2)}, u32[]{:S(2)}) collective-permute-start(bf16[3072,128]{1,0:T(8,128)(2,1)} %bitcast.59), channel_id=1, source_target_pairs={{0,4},{4,0},{1,5},{5,1},{2,6},{6,2},{3,7},{7,3},{8,12},{12,8},{9,1... | collective-permute-start | bytes 2359304 | tf_op jit(solution)/shard_map/ppermute | solution.py:553
  176.5 31.5 %collective-permute-start.19 = (bf16[3072,128]{1,0:T(8,128)(2,1)}, bf16[3072,128]{1,0:T(8,128)(2,1)S(1)}, u32[]{:S(2)}, u32[]{:S(2)}) collective-permute-start(bf16[3072,128]{1,0:T(8,128)(2,1)} %bitcast.58), channel_id=1, source_target_pairs={{0,2},{2,0},{1,3},{3,1},{4,6},{6,4},{5,7},{7,5},{8,10},{10,8},{9,1... | collective-permute-start | bytes 2359304 | tf_op jit(solution)/shard_map/ppermute | solution.py:553
  215.4 11.8 %collective-permute-start.21 = (bf16[896,896]{1,0:T(8,128)(2,1)}, bf16[896,896]{1,0:T(8,128)(2,1)S(1)}, u32[]{:S(2)}, u32[]{:S(2)}) collective-permute-start(bf16[896,896]{1,0:T(8,128)(2,1)} %get-tuple-element.244), channel_id=1, source_target_pairs={{0,1},{1,0},{2,3},{3,2},{4,5},{5,4},{6,7},{7,6},{8,9},{9,8},{10,11... | collective-permute-start | bytes 4816904 | tf_op jit(solution)/shard_map/ppermute | solution.py:549
  215.4 15.6 %collective-permute-start.20 = (bf16[1536,128]{1,0:T(8,128)(2,1)S(1)}, bf16[1536,128]{1,0:T(8,128)(2,1)S(1)}, u32[]{:S(2)}, u32[]{:S(2)}) collective-permute-start(bf16[1536,128]{1,0:T(8,128)(2,1)S(1)} %add_convert_fusion.13), channel_id=1, source_target_pairs={{0,4},{4,0},{1,5},{5,1},{2,6},{6,2},{3,7},{7,3},{8,12},{12,8},{9,1... | collective-permute-start | bytes 1179656 | tf_op jit(solution)/shard_map/ppermute | solution.py:553
  216.0 15.0 %collective-permute-start.18 = (bf16[1536,128]{1,0:T(8,128)(2,1)S(1)}, bf16[1536,128]{1,0:T(8,128)(2,1)S(1)}, u32[]{:S(2)}, u32[]{:S(2)}) collective-permute-start(bf16[1536,128]{1,0:T(8,128)(2,1)S(1)} %add_convert_fusion.14), channel_id=1, source_target_pairs={{0,2},{2,0},{1,3},{3,1},{4,6},{6,4},{5,7},{7,5},{8,10},{10,8},{9,1... | collective-permute-start | bytes 1179656 | tf_op jit(solution)/shard_map/ppermute | solution.py:553
  216.5 55.5 %collective-permute-start.23 = (bf16[608,896]{1,0:T(8,128)(2,1)}, bf16[608,896]{1,0:T(8,128)(2,1)}, u32[]{:S(2)}, u32[]{:S(2)}) collective-permute-start(bf16[608,896]{1,0:T(8,128)(2,1)} %add_convert_fusion.3), channel_id=1, source_target_pairs={{0,16},{8,24},{16,0},{24,8},{1,17},{9,25},{17,1},{25,9},{2,18},{10... | collective-permute-start | bytes 3268616 | tf_op jit(solution)/shard_map/ppermute | solution.py:553
  225.7 51.0 %collective-permute-start.15 = (bf16[224,2432]{1,0:T(8,128)(2,1)}, bf16[224,2432]{1,0:T(8,128)(2,1)}, u32[]{:S(2)}, u32[]{:S(2)}) collective-permute-start(bf16[224,2432]{1,0:T(8,128)(2,1)} %add_convert_fusion.4), channel_id=1, source_target_pairs={{0,2},{2,0},{1,3},{3,1},{4,6},{6,4},{5,7},{7,5},{8,10},{10,8},{9,1... | collective-permute-start | bytes 3268616 | tf_op jit(solution)/shard_map/ppermute | solution.py:553
  227.1 49.6 %collective-permute-start.13 = (bf16[224,2432]{1,0:T(8,128)(2,1)S(1)}, bf16[224,2432]{1,0:T(8,128)(2,1)}, u32[]{:S(2)}, u32[]{:S(2)}) collective-permute-start(bf16[224,2432]{1,0:T(8,128)(2,1)S(1)} %add_convert_fusion.5), channel_id=1, source_target_pairs={{0,4},{4,0},{1,5},{5,1},{2,6},{6,2},{3,7},{7,3},{8,12},{12,8},{9,1... | collective-permute-start | bytes 3268616 | tf_op jit(solution)/shard_map/ppermute | solution.py:553
  232.1 42.5 %collective-permute-start.22 = (bf16[768,256]{1,0:T(8,128)(2,1)}, bf16[768,256]{1,0:T(8,128)(2,1)}, u32[]{:S(2)}, u32[]{:S(2)}) collective-permute-start(bf16[768,256]{1,0:T(8,128)(2,1)} %fusion.3), channel_id=1, source_target_pairs={{0,8},{8,0},{16,24},{24,16},{1,9},{9,1},{17,25},{25,17},{2,10},{10... | collective-permute-start | bytes 1179656 | tf_op jit(solution)/shard_map/ppermute | solution.py:553
  232.1 52.3 %collective-permute-start.10 = (f32[384,896]{1,0:T(8,128)}, f32[384,896]{1,0:T(8,128)S(1)}, u32[]{:S(2)}, u32[]{:S(2)}) collective-permute-start(f32[384,896]{1,0:T(8,128)} %get-tuple-element.201), channel_id=1, source_target_pairs={{0,1},{1,0},{2,3},{3,2},{4,5},{5,4},{6,7},{7,6},{8,9},{9,8},{10,11... | collective-permute-start | bytes 4128776 | tf_op jit(solution)/shard_map/ppermute | solution.py:549
  272.0 21.0 %collective-permute-start.25 = (bf16[448,896]{1,0:T(8,128)(2,1)}, bf16[448,896]{1,0:T(8,128)(2,1)S(1)}, u32[]{:S(2)}, u32[]{:S(2)}) collective-permute-start(bf16[448,896]{1,0:T(8,128)(2,1)} %dynamic_slice.276), channel_id=1, source_target_pairs={{0,2},{2,0},{1,3},{3,1},{4,6},{6,4},{5,7},{7,5},{8,10},{10,8},{9,1... | collective-permute-start | bytes 2408456 | tf_op jit(solution)/shard_map/ppermute | solution.py:553
  274.6 29.1 %collective-permute-start.26 = (bf16[304,896]{1,0:T(8,128)(2,1)S(1)}, bf16[304,896]{1,0:T(8,128)(2,1)S(1)}, u32[]{:S(2)}, u32[]{:S(2)}) collective-permute-start(bf16[304,896]{1,0:T(8,128)(2,1)S(1)} %add_convert_fusion.9), channel_id=1, source_target_pairs={{0,2},{2,0},{1,3},{3,1},{4,6},{6,4},{5,7},{7,5},{8,10},{10,8},{9,1... | collective-permute-start | bytes 1634312 | tf_op jit(solution)/shard_map/ppermute | solution.py:553
  276.7 17.4 %collective-permute-start.24 = (bf16[384,256]{1,0:T(8,128)(2,1)S(1)}, bf16[384,256]{1,0:T(8,128)(2,1)S(1)}, u32[]{:S(2)}, u32[]{:S(2)}) collective-permute-start(bf16[384,256]{1,0:T(8,128)(2,1)S(1)} %add_convert_fusion.19), channel_id=1, source_target_pairs={{0,16},{8,24},{16,0},{24,8},{1,17},{9,25},{17,1},{25,9},{2,18},{10... | collective-permute-start | bytes 589832 | tf_op jit(solution)/shard_map/ppermute | solution.py:553
  281.1 35.5 %collective-permute-start.29 = (bf16[112,4864]{1,0:T(8,128)(2,1)S(1)}, bf16[112,4864]{1,0:T(8,128)(2,1)}, u32[]{:S(2)}, u32[]{:S(2)}) collective-permute-start(bf16[112,4864]{1,0:T(8,128)(2,1)S(1)} %fusion.2), channel_id=1, source_target_pairs={{0,8},{8,0},{16,24},{24,16},{1,9},{9,1},{17,25},{25,17},{2,10},{10... | collective-permute-start | bytes 3268616 | tf_op jit(solution)/shard_map/ppermute | solution.py:553
  293.1 32.2 %collective-permute-start.27 = (bf16[224,896]{1,0:T(8,128)(2,1)S(1)}, bf16[224,896]{1,0:T(8,128)(2,1)S(1)}, u32[]{:S(2)}, u32[]{:S(2)}) collective-permute-start(bf16[224,896]{1,0:T(8,128)(2,1)S(1)} %add_convert_fusion.10), channel_id=1, source_target_pairs={{0,4},{4,0},{1,5},{5,1},{2,6},{6,2},{3,7},{7,3},{8,12},{12,8},{9,1... | collective-permute-start | bytes 1204232 | tf_op jit(solution)/shard_map/ppermute | solution.py:553
  306.5 38.9 %collective-permute-start.33 = (bf16[152,896]{1,0:T(8,128)(2,1)}, bf16[152,896]{1,0:T(8,128)(2,1)S(1)}, u32[]{:S(2)}, u32[]{:S(2)}) collective-permute-start(bf16[152,896]{1,0:T(8,128)(2,1)} %add_convert_fusion.16), channel_id=1, source_target_pairs={{0,4},{4,0},{1,5},{5,1},{2,6},{6,2},{3,7},{7,3},{8,12},{12,8},{9,1... | collective-permute-start | bytes 817160 | tf_op jit(solution)/shard_map/ppermute | solution.py:553
  315.0 9.1 %collective-permute-start.28 = (bf16[448,384]{1,0:T(8,128)(2,1)S(1)}, bf16[448,384]{1,0:T(8,128)(2,1)S(1)}, u32[]{:S(2)}, u32[]{:S(2)}) collective-permute-start(bf16[448,384]{1,0:T(8,128)(2,1)S(1)} %dynamic_slice.277), channel_id=1, source_target_pairs={{0,2},{2,0},{1,3},{3,1},{4,6},{6,4},{5,7},{7,5},{8,10},{10,8},{9,1... | collective-permute-start | bytes 1032200 | tf_op jit(solution)/shard_map/ppermute | solution.py:553
  317.8 26.4 %collective-permute-start.34 = (bf16[56,4864]{1,0:T(8,128)(2,1)S(1)}, bf16[56,4864]{1,0:T(8,128)(2,1)S(1)}, u32[]{:S(2)}, u32[]{:S(2)}) collective-permute-start(bf16[56,4864]{1,0:T(8,128)(2,1)S(1)} %add_convert_fusion.8), channel_id=1, source_target_pairs={{0,16},{8,24},{16,0},{24,8},{1,17},{9,25},{17,1},{25,9},{2,18},{10... | collective-permute-start | bytes 1634312 | tf_op jit(solution)/shard_map/ppermute | solution.py:553
  325.4 12.6 %collective-permute-start.30 = (bf16[112,896]{1,0:T(8,128)(2,1)S(1)}, bf16[112,896]{1,0:T(8,128)(2,1)S(1)}, u32[]{:S(2)}, u32[]{:S(2)}) collective-permute-start(bf16[112,896]{1,0:T(8,128)(2,1)S(1)} %add_convert_fusion.17), channel_id=1, source_target_pairs={{0,8},{8,0},{16,24},{24,16},{1,9},{9,1},{17,25},{25,17},{2,10},{10... | collective-permute-start | bytes 602120 | tf_op jit(solution)/shard_map/ppermute | solution.py:553
  329.7 12.6 %collective-permute-start.35 = (bf16[112,384]{1,0:T(8,128)(2,1)S(1)}, bf16[112,384]{1,0:T(8,128)(2,1)S(1)}, u32[]{:S(2)}, u32[]{:S(2)}) collective-permute-start(bf16[112,384]{1,0:T(8,128)(2,1)S(1)} %add_convert_fusion.23), channel_id=1, source_target_pairs={{0,8},{8,0},{16,24},{24,16},{1,9},{9,1},{17,25},{25,17},{2,10},{10... | collective-permute-start | bytes 258056 | tf_op jit(solution)/shard_map/ppermute | solution.py:553
  (46 other events, 472.0 us)
where the time goes:
time: 367 us; the launch traced here: 361 us
  waiting for transfers between devices  124 us (34%)
  Pallas kernels  108 us (29%)
  starting transfers between devices  46.2 us (13%)
  other arithmetic  40.5 us (11%)
  local copies, waits for them, and re-layouts  36 us (10%)
  matrix products  4.11 us (1%)
    ppermute x32, waiting for transfers between devices, pair_up(): lax.ppermute(a, axis, [(i, i ^ step) for i in range(lax.axis_size(axis))])  121 us
    pallas_call x1, Pallas kernels, mlp(): pl.pallas_call(functools.partial(mlp_kernel, half), grid=(pl.cdiv(half, T...  47.9 us
    ppermute x32, starting transfers between devices, pair_up(): lax.ppermute(a, axis, [(i, i ^ step) for i in range(lax.axis_size(axis))])  39.7 us
    convert_element_type x26, other arithmetic, total(): functools.reduce(lambda a, b: a + b, [a.astype(F32) for a in terms])  24.4 us
    pallas_call x1, Pallas kernels, attend_back(): pl.pallas_call(functools.partial(backward_kernel, first), grid_spec=pltpu...  19.9 us
    pallas_call x1, Pallas kernels, attend(): pl.pallas_call(forward_kernel, grid_spec=pltpu.PrefetchScalarGridSpec(num...  13.3 us
    dynamic_slice x2, local copies, waits for them, and re-layouts, shards(): lax.dynamic_slice_in_dim(w, first + core * half, half, 1)  9.7 us
    unnamed x79, local copies, waits for them, and re-layouts  9.12 us
  transfers between devices with their start and end apart: 43, of which 17 were waited for; matrix products, arithmetic and copies ran while one was open for 19% of the time, Pallas kernels for 14%

commit v1 on v0

--- a/solution.py
+++ b/solution.py
@@ -62,16 +62,17 @@
     return part * cos + half_swap(part) * sin
 
 
-def project_kv_kernel(x_ref, w_ref, b_ref, g_ref, cos_ref, sin_ref, normed_ref, k_ref, v_ref):
+def project_kv_kernel(x_ref, w_ref, small_ref, cos_ref, sin_ref, normed_ref, k_ref, v_ref):
     step = pl.program_id(0)
 
     @pl.when(step == 0)
     def _():
         x = x_ref[...].astype(F32)
         inv = lax.rsqrt(jnp.mean(x * x, axis=-1, keepdims=True) + epsilon)
-        normed_ref[...] = (x * inv * g_ref[...].astype(F32)).astype(BF)
-
-    part = nn(normed_ref[...], w_ref[...]) + b_ref[...].astype(F32)
+        normed_ref[...] = (x * inv * small_ref[:, QW + 2 * KW :].astype(F32)).astype(BF)
+
+    at = pl.multiple_of(QW + step * KW, LANES)
+    part = nn(normed_ref[...], w_ref[...]) + small_ref[:, pl.ds(at, KW)].astype(F32)
 
     @pl.when(step == 0)
     def _():
@@ -82,7 +83,7 @@
         v_ref[...] = part.astype(BF)
 
 
-def project_kv(x, w, b, g, cos, sin):
+def project_kv(x, w, small, cos, sin):
     tokens, width = x.shape
     fixed = lambda *shape: pl.BlockSpec(shape, lambda i: (0, 0))
     return pl.pallas_call(
@@ -91,8 +92,7 @@
         in_specs=[
             fixed(tokens, width),
             pl.BlockSpec((width, KW), lambda i: (0, QW // KW + i)),
-            pl.BlockSpec((1, KW), lambda i: (0, QW // KW + i)),
-            fixed(1, width),
+            fixed(*small.shape),
             fixed(tokens, LANES),
             fixed(tokens, LANES),
         ],
@@ -105,7 +105,7 @@
         compiler_params=params(),
         cost_estimate=cost(3),
         name="project_kv",
-    )(x, w, b, g, cos, sin)
+    )(x, w, small, cos, sin)
 
 
 def project_q_kernel(normed_ref, w_ref, b_ref, cos_ref, sin_ref, q_ref):
@@ -152,11 +152,19 @@
     return (index <= start_ref[0, 1:2, cols]) & (index >= start_ref[0, 0:1, cols])
 
 
-def gathered(ref, spot_ref, which, j):
-    return jnp.concatenate([ref[spot_ref[which, j * GROUP + i], 0] for i in range(GROUP)], 0)
-
-
-def forward_kernel(low_ref, me_ref, spot_ref, q_ref, k_ref, v_ref, start_ref, out_ref, lse_ref, qa, qb, ma, la, oa, mb, lb, ob, weights):
+def gathered(first_ref, second_ref, spot_ref, which, j):
+    half = first_ref.shape[0]
+
+    def block(i):
+        spot = spot_ref[which, j * GROUP + i]
+        one = first_ref[jnp.minimum(spot, half - 1), 0]
+        two = second_ref[jnp.maximum(spot - half, 0), 0]
+        return jnp.where(jnp.broadcast_to(spot < half, one.shape), one, two)
+
+    return jnp.concatenate([block(i) for i in range(GROUP)], 0)
+
+
+def forward_kernel(low_ref, me_ref, spot_ref, q_ref, k1_ref, k2_ref, v1_ref, v2_ref, start_ref, out_ref, lse_ref, qa, qb, ma, la, oa, mb, lb, ob, weights):
     rows = q_ref.shape[1]
     stream = pl.program_id(0)
     me = me_ref[0]
@@ -169,8 +177,8 @@
     keys = GROUP * rows
 
     def step(j, carry):
-        key = gathered(k_ref, spot_ref, 0, j)
-        value = gathered(v_ref, spot_ref, 1, j)
+        key = gathered(k1_ref, k2_ref, spot_ref, 0, j)
+        value = gathered(v1_ref, v2_ref, spot_ref, 1, j)
         for swap, q, m, l, o in ((False, qa, ma, la, oa), (True, qb, mb, lb, ob)):
             width = q.shape[0]
             k = swapped(key) if swap else key
@@ -204,7 +212,7 @@
 
 def attend(q, k_all, v_all, start_rows, low, me, spots):
     streams, rows, width = q.shape
-    n = k_all.shape[0]
+    half = k_all[0].shape[0]
     a, b = len(SAME) * rows, len(OTHER) * rows
     tok = lambda w: pl.BlockSpec((1, rows, w), lambda s, *_: (s, 0, 0))
     two = pl.BlockSpec((1, 2, a), lambda s, *_: (s, 0, 0))
@@ -213,7 +221,7 @@
         grid_spec=pltpu.PrefetchScalarGridSpec(
             num_scalar_prefetch=3,
             grid=(streams,),
-            in_specs=[tok(width), *[pl.BlockSpec((n, 1, rows, KW), lambda s, *_: (0, s, 0, 0))] * 2, two],
+            in_specs=[tok(width), *[pl.BlockSpec((half, 1, rows, KW), lambda s, *_: (0, s, 0, 0))] * 4, two],
             out_specs=[tok(width), two],
             scratch_shapes=[
                 pltpu.VMEM((a, LANES), BF),
@@ -234,7 +242,7 @@
         compiler_params=params(),
         cost_estimate=cost(18),
         name="attend",
-    )(low, me, spots, q, k_all, v_all, start_rows)
+    )(low, me, spots, q, *k_all, *v_all, start_rows)
 
 
 def three_parts(column):
@@ -253,7 +261,7 @@
 
 
 def backward_kernel(
-    first, low_ref, me_ref, spot_ref, q_ref, k_ref, v_ref, start_ref, lse_ref, mixed_ref, grad_ref, cos_ref, sin_ref, dq_ref, dkk_ref,
+    first, low_ref, me_ref, spot_ref, q_ref, k1_ref, k2_ref, v1_ref, v2_ref, start_ref, lse_ref, mixed_ref, grad_ref, cos_ref, sin_ref, dq_ref, dkk_ref,
     dks_ref, dvk_ref, dvs_ref, qa, qb, ga, gb, ta, tb, dk_all, dv_all, weights, grads,
 ):
     rows = q_ref.shape[1]
@@ -280,8 +288,8 @@
     ones = (lane_iota((keys, LANES)) < 3).astype(F32).astype(BF)
 
     def step(j, carry):
-        key = gathered(k_ref, spot_ref, 0, j)
-        value = gathered(v_ref, spot_ref, 1, j)
+        key = gathered(k1_ref, k2_ref, spot_ref, 0, j)
+        value = gathered(v1_ref, v2_ref, spot_ref, 1, j)
         grad_keys = []
         grad_values = []
         for row, (q, g, t) in enumerate(((qa, ga, ta), (qb, gb, tb))):
@@ -321,7 +329,8 @@
 
 def attend_back(first, streams, q, k_all, v_all, start_rows, low, me, spots, lse, mixed, grad, cos, sin):
     rows, width = q.shape[1:]
-    n = k_all.shape[0]
+    half = k_all[0].shape[0]
+    n = 2 * half
     a, b = len(SAME) * rows, len(OTHER) * rows
     tok = lambda w: pl.BlockSpec((1, rows, w), lambda s, *_: (s + first, 0, 0))
     two = pl.BlockSpec((1, 2, a), lambda s, *_: (s + first, 0, 0))
@@ -333,7 +342,7 @@
             grid=(streams,),
             in_specs=[
                 tok(width),
-                *[pl.BlockSpec((n, 1, rows, KW), lambda s, *_: (0, s + first, 0, 0))] * 2,
+                *[pl.BlockSpec((half, 1, rows, KW), lambda s, *_: (0, s + first, 0, 0))] * 4,
                 two,
                 two,
                 tok(width),
@@ -360,15 +369,15 @@
         compiler_params=params(),
         cost_estimate=cost(8 * streams),
         name="attend_back",
-    )(low, me, spots, q, k_all, v_all, start_rows, lse, mixed, grad, cos, sin)
+    )(low, me, spots, q, *k_all, *v_all, start_rows, lse, mixed, grad, cos, sin)
 
 
 TILE = 256
 
 
 def mlp_kernel(
-    valid, mine_ref, theirs_ref, sm_ref, st_ref, og_ref, ou_ref, wg_ref, wu_ref, wd_ref, om_ref, ot_ref, bm_ref, bt_ref,
-    td_ref, gk_ref, gs_ref, uk_ref, us_ref, n_ref, s_ref, ng_ref, nu_ref,
+    valid, mine_ref, theirs_ref, sm_ref, st_ref, order_ref, wg_ref, wu_ref, wd_ref, om_ref, ot_ref, bm_ref, bt_ref,
+    td_ref, gk_ref, gs_ref, uk_ref, us_ref, n_ref, s_ref, turned_ref,
 ):
     rows = mine_ref.shape[0]
     step = pl.program_id(0)
@@ -380,8 +389,7 @@
         n_ref[rows:] = theirs_ref[...]
         s_ref[:rows] = sm_ref[...]
         s_ref[rows:] = st_ref[...]
-        ng_ref[...] = nt(og_ref[...], n_ref[...]).astype(BF)
-        nu_ref[...] = nt(ou_ref[...], n_ref[...]).astype(BF)
+        turned_ref[...] = nt(order_ref[...], n_ref[...]).astype(BF)
         for ref in sums:
             ref[...] = jnp.zeros_like(ref)
 
@@ -399,11 +407,13 @@
     grad_up = (grad * silu).astype(BF)
     grad_gate = (grad * up * (sig * (1.0 + gate * (1.0 - sig)))).astype(BF)
     td_ref[...] = tn(active, seed).astype(BF)
-    half = gk_ref.shape[0]
-    for turned, grad_pre, keep, send in ((ng_ref, grad_gate, gk_ref, gs_ref), (nu_ref, grad_up, uk_ref, us_ref)):
-        term = nn(turned[...], grad_pre).astype(BF)
-        keep[...] = term[:half]
-        send[...] = term[half:]
+    quarter = gk_ref.shape[0] // 2
+    rows_of = lambda a, i: a[i * quarter : (i + 1) * quarter]
+    for grad_pre, keep, send, quarters in ((grad_gate, gk_ref, gs_ref, (0, 1, 2, 3)), (grad_up, uk_ref, us_ref, (0, 2, 1, 3))):
+        term = nn(turned_ref[...], grad_pre).astype(BF)
+        for i in range(2):
+            keep[i * quarter : (i + 1) * quarter] = rows_of(term, quarters[i])
+            send[i * quarter : (i + 1) * quarter] = rows_of(term, quarters[2 + i])
     out = nn(active, wd)
     back = nt(grad_gate, wg) + nt(grad_up, wu)
     for ref, part in zip(sums, (out[:rows], out[rows:], back[:rows], back[rows:])):
@@ -418,7 +428,7 @@
     return jax.ShapeDtypeStruct(dims, dtype)
 
 
-def mlp(mine, theirs, seed_mine, seed_theirs, order_gate, order_up, w_gate, w_up, w_d):
+def mlp(mine, theirs, seed_mine, seed_theirs, order, w_gate, w_up, w_d):
     rows, width = mine.shape
     half = w_gate.shape[1]
     cols = lambda size: pl.BlockSpec((size, TILE), lambda i: (0, i))
@@ -427,14 +437,14 @@
     return pl.pallas_call(
         functools.partial(mlp_kernel, half),
         grid=(pl.cdiv(half, TILE),),
-        in_specs=[part] * 4 + [fixed(width, width)] * 2 + [cols(width)] * 2 + [down],
+        in_specs=[part] * 4 + [fixed(width, width)] + [cols(width)] * 2 + [down],
         out_specs=[part] * 4 + [down] + [cols(width // 2)] * 4,
         out_shape=[shaped(F32, rows, width)] * 4 + [shaped(BF, half, width)] + [shaped(BF, width // 2, half)] * 4,
-        scratch_shapes=[pltpu.VMEM((2 * rows, width), BF)] * 2 + [pltpu.VMEM((width, 2 * rows), BF)] * 2,
+        scratch_shapes=[pltpu.VMEM((2 * rows, width), BF)] * 2 + [pltpu.VMEM((width, 2 * rows), BF)],
         compiler_params=params(),
         cost_estimate=cost(40),
         name="mlp",
-    )(mine, theirs, seed_mine, seed_theirs, order_gate, order_up, w_gate, w_up, w_d)
+    )(mine, theirs, seed_mine, seed_theirs, order, w_gate, w_up, w_d)
 
 
 def middle_kernel(bm_ref, bt_ref, middle_ref, seed_ref, g_ref, w_ref, gm_ref, gb_ref, gx_ref, gain_ref):
@@ -564,7 +574,7 @@
 Z, Y, X = SEQ
 X_FIRST = ((X, 1), (Y, 1), (Z, 1), (Z, 2))
 Y_FIRST = ((Y, 1), (X, 1), (Z, 1), (Z, 2))
-Z_FIRST = ((Z, 1), (Z, 2), (X, 1), (Y, 1))
+Z_FIRST = ((Z, 1), (X, 1), (Y, 1), (Z, 2))
 KEY_GATHER = ((Y, 1), (X, 1), (Z, 2), (Z, 1))
 VALUE_GATHER = X_FIRST
 
@@ -685,10 +695,10 @@
         self.got = pair_up(self.all, *self.steps.pop(0))
 
     def go(self, order):
+        if not self.steps:
+            return self.all, self.got
         self.all = order(lambda a, b: jnp.concatenate([a, b], 0), self.all, self.got)
-        if self.steps:
-            self.got = pair_up(self.all, *self.steps.pop(0))
-        return self.all
+        self.got = pair_up(self.all, *self.steps.pop(0))
 
 
 def to_owner(a, order):
@@ -735,8 +745,8 @@
     sin = jnp.sin(angle) * sign
 
     x = inputs.reshape(tokens, width)
-    bias = b_qkv.reshape(1, -1)
-    normed, k, v = project_kv(x, w_qkv, bias, g_attn.reshape(1, -1), cos, sin)
+    small = jnp.concatenate([b_qkv, g_attn]).reshape(1, -1)
+    normed, k, v = project_kv(x, w_qkv, small, cos, sin)
     k, v = k.reshape(streams, length, KW), v.reshape(streams, length, KW)
     half = FF // 2
 
@@ -751,7 +761,7 @@
         spots = jnp.stack(
             [*map(spots_of_devices, (KEY_GATHER, VALUE_GATHER)), *map(devices_at_spots, (Y_FIRST, X_FIRST))]
         ).astype(jnp.int32)
-        return start_rows, spots, row_order(X_FIRST, width), row_order(Y_FIRST, width)
+        return start_rows, spots, row_order(X_FIRST, width)
 
     cut_cols = lambda w, first: lax.dynamic_slice_in_dim(w, first + core * half, half, 1)
     cut_rows = lambda w: lax.dynamic_slice_in_dim(w, core * half, half, 0)
@@ -760,7 +770,7 @@
     if fast:
         keys = Doubling(KEY_GATHER, k)
         values = Doubling(VALUE_GATHER, v)
-        q = order(project_q, normed, w_qkv, bias, cos, sin)
+        q = order(project_q, normed, w_qkv, small, cos, sin)
         keys.go(order), values.go(order)
         seed = order(lambda c: (c * valid[..., None].astype(BF)).reshape(tokens, width), cotangent)
         w_gate = order(functools.partial(cut_cols, first=0), w_gate_up)
@@ -769,16 +779,17 @@
         w_d = order(cut_rows, w_down)
         keys.go(order), values.go(order)
         seed_theirs = other_core(seed)
-        start_rows, spots, order_x, order_y = order(small_inputs, begins)
+        start_rows, spots, order_x = order(small_inputs, begins)
         normed_t = order(lambda a, b: nt(a, b).astype(BF), order_x, normed)
         k_all, v_all = keys.go(order), values.go(order)
     else:
-        k_all, v_all = lax.all_gather(k, SEQ, axis=0), lax.all_gather(v, SEQ, axis=0)
-        q = project_q(normed, w_qkv, bias, cos, sin)
+        in_halves = lambda a: (a[: n // 2], a[n // 2 :])
+        k_all, v_all = [in_halves(lax.all_gather(a, SEQ, axis=0)) for a in (k, v)]
+        q = project_q(normed, w_qkv, small, cos, sin)
         seed = (cotangent * valid[..., None].astype(BF)).reshape(tokens, width)
         seed_theirs = other_core(seed)
         w_gate, w_up, w_d = cut_cols(w_gate_up, 0), cut_cols(w_gate_up, FF), cut_rows(w_down)
-        start_rows, spots, order_x, order_y = small_inputs(begins)
+        start_rows, spots, order_x = small_inputs(begins)
         normed_t = nt(order_x, normed).astype(BF)
     low = begins[:, 0] // (GROUP * length)
     me_1 = jnp.reshape(me, (1,)).astype(jnp.int32)
@@ -792,7 +803,7 @@
     normed_mlp = (unit_mlp * gain_mlp).astype(BF)
     normed_theirs = other_core(normed_mlp)
     out_mine, out_theirs, back_mine, back_theirs, term_down, keep_gate, send_gate, keep_up, send_up = mlp(
-        normed_mlp, normed_theirs, seed, seed_theirs, order_x, order_y, w_gate, w_up, w_d
+        normed_mlp, normed_theirs, seed, seed_theirs, order_x, w_gate, w_up, w_d
     )
     order = Order(back_mine)
     back_theirs = other_core(back_theirs)
@@ -896,7 +907,8 @@
         rows_kv = add(rows_kv, other_core(rows_kv))
         sums = sum_over_all(sums.reshape(-1, LANES)).reshape(-1)
         rows_gate = reduce_rows(jnp.concatenate([keep_gate, send_gate], 0))
-        rows_up = reduce_rows(jnp.concatenate([keep_up, send_up], 0))
+        cut_up = keep_up.shape[0] // 2
+        rows_up = reduce_rows(jnp.concatenate([keep_up[:cut_up], send_up[:cut_up], keep_up[cut_up:], send_up[cut_up:]], 0))
         rows_down = reduce_rows(term_down)
 
     rows_down = to_owner(rows_down, Z_FIRST)
@@ -919,8 +931,8 @@
 
 PARTS = 1
 PLAN = (
-    "ab:0", "gu:0", "gu:1", "down", "keys:0:0", "keys:0:1", "terms", "attn0", "keys:0", "down", "keys:0",
-    "gu", "finish", "attn", "keys:0", "down", "last", "gu", "kv", "attn", "kv", "attn", "kv", "gu", "down",
+    "ab:0", "terms", "gu:0", "gu:1", "keys:0:0", "keys:0:1", "down", "keys:0", "attn0", "keys:0", "gu",
+    "keys:0", "down", "last", "attn", "gu", "kv", "attn", "down", "kv", "attn", "kv", "finish", "gu", "down",
     "attn", "kv",
 )
 

time: 367 us -> 336 us (0.916); the launches traced: 361 us -> 335 us
  waiting for transfers between devices: 124 us -> 99.3 us
  starting transfers between devices: 46.2 us -> 64.8 us
  local copies, waits for them, and re-layouts: 36 us -> 24.3 us
  other arithmetic: 40.5 us -> 34.6 us
    ppermute x32, waiting for transfers between devices: 121 us -> 97.7 us  [pair_up(): lax.ppermute(a, axis, [(i, i ^ step) for i in range(lax.axis_size(axis))])]
    ppermute x32, starting transfers between devices: 39.7 us -> 55.1 us  [pair_up(): lax.ppermute(a, axis, [(i, i ^ step) for i in range(lax.axis_size(axis))])]
    convert_element_type x26, other arithmetic: 24.4 us -> 18.2 us  [total(): functools.reduce(lambda a, b: a + b, [a.astype(F32) for a in terms])]
    unnamed x79 -> x63, local copies, waits for them, and re-layouts: 9.12 us -> 3.47 us
    concatenate x8 -> x6, local copies, waits for them, and re-layouts: 5.11 us -> 0.19 us  [go(): jnp.concatenate([a, b], 0)]
  transfers between devices with their start and end apart: 43 -> 43, of which waited for: 17 -> 20; matrix products, arithmetic and copies ran while one was open for 19% -> 16% of each run, Pallas kernels for 14% -> 17%
where the time goes in v1:
time: 336 us; the launch traced here: 335 us
  Pallas kernels  106 us (32%)
  waiting for transfers between devices  99.3 us (30%)
  starting transfers between devices  64.8 us (19%)
  other arithmetic  34.6 us (10%)
  local copies, waits for them, and re-layouts  24.3 us (7%)
  matrix products  4.06 us (1%)
    ppermute x32, waiting for transfers between devices, pair_up(): lax.ppermute(a, axis, [(i, i ^ step) for i in range(lax.axis_size(axis))])  97.7 us
    ppermute x32, starting transfers between devices, pair_up(): lax.ppermute(a, axis, [(i, i ^ step) for i in range(lax.axis_size(axis))])  55.1 us
    pallas_call x1, Pallas kernels, mlp(): pl.pallas_call(functools.partial(mlp_kernel, half), grid=(pl.cdiv(half, T...  46.2 us
    pallas_call x1, Pallas kernels, attend_back(): pl.pallas_call(functools.partial(backward_kernel, first), grid_spec=pltpu...  19.8 us
    convert_element_type x26, other arithmetic, total(): functools.reduce(lambda a, b: a + b, [a.astype(F32) for a in terms])  18.2 us
    pallas_call x1, Pallas kernels, attend(): pl.pallas_call(forward_kernel, grid_spec=pltpu.PrefetchScalarGridSpec(num...  13.5 us
    dynamic_slice x2, local copies, waits for them, and re-layouts, shards(): lax.dynamic_slice_in_dim(w, first + core * half, half, 1)  9.71 us
    ppermute x10, starting transfers between devices, other_core(): return lax.ppermute(a, 'dp', [(0, 1), (1, 0)])  9.06 us
  transfers between devices with their start and end apart: 43, of which 20 were waited for; matrix products, arithmetic and copies ran while one was open for 16% of the time, Pallas kernels for 17%

profile of v1, /device:TPU:0, one launch (start us, length us, event | category | flops | bytes accessed | tf_op | source)
XLA Modules:
  0.0 334.7 jit_solution(12187563633438273060)
XLA Ops:
  4.8 3.4 %project_kv.1 = (bf16[384,896]{1,0:T(8,128)(2,1)}, bf16[384,128]{1,0:T(8,128)(2,1)}, bf16[384,128]{1,0:T(8,128)(2,1)}) custom-call(bf16[384,896]{1,0:T(8,128)(2,1)} %bitcast.35, bf16[896,1152]{1,0:T(8,128)(2,1)} %w_ref.4, bf16[1,2048]{1,0:T(2,128)(2,1)} %reshape.374.small_ref.b_ref, f32[384,128]{1,0:T(8,128)} %get-tuple-element.264.cos_ref, ...), custom_call_target="tpu_custom_call" | custom-call | flops 270000000 | bytes 65536 | tf_op jit(solution)/shard_map/project_kv/pallas_call | solution.py:89
  8.2 3.0 collective-permute-start
  11.2 2.6 collective-permute-start.2
  14.2 4.0 %project_q.1 = bf16[384,896]{1,0:T(8,128)(2,1)} custom-call(bf16[384,896]{1,0:T(8,128)(2,1)} %get-tuple-element.255.normed_ref, bf16[896,1152]{1,0:T(8,128)(2,1)} %w_ref.4, bf16[1,2048]{1,0:T(2,128)(2,1)} %reshape.374.small_ref.b_ref, f32[384,128]{1,0:T(8,128)} %get-tuple-element.264.cos_ref, f32[384,128]{1,0:T(8,128)} %get-tuple-element.265.sin_ref), custom_call_target="tpu_custom_call" | custom-call | flops 360000000 | bytes 65536 | tf_op jit(solution)/shard_map/project_q/pallas_call | solution.py:125
  20.1 5.0 %constant_dynamic-slice_fusion.3.wg_ref = bf16[896,2432]{1,0:T(8,128)(2,1)} fusion(bf16[896,9728]{1,0:T(8,128)(2,1)} %param.17, s32[]{:T(128)S(6)} %select_n.255), kind=kLoop, calls=%fused_computation.96 | loop fusion | bytes 8716292 | tf_op jit(solution)/shard_map/dynamic_slice | solution.py:766
  25.1 4.3 %collective-permute-done.1 = bf16[2,4,96,128]{3,2,1,0:T(8,128)(2,1)S(1)} collective-permute-done((bf16[2,4,96,128]{3,2,1,0:T(8,128)(2,1)S(1)}, bf16[2,4,96,128]{3,2,1,0:T(8,128)(2,1)S(1)}, u32[]{:S(2)}, u32[]{:S(2)}) %collective-permute-start.1) | collective-permute-done | bytes 196640 | tf_op jit(solution)/shard_map/ppermute | solution.py:563
  32.7 4.7 %constant_dynamic-slice_fusion.2.wu_ref = bf16[896,2432]{1,0:T(8,128)(2,1)} fusion(bf16[896,9728]{1,0:T(8,128)(2,1)} %param.17, s32[]{:T(128)S(6)} %select_n.256), kind=kLoop, calls=%fused_computation.95 | loop fusion | bytes 8716292 | tf_op jit(solution)/shard_map/dynamic_slice | solution.py:766
  46.2 14.7 %collective-permute-done.7.v2_ref = bf16[8,4,96,128]{3,2,1,0:T(8,128)(2,1)} collective-permute-done((bf16[8,4,96,128]{3,2,1,0:T(8,128)(2,1)S(1)}, bf16[8,4,96,128]{3,2,1,0:T(8,128)(2,1)}, u32[]{:S(2)}, u32[]{:S(2)}) %collective-permute-start.7) | collective-permute-done | bytes 786464 | tf_op jit(solution)/shard_map/ppermute | solution.py:563
  60.9 13.5 %attend.1 = (bf16[4,96,896]{2,1,0:T(8,128)(2,1)}, f32[4,2,768]{2,1,0:T(2,128)}) custom-call(s32[4]{0:T(128)} %add_select_fusion.1.low_ref, s32[1]{0:T(128)} %bitcast.1.me_ref, s32[4,16]{1,0:T(4,128)} %pad_add_fusion.1.spot_ref, bf16[4,96,896]{2,1,0:T(8,128)(2,1)} %bitcast.48, bf16[8,4,96,128]{3,2,1,0:T(8,128)(2,1)} %copy-done.19, ...), custom_call_target="tpu_custom_call" | custom-call | flops 1620000000 | bytes 65536 | tf_op jit(solution)/shard_map/attend/pallas_call | solution.py:219
  80.3 46.2 %mlp.1 = (f32[384,896]{1,0:T(8,128)}, f32[384,896]{1,0:T(8,128)}, f32[384,896]{1,0:T(8,128)}, f32[384,896]{1,0:T(8,128)}, bf16[2432,896]{1,0:T(8,128)(2,1)}, /*i...) custom-call(bf16[384,896]{1,0:T(8,128)(2,1)} %copy-done.4, ...), custom_call_target="tpu_custom_call" | custom-call | flops 3600000000 | bytes 65536 | tf_op jit(solution)/shard_map/mlp/pallas_call | solution.py:437
  131.4 3.2 constant_dynamic-slice_fusion
  134.6 6.4 %middle_back.1 = (f32[384,896]{1,0:T(8,128)}, bf16[384,896]{1,0:T(8,128)(2,1)}, bf16[384,896]{1,0:T(8,128)(2,1)}, f32[1,896]{1,0:T(1,128)}) custom-call(f32[384,896]{1,0:T(8,128)} %get-tuple-element.196.bm_ref, f32[384,896]{1,0:T(8,128)} %collective-permute-done.11.bt_ref, f32[384,896]{1,0:T(8,128)} %copy-done.1, bf16[384,896]{1,0:T(8,128)(2,1)} %bitcast.32, ...), custom_call_target="tpu_custom_call" | custom-call | flops 450000000 | bytes 65536 | tf_op jit(solution)/shard_map/middle_back/pallas_call | solution.py:472
  141.0 19.8 %attend_back.1 = (bf16[4,96,896]{2,1,0:T(8,128)(2,1)}, bf16[8,4,96,128]{3,2,1,0:T(8,128)(2,1)}, bf16[8,4,96,128]{3,2,1,0:T(8,128)(2,1)}, bf16[8,4,96,128]{3,2,1,0:T(8,128)(2,1)}, bf16[8,4,96,128]{3,2,1,0:T(8,128)(2,1)}) custom-call(s32[4]{0:T(128)} %add_select_fusion.1.low_ref, s32[1]{0:T(128)} %bitcast.1.me_ref, s32[4,16]{1,0:T(4,128)} %pad_add_fusion.1.spot_ref, ...), custom_call_target="tpu_custom_call" | custom-call | flops 2880000000 | bytes 65536 | tf_op jit(solution)/shard_map/attend_back/pallas_call | solution.py:338
  162.9 7.3 %attention_terms.1 = (bf16[896,896]{1,0:T(8,128)(2,1)}, bf16[896,896]{1,0:T(8,128)(2,1)}) custom-call(s32[1]{0:T(128)} %bitcast.12.core_ref, bf16[384,896]{1,0:T(8,128)(2,1)} %get-tuple-element.255.normed_ref, bf16[384,896]{1,0:T(8,128)(2,1)} %bitcast.46, bf16[384,896]{1,0:T(8,128)(2,1)} %bitcast.33, bf16[384,896]{1,0:T(8,128)(2,1)} %get-tuple-element.219.gb_ref, ...), custom_call_target="tpu_custom_call" | custom-call | flops 450000000 | bytes 65536 | tf_op jit(solution)/shard_map/attention_terms/pallas_call | solution.py:496
  170.3 6.6 %collective-permute-done.14 = bf16[448,2432]{1,0:T(8,128)(2,1)S(1)} collective-permute-done((bf16[448,2432]{1,0:T(8,128)(2,1)}, bf16[448,2432]{1,0:T(8,128)(2,1)S(1)}, u32[]{:S(2)}, u32[]{:S(2)}) %collective-permute-start.14) | collective-permute-done | bytes 2179104 | tf_op jit(solution)/shard_map/ppermute | solution.py:563
  180.3 14.5 %collective-permute-done.12 = bf16[3072,128]{1,0:T(8,128)(2,1)S(1)} collective-permute-done((bf16[3072,128]{1,0:T(8,128)(2,1)}, bf16[3072,128]{1,0:T(8,128)(2,1)S(1)}, u32[]{:S(2)}, u32[]{:S(2)}) %collective-permute-start.12) | collective-permute-done | bytes 786464 | tf_op jit(solution)/shard_map/ppermute | solution.py:563
  202.2 4.9 %collective-permute-done.17 = bf16[1536,128]{1,0:T(8,128)(2,1)S(1)} collective-permute-done((bf16[1536,128]{1,0:T(8,128)(2,1)S(1)}, bf16[1536,128]{1,0:T(8,128)(2,1)S(1)}, u32[]{:S(2)}, u32[]{:S(2)}) %collective-permute-start.17) | collective-permute-done | bytes 393248 | tf_op jit(solution)/shard_map/ppermute | solution.py:563
  212.2 6.4 %collective-permute-done.19 = bf16[768,256]{1,0:T(8,128)(2,1)S(1)} collective-permute-done((bf16[768,256]{1,0:T(8,128)(2,1)S(1)}, bf16[768,256]{1,0:T(8,128)(2,1)S(1)}, u32[]{:S(2)}, u32[]{:S(2)}) %collective-permute-start.19) | collective-permute-done | bytes 393248 | tf_op jit(solution)/shard_map/ppermute | solution.py:563
  219.5 10.9 %collective-permute-done.23 = bf16[224,2432]{1,0:T(8,128)(2,1)S(1)} collective-permute-done((bf16[224,2432]{1,0:T(8,128)(2,1)S(1)}, bf16[224,2432]{1,0:T(8,128)(2,1)S(1)}, u32[]{:S(2)}, u32[]{:S(2)}) %collective-permute-start.23) | collective-permute-done | bytes 1089568 | tf_op jit(solution)/shard_map/ppermute | solution.py:563
  230.4 8.9 %collective-permute-start.21 = (bf16[384,256]{1,0:T(8,128)(2,1)S(1)}, bf16[384,256]{1,0:T(8,128)(2,1)S(1)}, u32[]{:S(2)}, u32[]{:S(2)}) collective-permute-start(bf16[384,256]{1,0:T(8,128)(2,1)S(1)} %add_convert_fusion.19), channel_id=1, source_target_pairs={{0,16},{8,24},{16,0},{24,8},{1,17},{9,25},{17,1},{25,9},{2,18},{10... | collective-permute-start | bytes 589832 | tf_op jit(solution)/shard_map/ppermute | solution.py:563
  241.7 2.9 collective-permute-done.21
  245.4 8.3 %collective-permute-done.24 = bf16[608,896]{1,0:T(8,128)(2,1)S(1)} collective-permute-done((bf16[608,896]{1,0:T(8,128)(2,1)S(1)}, bf16[608,896]{1,0:T(8,128)(2,1)S(1)}, u32[]{:S(2)}, u32[]{:S(2)}) %collective-permute-start.24) | collective-permute-done | bytes 1089568 | tf_op jit(solution)/shard_map/ppermute | solution.py:563
  257.4 5.6 %last_back.1 = (f32[384,896]{1,0:T(8,128)}, bf16[896,256]{1,0:T(8,128)(2,1)}, f32[1,2944]{1,0:T(1,128)}) custom-call(bf16[384,256]{1,0:T(8,128)(2,1)} %add_convert_fusion.18.gkv_ref, bf16[384,896]{1,0:T(8,128)(2,1)} %bitcast.34, bf16[896,1152]{1,0:T(8,128)(2,1)} %w_ref.4, bf16[384,896]{1,0:T(8,128)(2,1)} %bitcast.36, bf16[1,896]{1,0:T(2,128)(2,1)} %reshape.386.g_ref, ...), custom_call_target="tpu_custom_call" | custom-call | flops 540000000 | bytes 65536 | tf_op jit(solution)/shard_map/last_back/pallas_call | solution.py:529
  266.2 4.9 %collective-permute-done.27 = bf16[448,896]{1,0:T(8,128)(2,1)} collective-permute-done((bf16[448,896]{1,0:T(8,128)(2,1)}, bf16[448,896]{1,0:T(8,128)(2,1)}, u32[]{:S(2)}, u32[]{:S(2)}) %collective-permute-start.27) | collective-permute-done | bytes 802848 | tf_op jit(solution)/shard_map/ppermute | solution.py:563
  272.9 9.0 %collective-permute-start.35 = (bf16[56,4864]{1,0:T(8,128)(2,1)S(1)}, bf16[56,4864]{1,0:T(8,128)(2,1)S(1)}, u32[]{:S(2)}, u32[]{:S(2)}) collective-permute-start(bf16[56,4864]{1,0:T(8,128)(2,1)S(1)} %add_convert_fusion.8), channel_id=1, source_target_pairs={{0,16},{8,24},{16,0},{24,8},{1,17},{9,25},{17,1},{25,9},{2,18},{10... | collective-permute-start | bytes 1634312 | tf_op jit(solution)/shard_map/ppermute | solution.py:563
  285.8 7.8 %collective-permute-start.34 = (bf16[152,896]{1,0:T(8,128)(2,1)S(1)}, bf16[152,896]{1,0:T(8,128)(2,1)S(1)}, u32[]{:S(2)}, u32[]{:S(2)}) collective-permute-start(bf16[152,896]{1,0:T(8,128)(2,1)S(1)} %add_convert_fusion.16), channel_id=1, source_target_pairs={{0,16},{8,24},{16,0},{24,8},{1,17},{9,25},{17,1},{25,9},{2,18},{10... | collective-permute-start | bytes 817160 | tf_op jit(solution)/shard_map/ppermute | solution.py:563
  295.7 3.3 collective-permute-done.32
  300.0 4.0 %collective-permute-done.31 = bf16[112,384]{1,0:T(8,128)(2,1)S(1)} collective-permute-done((bf16[112,384]{1,0:T(8,128)(2,1)S(1)}, bf16[112,384]{1,0:T(8,128)(2,1)S(1)}, u32[]{:S(2)}, u32[]{:S(2)}) %collective-permute-start.31) | collective-permute-done | bytes 86048 | tf_op jit(solution)/shard_map/ppermute | solution.py:563
  304.2 2.5 add_convert_fusion.6
  306.7 2.5 collective-permute-done.35
  309.4 6.1 %collective-permute-done.34 = bf16[152,896]{1,0:T(8,128)(2,1)S(1)} collective-permute-done((bf16[152,896]{1,0:T(8,128)(2,1)S(1)}, bf16[152,896]{1,0:T(8,128)(2,1)S(1)}, u32[]{:S(2)}, u32[]{:S(2)}) %collective-permute-start.34) | collective-permute-done | bytes 272416 | tf_op jit(solution)/shard_map/ppermute | solution.py:563
  324.1 6.8 %collective-permute-start.42 = (bf16[152,896]{1,0:T(8,128)(2,1)S(1)}, bf16[152,896]{1,0:T(8,128)(2,1)S(1)}, u32[]{:S(2)}, u32[]{:S(2)}) collective-permute-start(bf16[152,896]{1,0:T(8,128)(2,1)S(1)} %collective-permute-done.41), channel_id=1, source_target_pairs={{0,1},{1,0},{2,3},{3,2},{4,5},{5,4},{6,7},{7,6},{8,9},{9,8},{10,11... | collective-permute-start | bytes 817160 | tf_op jit(solution)/shard_map/ppermute | solution.py:559
  (228 shorter events, 79.3 us)
Async XLA Ops:
  18.3 11.1 %collective-permute-start.1 = (bf16[2,4,96,128]{3,2,1,0:T(8,128)(2,1)S(1)}, bf16[2,4,96,128]{3,2,1,0:T(8,128)(2,1)S(1)}, u32[]{:S(2)}, u32[]{:S(2)}) collective-permute-start(bf16[2,4,96,128]{3,2,1,0:T(8,128)(2,1)S(1)} %constant_dynamic-update-slice_fusion), channel_id=1, source_target_pairs={{0,16},{8,24},{16,0},{24,8},{1,17},{9,25},{17,1},{25,9},{2,18},{10... | collective-permute-start | bytes 589832 | tf_op jit(solution)/shard_map/ppermute | solution.py:563
  18.8 12.2 %collective-permute-start.4 = (bf16[2,4,96,128]{3,2,1,0:T(8,128)(2,1)S(1)}, bf16[2,4,96,128]{3,2,1,0:T(8,128)(2,1)S(1)}, u32[]{:S(2)}, u32[]{:S(2)}) collective-permute-start(bf16[2,4,96,128]{3,2,1,0:T(8,128)(2,1)S(1)} %constant_dynamic-update-slice_fusion.2), channel_id=1, source_target_pairs={{0,8},{8,0},{16,24},{24,16},{1,9},{9,1},{17,25},{25,17},{2,10},{10... | collective-permute-start | bytes 589832 | tf_op jit(solution)/shard_map/ppermute | solution.py:563
  29.5 11.1 %collective-permute-start.3 = (bf16[4,4,96,128]{3,2,1,0:T(8,128)(2,1)S(1)}, bf16[4,4,96,128]{3,2,1,0:T(8,128)(2,1)S(1)}, u32[]{:S(2)}, u32[]{:S(2)}) collective-permute-start(bf16[4,4,96,128]{3,2,1,0:T(8,128)(2,1)S(1)} %constant_dynamic-update-slice_fusion.4), channel_id=1, source_target_pairs={{0,2},{2,0},{1,3},{3,1},{4,6},{6,4},{5,7},{7,5},{8,10},{10,8},{9,1... | collective-permute-start | bytes 1179656 | tf_op jit(solution)/shard_map/ppermute | solution.py:563
  31.1 11.2 %collective-permute-start.6 = (bf16[4,4,96,128]{3,2,1,0:T(8,128)(2,1)S(1)}, bf16[4,4,96,128]{3,2,1,0:T(8,128)(2,1)S(1)}, u32[]{:S(2)}, u32[]{:S(2)}) collective-permute-start(bf16[4,4,96,128]{3,2,1,0:T(8,128)(2,1)S(1)} %constant_dynamic-update-slice_fusion.6), channel_id=1, source_target_pairs={{0,4},{4,0},{1,5},{5,1},{2,6},{6,2},{3,7},{7,3},{8,12},{12,8},{9,1... | collective-permute-start | bytes 1179656 | tf_op jit(solution)/shard_map/ppermute | solution.py:563
  40.7 20.2 %collective-permute-start.5 = (bf16[8,4,96,128]{3,2,1,0:T(8,128)(2,1)S(1)}, bf16[8,4,96,128]{3,2,1,0:T(8,128)(2,1)}, u32[]{:S(2)}, u32[]{:S(2)}) collective-permute-start(bf16[8,4,96,128]{3,2,1,0:T(8,128)(2,1)S(1)} %constant_dynamic-update-slice_fusion.8.k1_ref), channel_id=1, source_target_pairs={{0,4},{4,0},{1,5},{5,1},{2,6},{6,2},{3,7},{7,3},{8,12},{12,8},{9,1... | collective-permute-start | bytes 2359304 | tf_op jit(solution)/shard_map/ppermute | solution.py:563
  42.4 18.5 %collective-permute-start.7 = (bf16[8,4,96,128]{3,2,1,0:T(8,128)(2,1)S(1)}, bf16[8,4,96,128]{3,2,1,0:T(8,128)(2,1)}, u32[]{:S(2)}, u32[]{:S(2)}) collective-permute-start(bf16[8,4,96,128]{3,2,1,0:T(8,128)(2,1)S(1)} %constant_dynamic-update-slice_fusion.10.v1_ref), channel_id=1, source_target_pairs={{0,2},{2,0},{1,3},{3,1},{4,6},{6,4},{5,7},{7,5},{8,10},{10,8},{9,1... | collective-permute-start | bytes 2359304 | tf_op jit(solution)/shard_map/ppermute | solution.py:563
  45.4 33.1 %collective-permute-start.9 = (bf16[384,896]{1,0:T(8,128)(2,1)S(1)}, bf16[384,896]{1,0:T(8,128)(2,1)S(1)}, u32[]{:S(2)}, u32[]{:S(2)}) collective-permute-start(bf16[384,896]{1,0:T(8,128)(2,1)S(1)} %bitcast.30), channel_id=1, source_target_pairs={{0,1},{1,0},{2,3},{3,2},{4,5},{5,4},{6,7},{7,6},{8,9},{9,8},{10,11... | collective-permute-start | bytes 2064392 | tf_op jit(solution)/shard_map/ppermute | solution.py:559
  126.4 50.5 %collective-permute-start.14 = (bf16[448,2432]{1,0:T(8,128)(2,1)}, bf16[448,2432]{1,0:T(8,128)(2,1)S(1)}, u32[]{:S(2)}, u32[]{:S(2)}) collective-permute-start(bf16[448,2432]{1,0:T(8,128)(2,1)} %get-tuple-element.213), channel_id=1, source_target_pairs={{0,2},{2,0},{1,3},{3,1},{4,6},{6,4},{5,7},{7,5},{8,10},{10,8},{9,1... | collective-permute-start | bytes 6537224 | tf_op jit(solution)/shard_map/ppermute | solution.py:563
  128.2 50.5 %collective-permute-start.13 = (bf16[448,2432]{1,0:T(8,128)(2,1)}, bf16[448,2432]{1,0:T(8,128)(2,1)}, u32[]{:S(2)}, u32[]{:S(2)}) collective-permute-start(bf16[448,2432]{1,0:T(8,128)(2,1)} %get-tuple-element.211), channel_id=1, source_target_pairs={{0,4},{4,0},{1,5},{5,1},{2,6},{6,2},{3,7},{7,3},{8,12},{12,8},{9,1... | collective-permute-start | bytes 6537224 | tf_op jit(solution)/shard_map/ppermute | solution.py:563
  134.6 65.2 %collective-permute-start.18 = (bf16[1216,896]{1,0:T(8,128)(2,1)}, bf16[1216,896]{1,0:T(8,128)(2,1)S(1)}, u32[]{:S(2)}, u32[]{:S(2)}) collective-permute-start(bf16[1216,896]{1,0:T(8,128)(2,1)} %constant_dynamic-slice_fusion), channel_id=1, source_target_pairs={{0,8},{8,0},{16,24},{24,16},{1,9},{9,1},{17,25},{25,17},{2,10},{10... | collective-permute-start | bytes 6537224 | tf_op jit(solution)/shard_map/ppermute | solution.py:563
  160.8 34.0 %collective-permute-start.12 = (bf16[3072,128]{1,0:T(8,128)(2,1)}, bf16[3072,128]{1,0:T(8,128)(2,1)S(1)}, u32[]{:S(2)}, u32[]{:S(2)}) collective-permute-start(bf16[3072,128]{1,0:T(8,128)(2,1)} %bitcast.59), channel_id=1, source_target_pairs={{0,4},{4,0},{1,5},{5,1},{2,6},{6,2},{3,7},{7,3},{8,12},{12,8},{9,1... | collective-permute-start | bytes 2359304 | tf_op jit(solution)/shard_map/ppermute | solution.py:563
  162.4 33.2 %collective-permute-start.16 = (bf16[3072,128]{1,0:T(8,128)(2,1)}, bf16[3072,128]{1,0:T(8,128)(2,1)}, u32[]{:S(2)}, u32[]{:S(2)}) collective-permute-start(bf16[3072,128]{1,0:T(8,128)(2,1)} %bitcast.58), channel_id=1, source_target_pairs={{0,2},{2,0},{1,3},{3,1},{4,6},{6,4},{5,7},{7,5},{8,10},{10,8},{9,1... | collective-permute-start | bytes 2359304 | tf_op jit(solution)/shard_map/ppermute | solution.py:563
  176.9 32.8 %collective-permute-start.20 = (bf16[896,896]{1,0:T(8,128)(2,1)}, bf16[896,896]{1,0:T(8,128)(2,1)S(1)}, u32[]{:S(2)}, u32[]{:S(2)}) collective-permute-start(bf16[896,896]{1,0:T(8,128)(2,1)} %get-tuple-element.221), channel_id=1, source_target_pairs={{0,1},{1,0},{2,3},{3,2},{4,5},{5,4},{6,7},{7,6},{8,9},{9,8},{10,11... | collective-permute-start | bytes 4816904 | tf_op jit(solution)/shard_map/ppermute | solution.py:559
  194.9 13.2 %collective-permute-start.15 = (bf16[1536,128]{1,0:T(8,128)(2,1)S(1)}, bf16[1536,128]{1,0:T(8,128)(2,1)S(1)}, u32[]{:S(2)}, u32[]{:S(2)}) collective-permute-start(bf16[1536,128]{1,0:T(8,128)(2,1)S(1)} %add_convert_fusion.14), channel_id=1, source_target_pairs={{0,2},{2,0},{1,3},{3,1},{4,6},{6,4},{5,7},{7,5},{8,10},{10,8},{9,1... | collective-permute-start | bytes 1179656 | tf_op jit(solution)/shard_map/ppermute | solution.py:563
  196.7 10.4 %collective-permute-start.17 = (bf16[1536,128]{1,0:T(8,128)(2,1)S(1)}, bf16[1536,128]{1,0:T(8,128)(2,1)S(1)}, u32[]{:S(2)}, u32[]{:S(2)}) collective-permute-start(bf16[1536,128]{1,0:T(8,128)(2,1)S(1)} %add_convert_fusion.13), channel_id=1, source_target_pairs={{0,4},{4,0},{1,5},{5,1},{2,6},{6,2},{3,7},{7,3},{8,12},{12,8},{9,1... | collective-permute-start | bytes 1179656 | tf_op jit(solution)/shard_map/ppermute | solution.py:563
  199.8 104.4 %collective-permute-start.10 = (f32[384,896]{1,0:T(8,128)}, f32[384,896]{1,0:T(8,128)}, u32[]{:S(2)}, u32[]{:S(2)}) collective-permute-start(f32[384,896]{1,0:T(8,128)} %get-tuple-element.191), channel_id=1, source_target_pairs={{0,1},{1,0},{2,3},{3,2},{4,5},{5,4},{6,7},{7,6},{8,9},{9,8},{10,11... | collective-permute-start | bytes 4128776 | tf_op jit(solution)/shard_map/ppermute | solution.py:559
  199.8 30.6 %collective-permute-start.23 = (bf16[224,2432]{1,0:T(8,128)(2,1)S(1)}, bf16[224,2432]{1,0:T(8,128)(2,1)S(1)}, u32[]{:S(2)}, u32[]{:S(2)}) collective-permute-start(bf16[224,2432]{1,0:T(8,128)(2,1)S(1)} %add_convert_fusion.4), channel_id=1, source_target_pairs={{0,2},{2,0},{1,3},{3,1},{4,6},{6,4},{5,7},{7,5},{8,10},{10,8},{9,1... | collective-permute-start | bytes 3268616 | tf_op jit(solution)/shard_map/ppermute | solution.py:563
  207.1 32.2 %collective-permute-start.22 = (bf16[224,2432]{1,0:T(8,128)(2,1)S(1)}, bf16[224,2432]{1,0:T(8,128)(2,1)S(1)}, u32[]{:S(2)}, u32[]{:S(2)}) collective-permute-start(bf16[224,2432]{1,0:T(8,128)(2,1)S(1)} %add_convert_fusion.5), channel_id=1, source_target_pairs={{0,4},{4,0},{1,5},{5,1},{2,6},{6,2},{3,7},{7,3},{8,12},{12,8},{9,1... | collective-permute-start | bytes 3268616 | tf_op jit(solution)/shard_map/ppermute | solution.py:563
  209.7 44.1 %collective-permute-start.24 = (bf16[608,896]{1,0:T(8,128)(2,1)S(1)}, bf16[608,896]{1,0:T(8,128)(2,1)S(1)}, u32[]{:S(2)}, u32[]{:S(2)}) collective-permute-start(bf16[608,896]{1,0:T(8,128)(2,1)S(1)} %add_convert_fusion.3), channel_id=1, source_target_pairs={{0,2},{2,0},{1,3},{3,1},{4,6},{6,4},{5,7},{7,5},{8,10},{10,8},{9,1... | collective-permute-start | bytes 3268616 | tf_op jit(solution)/shard_map/ppermute | solution.py:563
  218.6 52.4 %collective-permute-start.27 = (bf16[448,896]{1,0:T(8,128)(2,1)}, bf16[448,896]{1,0:T(8,128)(2,1)}, u32[]{:S(2)}, u32[]{:S(2)}) collective-permute-start(bf16[448,896]{1,0:T(8,128)(2,1)} %dynamic_slice.276), channel_id=1, source_target_pairs={{0,2},{2,0},{1,3},{3,1},{4,6},{6,4},{5,7},{7,5},{8,10},{10,8},{9,1... | collective-permute-start | bytes 2408456 | tf_op jit(solution)/shard_map/ppermute | solution.py:563
  230.4 14.3 %collective-permute-start.21 = (bf16[384,256]{1,0:T(8,128)(2,1)S(1)}, bf16[384,256]{1,0:T(8,128)(2,1)S(1)}, u32[]{:S(2)}, u32[]{:S(2)}) collective-permute-start(bf16[384,256]{1,0:T(8,128)(2,1)S(1)} %add_convert_fusion.19), channel_id=1, source_target_pairs={{0,16},{8,24},{16,0},{24,8},{1,17},{9,25},{17,1},{25,9},{2,18},{10... | collective-permute-start | bytes 589832 | tf_op jit(solution)/shard_map/ppermute | solution.py:563
  241.5 31.3 %collective-permute-start.26 = (bf16[112,4864]{1,0:T(8,128)(2,1)S(1)}, bf16[112,4864]{1,0:T(8,128)(2,1)S(1)}, u32[]{:S(2)}, u32[]{:S(2)}) collective-permute-start(bf16[112,4864]{1,0:T(8,128)(2,1)S(1)} %fusion.1), channel_id=1, source_target_pairs={{0,8},{8,0},{16,24},{24,16},{1,9},{9,1},{17,25},{25,17},{2,10},{10... | collective-permute-start | bytes 3268616 | tf_op jit(solution)/shard_map/ppermute | solution.py:563
  256.8 27.8 %collective-permute-start.29 = (bf16[304,896]{1,0:T(8,128)(2,1)}, bf16[304,896]{1,0:T(8,128)(2,1)}, u32[]{:S(2)}, u32[]{:S(2)}) collective-permute-start(bf16[304,896]{1,0:T(8,128)(2,1)} %add_convert_fusion.9), channel_id=1, source_target_pairs={{0,4},{4,0},{1,5},{5,1},{2,6},{6,2},{3,7},{7,3},{8,12},{12,8},{9,1... | collective-permute-start | bytes 1634312 | tf_op jit(solution)/shard_map/ppermute | solution.py:563
  265.0 16.9 %collective-permute-start.25 = (bf16[448,384]{1,0:T(8,128)(2,1)S(1)}, bf16[448,384]{1,0:T(8,128)(2,1)S(1)}, u32[]{:S(2)}, u32[]{:S(2)}) collective-permute-start(bf16[448,384]{1,0:T(8,128)(2,1)S(1)} %dynamic_slice.277), channel_id=1, source_target_pairs={{0,2},{2,0},{1,3},{3,1},{4,6},{6,4},{5,7},{7,5},{8,10},{10,8},{9,1... | collective-permute-start | bytes 1032200 | tf_op jit(solution)/shard_map/ppermute | solution.py:563
  272.2 11.4 %collective-permute-start.30 = (bf16[224,896]{1,0:T(8,128)(2,1)S(1)}, bf16[224,896]{1,0:T(8,128)(2,1)S(1)}, u32[]{:S(2)}, u32[]{:S(2)}) collective-permute-start(bf16[224,896]{1,0:T(8,128)(2,1)S(1)} %add_convert_fusion.10), channel_id=1, source_target_pairs={{0,4},{4,0},{1,5},{5,1},{2,6},{6,2},{3,7},{7,3},{8,12},{12,8},{9,1... | collective-permute-start | bytes 1204232 | tf_op jit(solution)/shard_map/ppermute | solution.py:563
  272.9 36.3 %collective-permute-start.35 = (bf16[56,4864]{1,0:T(8,128)(2,1)S(1)}, bf16[56,4864]{1,0:T(8,128)(2,1)S(1)}, u32[]{:S(2)}, u32[]{:S(2)}) collective-permute-start(bf16[56,4864]{1,0:T(8,128)(2,1)S(1)} %add_convert_fusion.8), channel_id=1, source_target_pairs={{0,16},{8,24},{16,0},{24,8},{1,17},{9,25},{17,1},{25,9},{2,18},{10... | collective-permute-start | bytes 1634312 | tf_op jit(solution)/shard_map/ppermute | solution.py:563
  282.0 11.7 %collective-permute-start.28 = (bf16[224,384]{1,0:T(8,128)(2,1)S(1)}, bf16[224,384]{1,0:T(8,128)(2,1)S(1)}, u32[]{:S(2)}, u32[]{:S(2)}) collective-permute-start(bf16[224,384]{1,0:T(8,128)(2,1)S(1)} %add_convert_fusion.20), channel_id=1, source_target_pairs={{0,4},{4,0},{1,5},{5,1},{2,6},{6,2},{3,7},{7,3},{8,12},{12,8},{9,1... | collective-permute-start | bytes 516104 | tf_op jit(solution)/shard_map/ppermute | solution.py:563
  284.5 14.5 %collective-permute-start.32 = (bf16[112,896]{1,0:T(8,128)(2,1)S(1)}, bf16[112,896]{1,0:T(8,128)(2,1)S(1)}, u32[]{:S(2)}, u32[]{:S(2)}) collective-permute-start(bf16[112,896]{1,0:T(8,128)(2,1)S(1)} %add_convert_fusion.17), channel_id=1, source_target_pairs={{0,8},{8,0},{16,24},{24,16},{1,9},{9,1},{17,25},{25,17},{2,10},{10... | collective-permute-start | bytes 602120 | tf_op jit(solution)/shard_map/ppermute | solution.py:563
  285.8 29.7 %collective-permute-start.34 = (bf16[152,896]{1,0:T(8,128)(2,1)S(1)}, bf16[152,896]{1,0:T(8,128)(2,1)S(1)}, u32[]{:S(2)}, u32[]{:S(2)}) collective-permute-start(bf16[152,896]{1,0:T(8,128)(2,1)S(1)} %add_convert_fusion.16), channel_id=1, source_target_pairs={{0,16},{8,24},{16,0},{24,8},{1,17},{9,25},{17,1},{25,9},{2,18},{10... | collective-permute-start | bytes 817160 | tf_op jit(solution)/shard_map/ppermute | solution.py:563
  293.7 10.4 %collective-permute-start.31 = (bf16[112,384]{1,0:T(8,128)(2,1)S(1)}, bf16[112,384]{1,0:T(8,128)(2,1)S(1)}, u32[]{:S(2)}, u32[]{:S(2)}) collective-permute-start(bf16[112,384]{1,0:T(8,128)(2,1)S(1)} %add_convert_fusion.23), channel_id=1, source_target_pairs={{0,8},{8,0},{16,24},{24,16},{1,9},{9,1},{17,25},{25,17},{2,10},{10... | collective-permute-start | bytes 258056 | tf_op jit(solution)/shard_map/ppermute | solution.py:563
  300.0 17.7 %collective-permute-start.33 = (bf16[56,896]{1,0:T(8,128)(2,1)S(1)}, bf16[56,896]{1,0:T(8,128)(2,1)S(1)}, u32[]{:S(2)}, u32[]{:S(2)}) collective-permute-start(bf16[56,896]{1,0:T(8,128)(2,1)S(1)} %add_convert_fusion.22), channel_id=1, source_target_pairs={{0,16},{8,24},{16,0},{24,8},{1,17},{9,25},{17,1},{25,9},{2,18},{10... | collective-permute-start | bytes 301064 | tf_op jit(solution)/shard_map/ppermute | solution.py:563
  304.1 14.5 %collective-permute-start.37 = (bf16[56,384]{1,0:T(8,128)(2,1)S(1)}, bf16[56,384]{1,0:T(8,128)(2,1)S(1)}, u32[]{:S(2)}, u32[]{:S(2)}) collective-permute-start(bf16[56,384]{1,0:T(8,128)(2,1)S(1)} %add_convert_fusion.26), channel_id=1, source_target_pairs={{0,16},{8,24},{16,0},{24,8},{1,17},{9,25},{17,1},{25,9},{2,18},{10... | collective-permute-start | bytes 129032 | tf_op jit(solution)/shard_map/ppermute | solution.py:563
  (39 other events, 417.5 us)

commit v2 on v1

--- a/solution.py
+++ b/solution.py
@@ -574,7 +574,7 @@
 Z, Y, X = SEQ
 X_FIRST = ((X, 1), (Y, 1), (Z, 1), (Z, 2))
 Y_FIRST = ((Y, 1), (X, 1), (Z, 1), (Z, 2))
-Z_FIRST = ((Z, 1), (X, 1), (Y, 1), (Z, 2))
+Z_FIRST = ((Z, 1), (Y, 1), (X, 1), (Z, 2))
 KEY_GATHER = ((Y, 1), (X, 1), (Z, 2), (Z, 1))
 VALUE_GATHER = X_FIRST
 
@@ -931,8 +931,8 @@
 
 PARTS = 1
 PLAN = (
-    "ab:0", "terms", "gu:0", "gu:1", "keys:0:0", "keys:0:1", "down", "keys:0", "attn0", "keys:0", "gu",
-    "keys:0", "down", "last", "attn", "gu", "kv", "attn", "down", "kv", "attn", "kv", "finish", "gu", "down",
+    "ab:0", "terms", "gu:0", "gu:1", "keys:0:0", "keys:0:1", "keys:0", "down", "attn0", "keys:0", "gu",
+    "finish", "keys:0", "down", "last", "attn", "gu", "kv", "attn", "down", "kv", "attn", "kv", "gu", "down",
     "attn", "kv",
 )
 

time: 336 us -> 329 us (0.979)
  waiting for transfers between devices: 99.3 us -> 85.7 us
  local copies, waits for them, and re-layouts: 24.3 us -> 29 us
    ppermute x32, waiting for transfers between devices: 97.7 us -> 84.1 us  [pair_up(): lax.ppermute(a, axis, [(i, i ^ step) for i in range(lax.axis_size(axis))])]
    unnamed x63 -> x91, local copies, waits for them, and re-layouts: 3.47 us -> 7.61 us
  transfers between devices with their start and end apart: 43 -> 43, of which waited for: 20 -> 18; matrix products, arithmetic and copies ran while one was open for 16% -> 17% of each run, Pallas kernels for 17% -> 17%
where the time goes in v2:
time: 329 us; the launch traced here: 327 us
  Pallas kernels  106 us (32%)
  waiting for transfers between devices  85.7 us (26%)
  starting transfers between devices  63.9 us (19%)
  other arithmetic  36.4 us (11%)
  local copies, waits for them, and re-layouts  29 us (9%)
  matrix products  4.1 us (1%)
    ppermute x32, waiting for transfers between devices, pair_up(): lax.ppermute(a, axis, [(i, i ^ step) for i in range(lax.axis_size(axis))])  84.1 us
    ppermute x32, starting transfers between devices, pair_up(): lax.ppermute(a, axis, [(i, i ^ step) for i in range(lax.axis_size(axis))])  53.8 us
    pallas_call x1, Pallas kernels, mlp(): pl.pallas_call(functools.partial(mlp_kernel, half), grid=(pl.cdiv(half, T...  46 us
    convert_element_type x26, other arithmetic, total(): functools.reduce(lambda a, b: a + b, [a.astype(F32) for a in terms])  20.8 us
    pallas_call x1, Pallas kernels, attend_back(): pl.pallas_call(functools.partial(backward_kernel, first), grid_spec=pltpu...  19.8 us
    pallas_call x1, Pallas kernels, attend(): pl.pallas_call(forward_kernel, grid_spec=pltpu.PrefetchScalarGridSpec(num...  13.5 us
    dynamic_slice x2, local copies, waits for them, and re-layouts, shards(): lax.dynamic_slice_in_dim(w, first + core * half, half, 1)  9.69 us
    ppermute x10, starting transfers between devices, other_core(): return lax.ppermute(a, 'dp', [(0, 1), (1, 0)])  9.35 us
  transfers between devices with their start and end apart: 43, of which 18 were waited for; matrix products, arithmetic and copies ran while one was open for 17% of the time, Pallas kernels for 17%

profile of v2, /device:TPU:0, one launch (start us, length us, event | category | flops | bytes accessed | tf_op | source)
XLA Modules:
  0.0 326.5 jit_solution(7571710155951743457)
XLA Ops:
  4.8 3.4 %project_kv.1 = (bf16[384,896]{1,0:T(8,128)(2,1)}, bf16[384,128]{1,0:T(8,128)(2,1)}, bf16[384,128]{1,0:T(8,128)(2,1)}) custom-call(bf16[384,896]{1,0:T(8,128)(2,1)} %bitcast.35, bf16[896,1152]{1,0:T(8,128)(2,1)} %w_ref.4, bf16[1,2048]{1,0:T(2,128)(2,1)} %reshape.374.small_ref.b_ref, f32[384,128]{1,0:T(8,128)} %get-tuple-element.267.cos_ref, ...), custom_call_target="tpu_custom_call" | custom-call | flops 270000000 | bytes 65536 | tf_op jit(solution)/shard_map/project_kv/pallas_call | solution.py:89
  8.2 3.1 collective-permute-start
  11.3 2.6 collective-permute-start.2
  14.3 4.0 %project_q.1 = bf16[384,896]{1,0:T(8,128)(2,1)} custom-call(bf16[384,896]{1,0:T(8,128)(2,1)} %get-tuple-element.258.normed_ref, bf16[896,1152]{1,0:T(8,128)(2,1)} %w_ref.4, bf16[1,2048]{1,0:T(2,128)(2,1)} %reshape.374.small_ref.b_ref, f32[384,128]{1,0:T(8,128)} %get-tuple-element.267.cos_ref, f32[384,128]{1,0:T(8,128)} %get-tuple-element.268.sin_ref), custom_call_target="tpu_custom_call" | custom-call | flops 360000000 | bytes 65536 | tf_op jit(solution)/shard_map/project_q/pallas_call | solution.py:125
  20.2 5.0 %constant_dynamic-slice_fusion.3.wg_ref = bf16[896,2432]{1,0:T(8,128)(2,1)} fusion(bf16[896,9728]{1,0:T(8,128)(2,1)} %param.17, s32[]{:T(128)S(6)} %select_n.255), kind=kLoop, calls=%fused_computation.96 | loop fusion | bytes 8716292 | tf_op jit(solution)/shard_map/dynamic_slice | solution.py:766
  25.2 4.3 %collective-permute-done.1 = bf16[2,4,96,128]{3,2,1,0:T(8,128)(2,1)S(1)} collective-permute-done((bf16[2,4,96,128]{3,2,1,0:T(8,128)(2,1)S(1)}, bf16[2,4,96,128]{3,2,1,0:T(8,128)(2,1)S(1)}, u32[]{:S(2)}, u32[]{:S(2)}) %collective-permute-start.1) | collective-permute-done | bytes 196640 | tf_op jit(solution)/shard_map/ppermute | solution.py:563
  32.8 4.6 %constant_dynamic-slice_fusion.2.wu_ref = bf16[896,2432]{1,0:T(8,128)(2,1)} fusion(bf16[896,9728]{1,0:T(8,128)(2,1)} %param.17, s32[]{:T(128)S(6)} %select_n.256), kind=kLoop, calls=%fused_computation.95 | loop fusion | bytes 8716292 | tf_op jit(solution)/shard_map/dynamic_slice | solution.py:766
  37.5 2.4 constant_dynamic-slice_fusion.1.wd_ref
  46.2 14.7 %collective-permute-done.7.v2_ref = bf16[8,4,96,128]{3,2,1,0:T(8,128)(2,1)} collective-permute-done((bf16[8,4,96,128]{3,2,1,0:T(8,128)(2,1)S(1)}, bf16[8,4,96,128]{3,2,1,0:T(8,128)(2,1)}, u32[]{:S(2)}, u32[]{:S(2)}) %collective-permute-start.7) | collective-permute-done | bytes 786464 | tf_op jit(solution)/shard_map/ppermute | solution.py:563
  61.0 13.5 %attend.1 = (bf16[4,96,896]{2,1,0:T(8,128)(2,1)}, f32[4,2,768]{2,1,0:T(2,128)}) custom-call(s32[4]{0:T(128)} %add_select_fusion.1.low_ref, s32[1]{0:T(128)} %bitcast.1.me_ref, s32[4,16]{1,0:T(4,128)} %pad_add_fusion.1.spot_ref, bf16[4,96,896]{2,1,0:T(8,128)(2,1)} %bitcast.48, bf16[8,4,96,128]{3,2,1,0:T(8,128)(2,1)} %copy-done.30, ...), custom_call_target="tpu_custom_call" | custom-call | flops 1620000000 | bytes 65536 | tf_op jit(solution)/shard_map/attend/pallas_call | solution.py:219
  74.5 2.1 multiply_reduce_fusion
  80.0 46.0 %mlp.1 = (f32[384,896]{1,0:T(8,128)}, f32[384,896]{1,0:T(8,128)}, f32[384,896]{1,0:T(8,128)}, f32[384,896]{1,0:T(8,128)}, bf16[2432,896]{1,0:T(8,128)(2,1)}, /*i...) custom-call(bf16[384,896]{1,0:T(8,128)(2,1)} %copy-done.4, ...), custom_call_target="tpu_custom_call" | custom-call | flops 3600000000 | bytes 65536 | tf_op jit(solution)/shard_map/mlp/pallas_call | solution.py:437
  129.3 2.2 fusion.4
  131.5 3.1 constant_dynamic-slice_fusion
  135.8 6.4 %middle_back.1 = (f32[384,896]{1,0:T(8,128)}, bf16[384,896]{1,0:T(8,128)(2,1)}, bf16[384,896]{1,0:T(8,128)(2,1)}, f32[1,896]{1,0:T(1,128)}) custom-call(f32[384,896]{1,0:T(8,128)} %get-tuple-element.198.bm_ref, f32[384,896]{1,0:T(8,128)} %copy-done.16, f32[384,896]{1,0:T(8,128)} %copy-done.1, bf16[384,896]{1,0:T(8,128)(2,1)} %bitcast.32, ...), custom_call_target="tpu_custom_call" | custom-call | flops 450000000 | bytes 65536 | tf_op jit(solution)/shard_map/middle_back/pallas_call | solution.py:472
  142.3 19.8 %attend_back.1 = (bf16[4,96,896]{2,1,0:T(8,128)(2,1)}, bf16[8,4,96,128]{3,2,1,0:T(8,128)(2,1)}, bf16[8,4,96,128]{3,2,1,0:T(8,128)(2,1)}, bf16[8,4,96,128]{3,2,1,0:T(8,128)(2,1)}, bf16[8,4,96,128]{3,2,1,0:T(8,128)(2,1)}) custom-call(s32[4]{0:T(128)} %add_select_fusion.1.low_ref, s32[1]{0:T(128)} %bitcast.1.me_ref, s32[4,16]{1,0:T(4,128)} %pad_add_fusion.1.spot_ref, ...), custom_call_target="tpu_custom_call" | custom-call | flops 2880000000 | bytes 65536 | tf_op jit(solution)/shard_map/attend_back/pallas_call | solution.py:338
  164.2 7.3 %attention_terms.1 = (bf16[896,896]{1,0:T(8,128)(2,1)}, bf16[896,896]{1,0:T(8,128)(2,1)}) custom-call(s32[1]{0:T(128)} %bitcast.9.core_ref, bf16[384,896]{1,0:T(8,128)(2,1)} %get-tuple-element.258.normed_ref, bf16[384,896]{1,0:T(8,128)(2,1)} %bitcast.47, bf16[384,896]{1,0:T(8,128)(2,1)} %bitcast.33, bf16[384,896]{1,0:T(8,128)(2,1)} %get-tuple-element.215.gb_ref, ...), custom_call_target="tpu_custom_call" | custom-call | flops 450000000 | bytes 65536 | tf_op jit(solution)/shard_map/attention_terms/pallas_call | solution.py:496
  171.5 5.0 %collective-permute-done.11 = bf16[448,2432]{1,0:T(8,128)(2,1)S(1)} collective-permute-done((bf16[448,2432]{1,0:T(8,128)(2,1)}, bf16[448,2432]{1,0:T(8,128)(2,1)S(1)}, u32[]{:S(2)}, u32[]{:S(2)}) %collective-permute-start.11) | collective-permute-done | bytes 2179104 | tf_op jit(solution)/shard_map/ppermute | solution.py:563
  178.9 2.6 add_convert_fusion.4
  181.5 12.9 %collective-permute-done.16 = bf16[3072,128]{1,0:T(8,128)(2,1)S(1)} collective-permute-done((bf16[3072,128]{1,0:T(8,128)(2,1)}, bf16[3072,128]{1,0:T(8,128)(2,1)S(1)}, u32[]{:S(2)}, u32[]{:S(2)}) %collective-permute-start.16) | collective-permute-done | bytes 786464 | tf_op jit(solution)/shard_map/ppermute | solution.py:563
  201.1 6.3 %collective-permute-done.19 = bf16[1536,128]{1,0:T(8,128)(2,1)} collective-permute-done((bf16[1536,128]{1,0:T(8,128)(2,1)}, bf16[1536,128]{1,0:T(8,128)(2,1)}, u32[]{:S(2)}, u32[]{:S(2)}) %collective-permute-start.19) | collective-permute-done | bytes 393248 | tf_op jit(solution)/shard_map/ppermute | solution.py:563
  216.0 5.0 %collective-permute-done.20 = bf16[768,256]{1,0:T(8,128)(2,1)S(1)} collective-permute-done((bf16[768,256]{1,0:T(8,128)(2,1)S(1)}, bf16[768,256]{1,0:T(8,128)(2,1)S(1)}, u32[]{:S(2)}, u32[]{:S(2)}) %collective-permute-start.20) | collective-permute-done | bytes 393248 | tf_op jit(solution)/shard_map/ppermute | solution.py:563
  221.9 12.5 %collective-permute-done.15 = bf16[224,2432]{1,0:T(8,128)(2,1)S(1)} collective-permute-done((bf16[224,2432]{1,0:T(8,128)(2,1)S(1)}, bf16[224,2432]{1,0:T(8,128)(2,1)S(1)}, u32[]{:S(2)}, u32[]{:S(2)}) %collective-permute-start.15) | collective-permute-done | bytes 1089568 | tf_op jit(solution)/shard_map/ppermute | solution.py:563
  234.4 8.7 %collective-permute-start.23 = (bf16[384,256]{1,0:T(8,128)(2,1)S(1)}, bf16[384,256]{1,0:T(8,128)(2,1)S(1)}, u32[]{:S(2)}, u32[]{:S(2)}) collective-permute-start(bf16[384,256]{1,0:T(8,128)(2,1)S(1)} %add_convert_fusion.19), channel_id=1, source_target_pairs={{0,16},{8,24},{16,0},{24,8},{1,17},{9,25},{17,1},{25,9},{2,18},{10... | collective-permute-start | bytes 589832 | tf_op jit(solution)/shard_map/ppermute | solution.py:563
  249.2 6.6 %collective-permute-done.24 = bf16[608,896]{1,0:T(8,128)(2,1)S(1)} collective-permute-done((bf16[608,896]{1,0:T(8,128)(2,1)S(1)}, bf16[608,896]{1,0:T(8,128)(2,1)S(1)}, u32[]{:S(2)}, u32[]{:S(2)}) %collective-permute-start.24) | collective-permute-done | bytes 1089568 | tf_op jit(solution)/shard_map/ppermute | solution.py:563
  259.7 5.6 %last_back.1 = (f32[384,896]{1,0:T(8,128)}, bf16[896,256]{1,0:T(8,128)(2,1)}, f32[1,2944]{1,0:T(1,128)}) custom-call(bf16[384,256]{1,0:T(8,128)(2,1)} %add_convert_fusion.18.gkv_ref, bf16[384,896]{1,0:T(8,128)(2,1)} %bitcast.34, bf16[896,1152]{1,0:T(8,128)(2,1)} %w_ref.4, bf16[384,896]{1,0:T(8,128)(2,1)} %bitcast.36, bf16[1,896]{1,0:T(2,128)(2,1)} %reshape.387.g_ref, ...), custom_call_target="tpu_custom_call" | custom-call | flops 540000000 | bytes 65536 | tf_op jit(solution)/shard_map/last_back/pallas_call | solution.py:529
  270.4 8.5 %collective-permute-start.34 = (bf16[56,4864]{1,0:T(8,128)(2,1)S(1)}, bf16[56,4864]{1,0:T(8,128)(2,1)S(1)}, u32[]{:S(2)}, u32[]{:S(2)}) collective-permute-start(bf16[56,4864]{1,0:T(8,128)(2,1)S(1)} %add_convert_fusion.8), channel_id=1, source_target_pairs={{0,16},{8,24},{16,0},{24,8},{1,17},{9,25},{17,1},{25,9},{2,18},{10... | collective-permute-start | bytes 1634312 | tf_op jit(solution)/shard_map/ppermute | solution.py:563
  282.5 6.8 %collective-permute-start.33 = (bf16[152,896]{1,0:T(8,128)(2,1)S(1)}, bf16[152,896]{1,0:T(8,128)(2,1)S(1)}, u32[]{:S(2)}, u32[]{:S(2)}) collective-permute-start(bf16[152,896]{1,0:T(8,128)(2,1)S(1)} %add_convert_fusion.16), channel_id=1, source_target_pairs={{0,16},{8,24},{16,0},{24,8},{1,17},{9,25},{17,1},{25,9},{2,18},{10... | collective-permute-start | bytes 817160 | tf_op jit(solution)/shard_map/ppermute | solution.py:563
  291.4 5.1 %collective-permute-done.29 = bf16[112,896]{1,0:T(8,128)(2,1)S(1)} collective-permute-done((bf16[112,896]{1,0:T(8,128)(2,1)S(1)}, bf16[112,896]{1,0:T(8,128)(2,1)S(1)}, u32[]{:S(2)}, u32[]{:S(2)}) %collective-permute-start.29) | collective-permute-done | bytes 200736 | tf_op jit(solution)/shard_map/ppermute | solution.py:563
  297.5 3.3 %collective-permute-done.35 = bf16[112,384]{1,0:T(8,128)(2,1)S(1)} collective-permute-done((bf16[112,384]{1,0:T(8,128)(2,1)S(1)}, bf16[112,384]{1,0:T(8,128)(2,1)S(1)}, u32[]{:S(2)}, u32[]{:S(2)}) %collective-permute-start.35) | collective-permute-done | bytes 86048 | tf_op jit(solution)/shard_map/ppermute | solution.py:563
  301.1 5.8 %collective-permute-done.33 = bf16[152,896]{1,0:T(8,128)(2,1)S(1)} collective-permute-done((bf16[152,896]{1,0:T(8,128)(2,1)S(1)}, bf16[152,896]{1,0:T(8,128)(2,1)S(1)}, u32[]{:S(2)}, u32[]{:S(2)}) %collective-permute-start.33) | collective-permute-done | bytes 272416 | tf_op jit(solution)/shard_map/ppermute | solution.py:563
  315.9 6.8 %collective-permute-start.42 = (bf16[152,896]{1,0:T(8,128)(2,1)S(1)}, bf16[152,896]{1,0:T(8,128)(2,1)S(1)}, u32[]{:S(2)}, u32[]{:S(2)}) collective-permute-start(bf16[152,896]{1,0:T(8,128)(2,1)S(1)} %collective-permute-done.41), channel_id=1, source_target_pairs={{0,1},{1,0},{2,3},{3,2},{4,5},{5,4},{6,7},{7,6},{8,9},{9,8},{10,11... | collective-permute-start | bytes 817160 | tf_op jit(solution)/shard_map/ppermute | solution.py:559
  (256 shorter events, 79.0 us)
Async XLA Ops:
  8.2 10.1 %collective-permute-start = (bf16[1,4,96,128]{3,2,1,0:T(8,128)(2,1)}, bf16[1,4,96,128]{3,2,1,0:T(8,128)(2,1)S(1)}, u32[]{:S(2)}, u32[]{:S(2)}) collective-permute-start(bf16[1,4,96,128]{3,2,1,0:T(8,128)(2,1)} %bitcast.52), channel_id=1, source_target_pairs={{0,8},{8,0},{16,24},{24,16},{1,9},{9,1},{17,25},{25,17},{2,10},{10... | collective-permute-start | bytes 294920 | tf_op jit(solution)/shard_map/ppermute | solution.py:563
  18.4 11.1 %collective-permute-start.1 = (bf16[2,4,96,128]{3,2,1,0:T(8,128)(2,1)S(1)}, bf16[2,4,96,128]{3,2,1,0:T(8,128)(2,1)S(1)}, u32[]{:S(2)}, u32[]{:S(2)}) collective-permute-start(bf16[2,4,96,128]{3,2,1,0:T(8,128)(2,1)S(1)} %constant_dynamic-update-slice_fusion), channel_id=1, source_target_pairs={{0,16},{8,24},{16,0},{24,8},{1,17},{9,25},{17,1},{25,9},{2,18},{10... | collective-permute-start | bytes 589832 | tf_op jit(solution)/shard_map/ppermute | solution.py:563
  18.9 12.3 %collective-permute-start.4 = (bf16[2,4,96,128]{3,2,1,0:T(8,128)(2,1)S(1)}, bf16[2,4,96,128]{3,2,1,0:T(8,128)(2,1)S(1)}, u32[]{:S(2)}, u32[]{:S(2)}) collective-permute-start(bf16[2,4,96,128]{3,2,1,0:T(8,128)(2,1)S(1)} %constant_dynamic-update-slice_fusion.2), channel_id=1, source_target_pairs={{0,8},{8,0},{16,24},{24,16},{1,9},{9,1},{17,25},{25,17},{2,10},{10... | collective-permute-start | bytes 589832 | tf_op jit(solution)/shard_map/ppermute | solution.py:563
  29.6 11.1 %collective-permute-start.3 = (bf16[4,4,96,128]{3,2,1,0:T(8,128)(2,1)S(1)}, bf16[4,4,96,128]{3,2,1,0:T(8,128)(2,1)S(1)}, u32[]{:S(2)}, u32[]{:S(2)}) collective-permute-start(bf16[4,4,96,128]{3,2,1,0:T(8,128)(2,1)S(1)} %constant_dynamic-update-slice_fusion.4), channel_id=1, source_target_pairs={{0,2},{2,0},{1,3},{3,1},{4,6},{6,4},{5,7},{7,5},{8,10},{10,8},{9,1... | collective-permute-start | bytes 1179656 | tf_op jit(solution)/shard_map/ppermute | solution.py:563
  31.2 11.2 %collective-permute-start.6 = (bf16[4,4,96,128]{3,2,1,0:T(8,128)(2,1)S(1)}, bf16[4,4,96,128]{3,2,1,0:T(8,128)(2,1)S(1)}, u32[]{:S(2)}, u32[]{:S(2)}) collective-permute-start(bf16[4,4,96,128]{3,2,1,0:T(8,128)(2,1)S(1)} %constant_dynamic-update-slice_fusion.6), channel_id=1, source_target_pairs={{0,4},{4,0},{1,5},{5,1},{2,6},{6,2},{3,7},{7,3},{8,12},{12,8},{9,1... | collective-permute-start | bytes 1179656 | tf_op jit(solution)/shard_map/ppermute | solution.py:563
  40.8 20.2 %collective-permute-start.5 = (bf16[8,4,96,128]{3,2,1,0:T(8,128)(2,1)S(1)}, bf16[8,4,96,128]{3,2,1,0:T(8,128)(2,1)}, u32[]{:S(2)}, u32[]{:S(2)}) collective-permute-start(bf16[8,4,96,128]{3,2,1,0:T(8,128)(2,1)S(1)} %constant_dynamic-update-slice_fusion.8.k1_ref), channel_id=1, source_target_pairs={{0,4},{4,0},{1,5},{5,1},{2,6},{6,2},{3,7},{7,3},{8,12},{12,8},{9,1... | collective-permute-start | bytes 2359304 | tf_op jit(solution)/shard_map/ppermute | solution.py:563
  42.5 18.5 %collective-permute-start.7 = (bf16[8,4,96,128]{3,2,1,0:T(8,128)(2,1)S(1)}, bf16[8,4,96,128]{3,2,1,0:T(8,128)(2,1)}, u32[]{:S(2)}, u32[]{:S(2)}) collective-permute-start(bf16[8,4,96,128]{3,2,1,0:T(8,128)(2,1)S(1)} %constant_dynamic-update-slice_fusion.10.v1_ref), channel_id=1, source_target_pairs={{0,2},{2,0},{1,3},{3,1},{4,6},{6,4},{5,7},{7,5},{8,10},{10,8},{9,1... | collective-permute-start | bytes 2359304 | tf_op jit(solution)/shard_map/ppermute | solution.py:563
  45.5 33.1 %collective-permute-start.9 = (bf16[384,896]{1,0:T(8,128)(2,1)S(1)}, bf16[384,896]{1,0:T(8,128)(2,1)}, u32[]{:S(2)}, u32[]{:S(2)}) collective-permute-start(bf16[384,896]{1,0:T(8,128)(2,1)S(1)} %bitcast.30), channel_id=1, source_target_pairs={{0,1},{1,0},{2,3},{3,2},{4,5},{5,4},{6,7},{7,6},{8,9},{9,8},{10,11... | collective-permute-start | bytes 2064392 | tf_op jit(solution)/shard_map/ppermute | solution.py:559
  126.0 50.5 %collective-permute-start.11 = (bf16[448,2432]{1,0:T(8,128)(2,1)}, bf16[448,2432]{1,0:T(8,128)(2,1)S(1)}, u32[]{:S(2)}, u32[]{:S(2)}) collective-permute-start(bf16[448,2432]{1,0:T(8,128)(2,1)} %get-tuple-element.193), channel_id=1, source_target_pairs={{0,2},{2,0},{1,3},{3,1},{4,6},{6,4},{5,7},{7,5},{8,10},{10,8},{9,1... | collective-permute-start | bytes 6537224 | tf_op jit(solution)/shard_map/ppermute | solution.py:563
  127.5 50.5 %collective-permute-start.14 = (bf16[448,2432]{1,0:T(8,128)(2,1)}, bf16[448,2432]{1,0:T(8,128)(2,1)}, u32[]{:S(2)}, u32[]{:S(2)}) collective-permute-start(bf16[448,2432]{1,0:T(8,128)(2,1)} %get-tuple-element.222), channel_id=1, source_target_pairs={{0,4},{4,0},{1,5},{5,1},{2,6},{6,2},{3,7},{7,3},{8,12},{12,8},{9,1... | collective-permute-start | bytes 6537224 | tf_op jit(solution)/shard_map/ppermute | solution.py:563
  134.7 76.9 %collective-permute-start.22 = (bf16[1216,896]{1,0:T(8,128)(2,1)}, bf16[1216,896]{1,0:T(8,128)(2,1)}, u32[]{:S(2)}, u32[]{:S(2)}) collective-permute-start(bf16[1216,896]{1,0:T(8,128)(2,1)} %constant_dynamic-slice_fusion), channel_id=1, source_target_pairs={{0,8},{8,0},{16,24},{24,16},{1,9},{9,1},{17,25},{25,17},{2,10},{10... | collective-permute-start | bytes 6537224 | tf_op jit(solution)/shard_map/ppermute | solution.py:563
  162.1 32.3 %collective-permute-start.16 = (bf16[3072,128]{1,0:T(8,128)(2,1)}, bf16[3072,128]{1,0:T(8,128)(2,1)S(1)}, u32[]{:S(2)}, u32[]{:S(2)}) collective-permute-start(bf16[3072,128]{1,0:T(8,128)(2,1)} %bitcast.59), channel_id=1, source_target_pairs={{0,4},{4,0},{1,5},{5,1},{2,6},{6,2},{3,7},{7,3},{8,12},{12,8},{9,1... | collective-permute-start | bytes 2359304 | tf_op jit(solution)/shard_map/ppermute | solution.py:563
  163.7 31.7 %collective-permute-start.18 = (bf16[3072,128]{1,0:T(8,128)(2,1)}, bf16[3072,128]{1,0:T(8,128)(2,1)S(1)}, u32[]{:S(2)}, u32[]{:S(2)}) collective-permute-start(bf16[3072,128]{1,0:T(8,128)(2,1)} %bitcast.58), channel_id=1, source_target_pairs={{0,2},{2,0},{1,3},{3,1},{4,6},{6,4},{5,7},{7,5},{8,10},{10,8},{9,1... | collective-permute-start | bytes 2359304 | tf_op jit(solution)/shard_map/ppermute | solution.py:563
  196.3 11.1 %collective-permute-start.19 = (bf16[1536,128]{1,0:T(8,128)(2,1)}, bf16[1536,128]{1,0:T(8,128)(2,1)}, u32[]{:S(2)}, u32[]{:S(2)}) collective-permute-start(bf16[1536,128]{1,0:T(8,128)(2,1)} %add_convert_fusion.13), channel_id=1, source_target_pairs={{0,4},{4,0},{1,5},{5,1},{2,6},{6,2},{3,7},{7,3},{8,12},{12,8},{9,1... | collective-permute-start | bytes 1179656 | tf_op jit(solution)/shard_map/ppermute | solution.py:563
  196.8 11.1 %collective-permute-start.17 = (bf16[1536,128]{1,0:T(8,128)(2,1)}, bf16[1536,128]{1,0:T(8,128)(2,1)}, u32[]{:S(2)}, u32[]{:S(2)}) collective-permute-start(bf16[1536,128]{1,0:T(8,128)(2,1)} %add_convert_fusion.14), channel_id=1, source_target_pairs={{0,2},{2,0},{1,3},{3,1},{4,6},{6,4},{5,7},{7,5},{8,10},{10,8},{9,1... | collective-permute-start | bytes 1179656 | tf_op jit(solution)/shard_map/ppermute | solution.py:563
  198.6 15.1 %collective-permute-start.21 = (bf16[896,896]{1,0:T(8,128)(2,1)}, bf16[896,896]{1,0:T(8,128)(2,1)S(1)}, u32[]{:S(2)}, u32[]{:S(2)}) collective-permute-start(bf16[896,896]{1,0:T(8,128)(2,1)} %get-tuple-element.217), channel_id=1, source_target_pairs={{0,1},{1,0},{2,3},{3,2},{4,5},{5,4},{6,7},{7,6},{8,9},{9,8},{10,11... | collective-permute-start | bytes 4816904 | tf_op jit(solution)/shard_map/ppermute | solution.py:559
  200.6 44.9 %collective-permute-start.10 = (f32[384,896]{1,0:T(8,128)}, f32[384,896]{1,0:T(8,128)S(1)}, u32[]{:S(2)}, u32[]{:S(2)}) collective-permute-start(f32[384,896]{1,0:T(8,128)} %get-tuple-element.191), channel_id=1, source_target_pairs={{0,1},{1,0},{2,3},{3,2},{4,5},{5,4},{6,7},{7,6},{8,9},{9,8},{10,11... | collective-permute-start | bytes 4128776 | tf_op jit(solution)/shard_map/ppermute | solution.py:559
  207.4 27.0 %collective-permute-start.15 = (bf16[224,2432]{1,0:T(8,128)(2,1)S(1)}, bf16[224,2432]{1,0:T(8,128)(2,1)S(1)}, u32[]{:S(2)}, u32[]{:S(2)}) collective-permute-start(bf16[224,2432]{1,0:T(8,128)(2,1)S(1)} %copy-done.17), channel_id=1, source_target_pairs={{0,2},{2,0},{1,3},{3,1},{4,6},{6,4},{5,7},{7,5},{8,10},{10,8},{9,1... | collective-permute-start | bytes 3268616 | tf_op jit(solution)/shard_map/ppermute | solution.py:563
  207.9 35.1 %collective-permute-start.13 = (bf16[224,2432]{1,0:T(8,128)(2,1)S(1)}, bf16[224,2432]{1,0:T(8,128)(2,1)S(1)}, u32[]{:S(2)}, u32[]{:S(2)}) collective-permute-start(bf16[224,2432]{1,0:T(8,128)(2,1)S(1)} %add_convert_fusion.5), channel_id=1, source_target_pairs={{0,4},{4,0},{1,5},{5,1},{2,6},{6,2},{3,7},{7,3},{8,12},{12,8},{9,1... | collective-permute-start | bytes 3268616 | tf_op jit(solution)/shard_map/ppermute | solution.py:563
  213.7 42.1 %collective-permute-start.24 = (bf16[608,896]{1,0:T(8,128)(2,1)S(1)}, bf16[608,896]{1,0:T(8,128)(2,1)S(1)}, u32[]{:S(2)}, u32[]{:S(2)}) collective-permute-start(bf16[608,896]{1,0:T(8,128)(2,1)S(1)} %add_convert_fusion.3), channel_id=1, source_target_pairs={{0,4},{4,0},{1,5},{5,1},{2,6},{6,2},{3,7},{7,3},{8,12},{12,8},{9,1... | collective-permute-start | bytes 3268616 | tf_op jit(solution)/shard_map/ppermute | solution.py:563
  221.0 46.9 %collective-permute-start.25 = (bf16[448,896]{1,0:T(8,128)(2,1)}, bf16[448,896]{1,0:T(8,128)(2,1)}, u32[]{:S(2)}, u32[]{:S(2)}) collective-permute-start(bf16[448,896]{1,0:T(8,128)(2,1)} %dynamic_slice.276), channel_id=1, source_target_pairs={{0,2},{2,0},{1,3},{3,1},{4,6},{6,4},{5,7},{7,5},{8,10},{10,8},{9,1... | collective-permute-start | bytes 2408456 | tf_op jit(solution)/shard_map/ppermute | solution.py:563
  234.4 14.1 %collective-permute-start.23 = (bf16[384,256]{1,0:T(8,128)(2,1)S(1)}, bf16[384,256]{1,0:T(8,128)(2,1)S(1)}, u32[]{:S(2)}, u32[]{:S(2)}) collective-permute-start(bf16[384,256]{1,0:T(8,128)(2,1)S(1)} %add_convert_fusion.19), channel_id=1, source_target_pairs={{0,16},{8,24},{16,0},{24,8},{1,17},{9,25},{17,1},{25,9},{2,18},{10... | collective-permute-start | bytes 589832 | tf_op jit(solution)/shard_map/ppermute | solution.py:563
  245.6 24.7 %collective-permute-start.28 = (bf16[112,4864]{1,0:T(8,128)(2,1)S(1)}, bf16[112,4864]{1,0:T(8,128)(2,1)S(1)}, u32[]{:S(2)}, u32[]{:S(2)}) collective-permute-start(bf16[112,4864]{1,0:T(8,128)(2,1)S(1)} %fusion.1), channel_id=1, source_target_pairs={{0,8},{8,0},{16,24},{24,16},{1,9},{9,1},{17,25},{25,17},{2,10},{10... | collective-permute-start | bytes 3268616 | tf_op jit(solution)/shard_map/ppermute | solution.py:563
  258.2 23.1 %collective-permute-start.31 = (bf16[304,896]{1,0:T(8,128)(2,1)S(1)}, bf16[304,896]{1,0:T(8,128)(2,1)S(1)}, u32[]{:S(2)}, u32[]{:S(2)}) collective-permute-start(bf16[304,896]{1,0:T(8,128)(2,1)S(1)} %add_convert_fusion.9), channel_id=1, source_target_pairs={{0,2},{2,0},{1,3},{3,1},{4,6},{6,4},{5,7},{7,5},{8,10},{10,8},{9,1... | collective-permute-start | bytes 1634312 | tf_op jit(solution)/shard_map/ppermute | solution.py:563
  267.3 11.6 %collective-permute-start.27 = (bf16[448,384]{1,0:T(8,128)(2,1)S(1)}, bf16[448,384]{1,0:T(8,128)(2,1)S(1)}, u32[]{:S(2)}, u32[]{:S(2)}) collective-permute-start(bf16[448,384]{1,0:T(8,128)(2,1)S(1)} %dynamic_slice.277), channel_id=1, source_target_pairs={{0,2},{2,0},{1,3},{3,1},{4,6},{6,4},{5,7},{7,5},{8,10},{10,8},{9,1... | collective-permute-start | bytes 1032200 | tf_op jit(solution)/shard_map/ppermute | solution.py:563
  269.0 11.2 %collective-permute-start.26 = (bf16[224,896]{1,0:T(8,128)(2,1)S(1)}, bf16[224,896]{1,0:T(8,128)(2,1)S(1)}, u32[]{:S(2)}, u32[]{:S(2)}) collective-permute-start(bf16[224,896]{1,0:T(8,128)(2,1)S(1)} %add_convert_fusion.10), channel_id=1, source_target_pairs={{0,4},{4,0},{1,5},{5,1},{2,6},{6,2},{3,7},{7,3},{8,12},{12,8},{9,1... | collective-permute-start | bytes 1204232 | tf_op jit(solution)/shard_map/ppermute | solution.py:563
  270.4 30.5 %collective-permute-start.34 = (bf16[56,4864]{1,0:T(8,128)(2,1)S(1)}, bf16[56,4864]{1,0:T(8,128)(2,1)S(1)}, u32[]{:S(2)}, u32[]{:S(2)}) collective-permute-start(bf16[56,4864]{1,0:T(8,128)(2,1)S(1)} %add_convert_fusion.8), channel_id=1, source_target_pairs={{0,16},{8,24},{16,0},{24,8},{1,17},{9,25},{17,1},{25,9},{2,18},{10... | collective-permute-start | bytes 1634312 | tf_op jit(solution)/shard_map/ppermute | solution.py:563
  278.9 10.3 %collective-permute-start.30 = (bf16[224,384]{1,0:T(8,128)(2,1)S(1)}, bf16[224,384]{1,0:T(8,128)(2,1)S(1)}, u32[]{:S(2)}, u32[]{:S(2)}) collective-permute-start(bf16[224,384]{1,0:T(8,128)(2,1)S(1)} %add_convert_fusion.20), channel_id=1, source_target_pairs={{0,4},{4,0},{1,5},{5,1},{2,6},{6,2},{3,7},{7,3},{8,12},{12,8},{9,1... | collective-permute-start | bytes 516104 | tf_op jit(solution)/shard_map/ppermute | solution.py:563
  281.2 15.2 %collective-permute-start.29 = (bf16[112,896]{1,0:T(8,128)(2,1)S(1)}, bf16[112,896]{1,0:T(8,128)(2,1)S(1)}, u32[]{:S(2)}, u32[]{:S(2)}) collective-permute-start(bf16[112,896]{1,0:T(8,128)(2,1)S(1)} %add_convert_fusion.17), channel_id=1, source_target_pairs={{0,8},{8,0},{16,24},{24,16},{1,9},{9,1},{17,25},{25,17},{2,10},{10... | collective-permute-start | bytes 602120 | tf_op jit(solution)/shard_map/ppermute | solution.py:563
  282.5 24.4 %collective-permute-start.33 = (bf16[152,896]{1,0:T(8,128)(2,1)S(1)}, bf16[152,896]{1,0:T(8,128)(2,1)S(1)}, u32[]{:S(2)}, u32[]{:S(2)}) collective-permute-start(bf16[152,896]{1,0:T(8,128)(2,1)S(1)} %add_convert_fusion.16), channel_id=1, source_target_pairs={{0,16},{8,24},{16,0},{24,8},{1,17},{9,25},{17,1},{25,9},{2,18},{10... | collective-permute-start | bytes 817160 | tf_op jit(solution)/shard_map/ppermute | solution.py:563
  289.3 11.4 %collective-permute-start.35 = (bf16[112,384]{1,0:T(8,128)(2,1)S(1)}, bf16[112,384]{1,0:T(8,128)(2,1)S(1)}, u32[]{:S(2)}, u32[]{:S(2)}) collective-permute-start(bf16[112,384]{1,0:T(8,128)(2,1)S(1)} %add_convert_fusion.23), channel_id=1, source_target_pairs={{0,8},{8,0},{16,24},{24,16},{1,9},{9,1},{17,25},{25,17},{2,10},{10... | collective-permute-start | bytes 258056 | tf_op jit(solution)/shard_map/ppermute | solution.py:563
  297.4 12.1 %collective-permute-start.32 = (bf16[56,896]{1,0:T(8,128)(2,1)S(1)}, bf16[56,896]{1,0:T(8,128)(2,1)S(1)}, u32[]{:S(2)}, u32[]{:S(2)}) collective-permute-start(bf16[56,896]{1,0:T(8,128)(2,1)S(1)} %add_convert_fusion.22), channel_id=1, source_target_pairs={{0,16},{8,24},{16,0},{24,8},{1,17},{9,25},{17,1},{25,9},{2,18},{10... | collective-permute-start | bytes 301064 | tf_op jit(solution)/shard_map/ppermute | solution.py:563
  (53 other events, 496.7 us)

commit v3 on v2

--- a/solution.py
+++ b/solution.py
@@ -932,7 +932,7 @@
 PARTS = 1
 PLAN = (
     "ab:0", "terms", "gu:0", "gu:1", "keys:0:0", "keys:0:1", "keys:0", "down", "attn0", "keys:0", "gu",
-    "finish", "keys:0", "down", "last", "attn", "gu", "kv", "attn", "down", "kv", "attn", "kv", "gu", "down",
+    "finish", "keys:0", "attn", "down", "last", "gu", "kv", "attn", "down", "kv", "attn", "kv", "gu", "down",
     "attn", "kv",
 )
 

time: 329 us -> 330 us (level)
  starting transfers between devices: 63.9 us -> 68.2 us
    ppermute x32, starting transfers between devices: 53.8 us -> 58.2 us  [pair_up(): lax.ppermute(a, axis, [(i, i ^ step) for i in range(lax.axis_size(axis))])]
    unnamed x91 -> x95, local copies, waits for them, and re-layouts: 7.61 us -> 7.64 us
  transfers between devices with their start and end apart: 43 -> 43, of which waited for: 18 -> 19; matrix products, arithmetic and copies ran while one was open for 17% -> 17% of each run, Pallas kernels for 17% -> 17%
where the time goes in v3:
time: 330 us; the launch traced here: 327 us
  Pallas kernels  106 us (32%)
  waiting for transfers between devices  82.5 us (25%)
  starting transfers between devices  68.2 us (21%)
  other arithmetic  36.2 us (11%)
  local copies, waits for them, and re-layouts  28.2 us (9%)
  matrix products  4.09 us (1%)
    ppermute x32, waiting for transfers between devices, pair_up(): lax.ppermute(a, axis, [(i, i ^ step) for i in range(lax.axis_size(axis))])  81 us
    ppermute x32, starting transfers between devices, pair_up(): lax.ppermute(a, axis, [(i, i ^ step) for i in range(lax.axis_size(axis))])  58.2 us
    pallas_call x1, Pallas kernels, mlp(): pl.pallas_call(functools.partial(mlp_kernel, half), grid=(pl.cdiv(half, T...  46 us
    convert_element_type x26, other arithmetic, total(): functools.reduce(lambda a, b: a + b, [a.astype(F32) for a in terms])  20.7 us
    pallas_call x1, Pallas kernels, attend_back(): pl.pallas_call(functools.partial(backward_kernel, first), grid_spec=pltpu...  19.8 us
    pallas_call x1, Pallas kernels, attend(): pl.pallas_call(forward_kernel, grid_spec=pltpu.PrefetchScalarGridSpec(num...  13.5 us
    dynamic_slice x2, local copies, waits for them, and re-layouts, shards(): lax.dynamic_slice_in_dim(w, first + core * half, half, 1)  9.7 us
    ppermute x10, starting transfers between devices, other_core(): return lax.ppermute(a, 'dp', [(0, 1), (1, 0)])  9.35 us
  transfers between devices with their start and end apart: 43, of which 19 were waited for; matrix products, arithmetic and copies ran while one was open for 17% of the time, Pallas kernels for 17%

profile of v3, /device:TPU:0, one launch (start us, length us, event | category | flops | bytes accessed | tf_op | source)
XLA Modules:
  0.0 326.7 jit_solution(11129154972045011671)
XLA Ops:
  4.8 3.4 %project_kv.1 = (bf16[384,896]{1,0:T(8,128)(2,1)}, bf16[384,128]{1,0:T(8,128)(2,1)}, bf16[384,128]{1,0:T(8,128)(2,1)}) custom-call(bf16[384,896]{1,0:T(8,128)(2,1)} %bitcast.35, bf16[896,1152]{1,0:T(8,128)(2,1)} %w_ref.4, bf16[1,2048]{1,0:T(2,128)(2,1)} %reshape.374.small_ref.b_ref, f32[384,128]{1,0:T(8,128)} %get-tuple-element.269.cos_ref, ...), custom_call_target="tpu_custom_call" | custom-call | flops 270000000 | bytes 65536 | tf_op jit(solution)/shard_map/project_kv/pallas_call | solution.py:89
  8.2 3.1 collective-permute-start
  11.3 2.6 collective-permute-start.2
  14.3 4.0 %project_q.1 = bf16[384,896]{1,0:T(8,128)(2,1)} custom-call(bf16[384,896]{1,0:T(8,128)(2,1)} %get-tuple-element.258.normed_ref, bf16[896,1152]{1,0:T(8,128)(2,1)} %w_ref.4, bf16[1,2048]{1,0:T(2,128)(2,1)} %reshape.374.small_ref.b_ref, f32[384,128]{1,0:T(8,128)} %get-tuple-element.269.cos_ref, f32[384,128]{1,0:T(8,128)} %get-tuple-element.270.sin_ref), custom_call_target="tpu_custom_call" | custom-call | flops 360000000 | bytes 65536 | tf_op jit(solution)/shard_map/project_q/pallas_call | solution.py:125
  20.2 5.0 %constant_dynamic-slice_fusion.3.wg_ref = bf16[896,2432]{1,0:T(8,128)(2,1)} fusion(bf16[896,9728]{1,0:T(8,128)(2,1)} %param.17, s32[]{:T(128)S(6)} %select_n.255), kind=kLoop, calls=%fused_computation.96 | loop fusion | bytes 8716292 | tf_op jit(solution)/shard_map/dynamic_slice | solution.py:766
  25.2 4.3 %collective-permute-done.1 = bf16[2,4,96,128]{3,2,1,0:T(8,128)(2,1)S(1)} collective-permute-done((bf16[2,4,96,128]{3,2,1,0:T(8,128)(2,1)S(1)}, bf16[2,4,96,128]{3,2,1,0:T(8,128)(2,1)S(1)}, u32[]{:S(2)}, u32[]{:S(2)}) %collective-permute-start.1) | collective-permute-done | bytes 196640 | tf_op jit(solution)/shard_map/ppermute | solution.py:563
  32.8 4.7 %constant_dynamic-slice_fusion.2.wu_ref = bf16[896,2432]{1,0:T(8,128)(2,1)} fusion(bf16[896,9728]{1,0:T(8,128)(2,1)} %param.17, s32[]{:T(128)S(6)} %select_n.256), kind=kLoop, calls=%fused_computation.95 | loop fusion | bytes 8716292 | tf_op jit(solution)/shard_map/dynamic_slice | solution.py:766
  37.5 2.4 constant_dynamic-slice_fusion.1.wd_ref
  46.2 14.8 %collective-permute-done.7.v2_ref = bf16[8,4,96,128]{3,2,1,0:T(8,128)(2,1)} collective-permute-done((bf16[8,4,96,128]{3,2,1,0:T(8,128)(2,1)S(1)}, bf16[8,4,96,128]{3,2,1,0:T(8,128)(2,1)}, u32[]{:S(2)}, u32[]{:S(2)}) %collective-permute-start.7) | collective-permute-done | bytes 786464 | tf_op jit(solution)/shard_map/ppermute | solution.py:563
  61.0 13.5 %attend.1 = (bf16[4,96,896]{2,1,0:T(8,128)(2,1)}, f32[4,2,768]{2,1,0:T(2,128)}) custom-call(s32[4]{0:T(128)} %add_select_fusion.1.low_ref, s32[1]{0:T(128)} %bitcast.1.me_ref, s32[4,16]{1,0:T(4,128)} %pad_add_fusion.1.spot_ref, bf16[4,96,896]{2,1,0:T(8,128)(2,1)} %bitcast.48, bf16[8,4,96,128]{3,2,1,0:T(8,128)(2,1)} %copy-done.32, ...), custom_call_target="tpu_custom_call" | custom-call | flops 1620000000 | bytes 65536 | tf_op jit(solution)/shard_map/attend/pallas_call | solution.py:219
  74.5 2.1 multiply_reduce_fusion
  80.0 46.0 %mlp.1 = (f32[384,896]{1,0:T(8,128)}, f32[384,896]{1,0:T(8,128)}, f32[384,896]{1,0:T(8,128)}, f32[384,896]{1,0:T(8,128)}, bf16[2432,896]{1,0:T(8,128)(2,1)}, /*i...) custom-call(bf16[384,896]{1,0:T(8,128)(2,1)} %copy-done.4, ...), custom_call_target="tpu_custom_call" | custom-call | flops 3600000000 | bytes 65536 | tf_op jit(solution)/shard_map/mlp/pallas_call | solution.py:437
  129.3 2.2 fusion.4
  131.5 3.1 constant_dynamic-slice_fusion
  135.8 6.5 %middle_back.1 = (f32[384,896]{1,0:T(8,128)}, bf16[384,896]{1,0:T(8,128)(2,1)}, bf16[384,896]{1,0:T(8,128)(2,1)}, f32[1,896]{1,0:T(1,128)}) custom-call(f32[384,896]{1,0:T(8,128)} %get-tuple-element.198.bm_ref, f32[384,896]{1,0:T(8,128)} %copy-done.16, f32[384,896]{1,0:T(8,128)} %copy-done.1, bf16[384,896]{1,0:T(8,128)(2,1)} %bitcast.32, ...), custom_call_target="tpu_custom_call" | custom-call | flops 450000000 | bytes 65536 | tf_op jit(solution)/shard_map/middle_back/pallas_call | solution.py:472
  142.3 19.8 %attend_back.1 = (bf16[4,96,896]{2,1,0:T(8,128)(2,1)}, bf16[8,4,96,128]{3,2,1,0:T(8,128)(2,1)}, bf16[8,4,96,128]{3,2,1,0:T(8,128)(2,1)}, bf16[8,4,96,128]{3,2,1,0:T(8,128)(2,1)}, bf16[8,4,96,128]{3,2,1,0:T(8,128)(2,1)}) custom-call(s32[4]{0:T(128)} %add_select_fusion.1.low_ref, s32[1]{0:T(128)} %bitcast.1.me_ref, s32[4,16]{1,0:T(4,128)} %pad_add_fusion.1.spot_ref, ...), custom_call_target="tpu_custom_call" | custom-call | flops 2880000000 | bytes 65536 | tf_op jit(solution)/shard_map/attend_back/pallas_call | solution.py:338
  164.2 7.3 %attention_terms.1 = (bf16[896,896]{1,0:T(8,128)(2,1)}, bf16[896,896]{1,0:T(8,128)(2,1)}) custom-call(s32[1]{0:T(128)} %bitcast.9.core_ref, bf16[384,896]{1,0:T(8,128)(2,1)} %get-tuple-element.258.normed_ref, bf16[384,896]{1,0:T(8,128)(2,1)} %bitcast.47, bf16[384,896]{1,0:T(8,128)(2,1)} %bitcast.33, bf16[384,896]{1,0:T(8,128)(2,1)} %get-tuple-element.215.gb_ref, ...), custom_call_target="tpu_custom_call" | custom-call | flops 450000000 | bytes 65536 | tf_op jit(solution)/shard_map/attention_terms/pallas_call | solution.py:496
  171.5 5.0 %collective-permute-done.11 = bf16[448,2432]{1,0:T(8,128)(2,1)S(1)} collective-permute-done((bf16[448,2432]{1,0:T(8,128)(2,1)}, bf16[448,2432]{1,0:T(8,128)(2,1)S(1)}, u32[]{:S(2)}, u32[]{:S(2)}) %collective-permute-start.11) | collective-permute-done | bytes 2179104 | tf_op jit(solution)/shard_map/ppermute | solution.py:563
  178.9 2.6 add_convert_fusion.4
  181.5 12.9 %collective-permute-done.16 = bf16[3072,128]{1,0:T(8,128)(2,1)S(1)} collective-permute-done((bf16[3072,128]{1,0:T(8,128)(2,1)}, bf16[3072,128]{1,0:T(8,128)(2,1)S(1)}, u32[]{:S(2)}, u32[]{:S(2)}) %collective-permute-start.16) | collective-permute-done | bytes 786464 | tf_op jit(solution)/shard_map/ppermute | solution.py:563
  201.1 6.3 %collective-permute-done.19 = bf16[1536,128]{1,0:T(8,128)(2,1)} collective-permute-done((bf16[1536,128]{1,0:T(8,128)(2,1)}, bf16[1536,128]{1,0:T(8,128)(2,1)}, u32[]{:S(2)}, u32[]{:S(2)}) %collective-permute-start.19) | collective-permute-done | bytes 393248 | tf_op jit(solution)/shard_map/ppermute | solution.py:563
  215.1 5.9 %collective-permute-done.20 = bf16[768,256]{1,0:T(8,128)(2,1)S(1)} collective-permute-done((bf16[768,256]{1,0:T(8,128)(2,1)S(1)}, bf16[768,256]{1,0:T(8,128)(2,1)S(1)}, u32[]{:S(2)}, u32[]{:S(2)}) %collective-permute-start.20) | collective-permute-done | bytes 393248 | tf_op jit(solution)/shard_map/ppermute | solution.py:563
  221.9 12.5 %collective-permute-done.15 = bf16[224,2432]{1,0:T(8,128)(2,1)S(1)} collective-permute-done((bf16[224,2432]{1,0:T(8,128)(2,1)S(1)}, bf16[224,2432]{1,0:T(8,128)(2,1)S(1)}, u32[]{:S(2)}, u32[]{:S(2)}) %collective-permute-start.15) | collective-permute-done | bytes 1089568 | tf_op jit(solution)/shard_map/ppermute | solution.py:563
  234.4 8.8 %collective-permute-start.23 = (bf16[384,256]{1,0:T(8,128)(2,1)S(1)}, bf16[384,256]{1,0:T(8,128)(2,1)S(1)}, u32[]{:S(2)}, u32[]{:S(2)}) collective-permute-start(bf16[384,256]{1,0:T(8,128)(2,1)S(1)} %add_convert_fusion.19), channel_id=1, source_target_pairs={{0,16},{8,24},{16,0},{24,8},{1,17},{9,25},{17,1},{25,9},{2,18},{10... | collective-permute-start | bytes 589832 | tf_op jit(solution)/shard_map/ppermute | solution.py:563
  250.9 7.4 %collective-permute-done.24 = bf16[608,896]{1,0:T(8,128)(2,1)S(1)} collective-permute-done((bf16[608,896]{1,0:T(8,128)(2,1)S(1)}, bf16[608,896]{1,0:T(8,128)(2,1)S(1)}, u32[]{:S(2)}, u32[]{:S(2)}) %collective-permute-start.24) | collective-permute-done | bytes 1089568 | tf_op jit(solution)/shard_map/ppermute | solution.py:563
  262.2 5.6 %last_back.1 = (f32[384,896]{1,0:T(8,128)}, bf16[896,256]{1,0:T(8,128)(2,1)}, f32[1,2944]{1,0:T(1,128)}) custom-call(bf16[384,256]{1,0:T(8,128)(2,1)} %add_convert_fusion.18.gkv_ref, bf16[384,896]{1,0:T(8,128)(2,1)} %bitcast.34, bf16[896,1152]{1,0:T(8,128)(2,1)} %w_ref.4, bf16[384,896]{1,0:T(8,128)(2,1)} %bitcast.36, bf16[1,896]{1,0:T(2,128)(2,1)} %reshape.387.g_ref, ...), custom_call_target="tpu_custom_call" | custom-call | flops 540000000 | bytes 65536 | tf_op jit(solution)/shard_map/last_back/pallas_call | solution.py:529
  270.6 8.4 %collective-permute-start.34 = (bf16[56,4864]{1,0:T(8,128)(2,1)S(1)}, bf16[56,4864]{1,0:T(8,128)(2,1)S(1)}, u32[]{:S(2)}, u32[]{:S(2)}) collective-permute-start(bf16[56,4864]{1,0:T(8,128)(2,1)S(1)} %add_convert_fusion.8), channel_id=1, source_target_pairs={{0,16},{8,24},{16,0},{24,8},{1,17},{9,25},{17,1},{25,9},{2,18},{10... | collective-permute-start | bytes 1634312 | tf_op jit(solution)/shard_map/ppermute | solution.py:563
  279.0 2.1 collective-permute-start.30
  283.4 6.9 %collective-permute-start.33 = (bf16[152,896]{1,0:T(8,128)(2,1)S(1)}, bf16[152,896]{1,0:T(8,128)(2,1)S(1)}, u32[]{:S(2)}, u32[]{:S(2)}) collective-permute-start(bf16[152,896]{1,0:T(8,128)(2,1)S(1)} %add_convert_fusion.16), channel_id=1, source_target_pairs={{0,16},{8,24},{16,0},{24,8},{1,17},{9,25},{17,1},{25,9},{2,18},{10... | collective-permute-start | bytes 817160 | tf_op jit(solution)/shard_map/ppermute | solution.py:563
  294.7 2.7 collective-permute-start.32
  302.9 5.5 %collective-permute-done.33 = bf16[152,896]{1,0:T(8,128)(2,1)S(1)} collective-permute-done((bf16[152,896]{1,0:T(8,128)(2,1)S(1)}, bf16[152,896]{1,0:T(8,128)(2,1)S(1)}, u32[]{:S(2)}, u32[]{:S(2)}) %collective-permute-start.33) | collective-permute-done | bytes 272416 | tf_op jit(solution)/shard_map/ppermute | solution.py:563
  316.1 6.8 %collective-permute-start.42 = (bf16[152,896]{1,0:T(8,128)(2,1)S(1)}, bf16[152,896]{1,0:T(8,128)(2,1)S(1)}, u32[]{:S(2)}, u32[]{:S(2)}) collective-permute-start(bf16[152,896]{1,0:T(8,128)(2,1)S(1)} %collective-permute-done.41), channel_id=1, source_target_pairs={{0,1},{1,0},{2,3},{3,2},{4,5},{5,4},{6,7},{7,6},{8,9},{9,8},{10,11... | collective-permute-start | bytes 817160 | tf_op jit(solution)/shard_map/ppermute | solution.py:559
  (260 shorter events, 81.1 us)
Async XLA Ops:
  8.2 10.1 %collective-permute-start = (bf16[1,4,96,128]{3,2,1,0:T(8,128)(2,1)}, bf16[1,4,96,128]{3,2,1,0:T(8,128)(2,1)S(1)}, u32[]{:S(2)}, u32[]{:S(2)}) collective-permute-start(bf16[1,4,96,128]{3,2,1,0:T(8,128)(2,1)} %bitcast.52), channel_id=1, source_target_pairs={{0,8},{8,0},{16,24},{24,16},{1,9},{9,1},{17,25},{25,17},{2,10},{10... | collective-permute-start | bytes 294920 | tf_op jit(solution)/shard_map/ppermute | solution.py:563
  18.4 11.1 %collective-permute-start.1 = (bf16[2,4,96,128]{3,2,1,0:T(8,128)(2,1)S(1)}, bf16[2,4,96,128]{3,2,1,0:T(8,128)(2,1)S(1)}, u32[]{:S(2)}, u32[]{:S(2)}) collective-permute-start(bf16[2,4,96,128]{3,2,1,0:T(8,128)(2,1)S(1)} %constant_dynamic-update-slice_fusion), channel_id=1, source_target_pairs={{0,16},{8,24},{16,0},{24,8},{1,17},{9,25},{17,1},{25,9},{2,18},{10... | collective-permute-start | bytes 589832 | tf_op jit(solution)/shard_map/ppermute | solution.py:563
  18.9 12.3 %collective-permute-start.4 = (bf16[2,4,96,128]{3,2,1,0:T(8,128)(2,1)S(1)}, bf16[2,4,96,128]{3,2,1,0:T(8,128)(2,1)S(1)}, u32[]{:S(2)}, u32[]{:S(2)}) collective-permute-start(bf16[2,4,96,128]{3,2,1,0:T(8,128)(2,1)S(1)} %constant_dynamic-update-slice_fusion.2), channel_id=1, source_target_pairs={{0,8},{8,0},{16,24},{24,16},{1,9},{9,1},{17,25},{25,17},{2,10},{10... | collective-permute-start | bytes 589832 | tf_op jit(solution)/shard_map/ppermute | solution.py:563
  29.6 11.1 %collective-permute-start.3 = (bf16[4,4,96,128]{3,2,1,0:T(8,128)(2,1)S(1)}, bf16[4,4,96,128]{3,2,1,0:T(8,128)(2,1)S(1)}, u32[]{:S(2)}, u32[]{:S(2)}) collective-permute-start(bf16[4,4,96,128]{3,2,1,0:T(8,128)(2,1)S(1)} %constant_dynamic-update-slice_fusion.4), channel_id=1, source_target_pairs={{0,2},{2,0},{1,3},{3,1},{4,6},{6,4},{5,7},{7,5},{8,10},{10,8},{9,1... | collective-permute-start | bytes 1179656 | tf_op jit(solution)/shard_map/ppermute | solution.py:563
  31.2 11.2 %collective-permute-start.6 = (bf16[4,4,96,128]{3,2,1,0:T(8,128)(2,1)S(1)}, bf16[4,4,96,128]{3,2,1,0:T(8,128)(2,1)S(1)}, u32[]{:S(2)}, u32[]{:S(2)}) collective-permute-start(bf16[4,4,96,128]{3,2,1,0:T(8,128)(2,1)S(1)} %constant_dynamic-update-slice_fusion.6), channel_id=1, source_target_pairs={{0,4},{4,0},{1,5},{5,1},{2,6},{6,2},{3,7},{7,3},{8,12},{12,8},{9,1... | collective-permute-start | bytes 1179656 | tf_op jit(solution)/shard_map/ppermute | solution.py:563
  40.8 20.2 %collective-permute-start.5 = (bf16[8,4,96,128]{3,2,1,0:T(8,128)(2,1)S(1)}, bf16[8,4,96,128]{3,2,1,0:T(8,128)(2,1)}, u32[]{:S(2)}, u32[]{:S(2)}) collective-permute-start(bf16[8,4,96,128]{3,2,1,0:T(8,128)(2,1)S(1)} %constant_dynamic-update-slice_fusion.8.k1_ref), channel_id=1, source_target_pairs={{0,4},{4,0},{1,5},{5,1},{2,6},{6,2},{3,7},{7,3},{8,12},{12,8},{9,1... | collective-permute-start | bytes 2359304 | tf_op jit(solution)/shard_map/ppermute | solution.py:563
  42.5 18.5 %collective-permute-start.7 = (bf16[8,4,96,128]{3,2,1,0:T(8,128)(2,1)S(1)}, bf16[8,4,96,128]{3,2,1,0:T(8,128)(2,1)}, u32[]{:S(2)}, u32[]{:S(2)}) collective-permute-start(bf16[8,4,96,128]{3,2,1,0:T(8,128)(2,1)S(1)} %constant_dynamic-update-slice_fusion.10.v1_ref), channel_id=1, source_target_pairs={{0,2},{2,0},{1,3},{3,1},{4,6},{6,4},{5,7},{7,5},{8,10},{10,8},{9,1... | collective-permute-start | bytes 2359304 | tf_op jit(solution)/shard_map/ppermute | solution.py:563
  45.5 33.1 %collective-permute-start.9 = (bf16[384,896]{1,0:T(8,128)(2,1)S(1)}, bf16[384,896]{1,0:T(8,128)(2,1)}, u32[]{:S(2)}, u32[]{:S(2)}) collective-permute-start(bf16[384,896]{1,0:T(8,128)(2,1)S(1)} %bitcast.30), channel_id=1, source_target_pairs={{0,1},{1,0},{2,3},{3,2},{4,5},{5,4},{6,7},{7,6},{8,9},{9,8},{10,11... | collective-permute-start | bytes 2064392 | tf_op jit(solution)/shard_map/ppermute | solution.py:559
  126.0 50.5 %collective-permute-start.11 = (bf16[448,2432]{1,0:T(8,128)(2,1)}, bf16[448,2432]{1,0:T(8,128)(2,1)S(1)}, u32[]{:S(2)}, u32[]{:S(2)}) collective-permute-start(bf16[448,2432]{1,0:T(8,128)(2,1)} %get-tuple-element.193), channel_id=1, source_target_pairs={{0,2},{2,0},{1,3},{3,1},{4,6},{6,4},{5,7},{7,5},{8,10},{10,8},{9,1... | collective-permute-start | bytes 6537224 | tf_op jit(solution)/shard_map/ppermute | solution.py:563
  127.5 50.5 %collective-permute-start.14 = (bf16[448,2432]{1,0:T(8,128)(2,1)}, bf16[448,2432]{1,0:T(8,128)(2,1)}, u32[]{:S(2)}, u32[]{:S(2)}) collective-permute-start(bf16[448,2432]{1,0:T(8,128)(2,1)} %get-tuple-element.222), channel_id=1, source_target_pairs={{0,4},{4,0},{1,5},{5,1},{2,6},{6,2},{3,7},{7,3},{8,12},{12,8},{9,1... | collective-permute-start | bytes 6537224 | tf_op jit(solution)/shard_map/ppermute | solution.py:563
  134.7 76.9 %collective-permute-start.22 = (bf16[1216,896]{1,0:T(8,128)(2,1)}, bf16[1216,896]{1,0:T(8,128)(2,1)}, u32[]{:S(2)}, u32[]{:S(2)}) collective-permute-start(bf16[1216,896]{1,0:T(8,128)(2,1)} %constant_dynamic-slice_fusion), channel_id=1, source_target_pairs={{0,8},{8,0},{16,24},{24,16},{1,9},{9,1},{17,25},{25,17},{2,10},{10... | collective-permute-start | bytes 6537224 | tf_op jit(solution)/shard_map/ppermute | solution.py:563
  162.1 32.3 %collective-permute-start.16 = (bf16[3072,128]{1,0:T(8,128)(2,1)}, bf16[3072,128]{1,0:T(8,128)(2,1)S(1)}, u32[]{:S(2)}, u32[]{:S(2)}) collective-permute-start(bf16[3072,128]{1,0:T(8,128)(2,1)} %bitcast.59), channel_id=1, source_target_pairs={{0,4},{4,0},{1,5},{5,1},{2,6},{6,2},{3,7},{7,3},{8,12},{12,8},{9,1... | collective-permute-start | bytes 2359304 | tf_op jit(solution)/shard_map/ppermute | solution.py:563
  163.6 31.7 %collective-permute-start.18 = (bf16[3072,128]{1,0:T(8,128)(2,1)}, bf16[3072,128]{1,0:T(8,128)(2,1)S(1)}, u32[]{:S(2)}, u32[]{:S(2)}) collective-permute-start(bf16[3072,128]{1,0:T(8,128)(2,1)} %bitcast.58), channel_id=1, source_target_pairs={{0,2},{2,0},{1,3},{3,1},{4,6},{6,4},{5,7},{7,5},{8,10},{10,8},{9,1... | collective-permute-start | bytes 2359304 | tf_op jit(solution)/shard_map/ppermute | solution.py:563
  196.3 11.1 %collective-permute-start.19 = (bf16[1536,128]{1,0:T(8,128)(2,1)}, bf16[1536,128]{1,0:T(8,128)(2,1)}, u32[]{:S(2)}, u32[]{:S(2)}) collective-permute-start(bf16[1536,128]{1,0:T(8,128)(2,1)} %add_convert_fusion.13), channel_id=1, source_target_pairs={{0,4},{4,0},{1,5},{5,1},{2,6},{6,2},{3,7},{7,3},{8,12},{12,8},{9,1... | collective-permute-start | bytes 1179656 | tf_op jit(solution)/shard_map/ppermute | solution.py:563
  196.9 11.1 %collective-permute-start.17 = (bf16[1536,128]{1,0:T(8,128)(2,1)}, bf16[1536,128]{1,0:T(8,128)(2,1)}, u32[]{:S(2)}, u32[]{:S(2)}) collective-permute-start(bf16[1536,128]{1,0:T(8,128)(2,1)} %add_convert_fusion.14), channel_id=1, source_target_pairs={{0,2},{2,0},{1,3},{3,1},{4,6},{6,4},{5,7},{7,5},{8,10},{10,8},{9,1... | collective-permute-start | bytes 1179656 | tf_op jit(solution)/shard_map/ppermute | solution.py:563
  198.6 15.1 %collective-permute-start.21 = (bf16[896,896]{1,0:T(8,128)(2,1)}, bf16[896,896]{1,0:T(8,128)(2,1)S(1)}, u32[]{:S(2)}, u32[]{:S(2)}) collective-permute-start(bf16[896,896]{1,0:T(8,128)(2,1)} %get-tuple-element.217), channel_id=1, source_target_pairs={{0,1},{1,0},{2,3},{3,2},{4,5},{5,4},{6,7},{7,6},{8,9},{9,8},{10,11... | collective-permute-start | bytes 4816904 | tf_op jit(solution)/shard_map/ppermute | solution.py:559
  200.6 45.1 %collective-permute-start.10 = (f32[384,896]{1,0:T(8,128)}, f32[384,896]{1,0:T(8,128)S(1)}, u32[]{:S(2)}, u32[]{:S(2)}) collective-permute-start(f32[384,896]{1,0:T(8,128)} %get-tuple-element.191), channel_id=1, source_target_pairs={{0,1},{1,0},{2,3},{3,2},{4,5},{5,4},{6,7},{7,6},{8,9},{9,8},{10,11... | collective-permute-start | bytes 4128776 | tf_op jit(solution)/shard_map/ppermute | solution.py:559
  207.4 27.0 %collective-permute-start.15 = (bf16[224,2432]{1,0:T(8,128)(2,1)S(1)}, bf16[224,2432]{1,0:T(8,128)(2,1)S(1)}, u32[]{:S(2)}, u32[]{:S(2)}) collective-permute-start(bf16[224,2432]{1,0:T(8,128)(2,1)S(1)} %copy-done.17), channel_id=1, source_target_pairs={{0,2},{2,0},{1,3},{3,1},{4,6},{6,4},{5,7},{7,5},{8,10},{10,8},{9,1... | collective-permute-start | bytes 3268616 | tf_op jit(solution)/shard_map/ppermute | solution.py:563
  207.9 35.2 %collective-permute-start.13 = (bf16[224,2432]{1,0:T(8,128)(2,1)S(1)}, bf16[224,2432]{1,0:T(8,128)(2,1)S(1)}, u32[]{:S(2)}, u32[]{:S(2)}) collective-permute-start(bf16[224,2432]{1,0:T(8,128)(2,1)S(1)} %add_convert_fusion.5), channel_id=1, source_target_pairs={{0,4},{4,0},{1,5},{5,1},{2,6},{6,2},{3,7},{7,3},{8,12},{12,8},{9,1... | collective-permute-start | bytes 3268616 | tf_op jit(solution)/shard_map/ppermute | solution.py:563
  213.7 44.6 %collective-permute-start.24 = (bf16[608,896]{1,0:T(8,128)(2,1)S(1)}, bf16[608,896]{1,0:T(8,128)(2,1)S(1)}, u32[]{:S(2)}, u32[]{:S(2)}) collective-permute-start(bf16[608,896]{1,0:T(8,128)(2,1)S(1)} %add_convert_fusion.3), channel_id=1, source_target_pairs={{0,4},{4,0},{1,5},{5,1},{2,6},{6,2},{3,7},{7,3},{8,12},{12,8},{9,1... | collective-permute-start | bytes 3268616 | tf_op jit(solution)/shard_map/ppermute | solution.py:563
  221.0 28.4 %collective-permute-start.25 = (bf16[448,896]{1,0:T(8,128)(2,1)S(1)}, bf16[448,896]{1,0:T(8,128)(2,1)S(1)}, u32[]{:S(2)}, u32[]{:S(2)}) collective-permute-start(bf16[448,896]{1,0:T(8,128)(2,1)S(1)} %dynamic_slice.276), channel_id=1, source_target_pairs={{0,2},{2,0},{1,3},{3,1},{4,6},{6,4},{5,7},{7,5},{8,10},{10,8},{9,1... | collective-permute-start | bytes 2408456 | tf_op jit(solution)/shard_map/ppermute | solution.py:563
  234.4 14.1 %collective-permute-start.23 = (bf16[384,256]{1,0:T(8,128)(2,1)S(1)}, bf16[384,256]{1,0:T(8,128)(2,1)S(1)}, u32[]{:S(2)}, u32[]{:S(2)}) collective-permute-start(bf16[384,256]{1,0:T(8,128)(2,1)S(1)} %add_convert_fusion.19), channel_id=1, source_target_pairs={{0,16},{8,24},{16,0},{24,8},{1,17},{9,25},{17,1},{25,9},{2,18},{10... | collective-permute-start | bytes 589832 | tf_op jit(solution)/shard_map/ppermute | solution.py:563
  245.6 24.8 %collective-permute-start.28 = (bf16[112,4864]{1,0:T(8,128)(2,1)S(1)}, bf16[112,4864]{1,0:T(8,128)(2,1)S(1)}, u32[]{:S(2)}, u32[]{:S(2)}) collective-permute-start(bf16[112,4864]{1,0:T(8,128)(2,1)S(1)} %fusion.1), channel_id=1, source_target_pairs={{0,8},{8,0},{16,24},{24,16},{1,9},{9,1},{17,25},{25,17},{2,10},{10... | collective-permute-start | bytes 3268616 | tf_op jit(solution)/shard_map/ppermute | solution.py:563
  250.3 30.8 %collective-permute-start.26 = (bf16[224,896]{1,0:T(8,128)(2,1)}, bf16[224,896]{1,0:T(8,128)(2,1)}, u32[]{:S(2)}, u32[]{:S(2)}) collective-permute-start(bf16[224,896]{1,0:T(8,128)(2,1)} %add_convert_fusion.10), channel_id=1, source_target_pairs={{0,4},{4,0},{1,5},{5,1},{2,6},{6,2},{3,7},{7,3},{8,12},{12,8},{9,1... | collective-permute-start | bytes 1204232 | tf_op jit(solution)/shard_map/ppermute | solution.py:563
  260.7 21.5 %collective-permute-start.31 = (bf16[304,896]{1,0:T(8,128)(2,1)S(1)}, bf16[304,896]{1,0:T(8,128)(2,1)S(1)}, u32[]{:S(2)}, u32[]{:S(2)}) collective-permute-start(bf16[304,896]{1,0:T(8,128)(2,1)S(1)} %add_convert_fusion.9), channel_id=1, source_target_pairs={{0,2},{2,0},{1,3},{3,1},{4,6},{6,4},{5,7},{7,5},{8,10},{10,8},{9,1... | collective-permute-start | bytes 1634312 | tf_op jit(solution)/shard_map/ppermute | solution.py:563
  270.6 32.1 %collective-permute-start.34 = (bf16[56,4864]{1,0:T(8,128)(2,1)S(1)}, bf16[56,4864]{1,0:T(8,128)(2,1)S(1)}, u32[]{:S(2)}, u32[]{:S(2)}) collective-permute-start(bf16[56,4864]{1,0:T(8,128)(2,1)S(1)} %add_convert_fusion.8), channel_id=1, source_target_pairs={{0,16},{8,24},{16,0},{24,8},{1,17},{9,25},{17,1},{25,9},{2,18},{10... | collective-permute-start | bytes 1634312 | tf_op jit(solution)/shard_map/ppermute | solution.py:563
  279.0 11.3 %collective-permute-start.30 = (bf16[224,384]{1,0:T(8,128)(2,1)S(1)}, bf16[224,384]{1,0:T(8,128)(2,1)S(1)}, u32[]{:S(2)}, u32[]{:S(2)}) collective-permute-start(bf16[224,384]{1,0:T(8,128)(2,1)S(1)} %add_convert_fusion.20), channel_id=1, source_target_pairs={{0,4},{4,0},{1,5},{5,1},{2,6},{6,2},{3,7},{7,3},{8,12},{12,8},{9,1... | collective-permute-start | bytes 516104 | tf_op jit(solution)/shard_map/ppermute | solution.py:563
  282.1 11.6 %collective-permute-start.29 = (bf16[112,896]{1,0:T(8,128)(2,1)S(1)}, bf16[112,896]{1,0:T(8,128)(2,1)S(1)}, u32[]{:S(2)}, u32[]{:S(2)}) collective-permute-start(bf16[112,896]{1,0:T(8,128)(2,1)S(1)} %add_convert_fusion.17), channel_id=1, source_target_pairs={{0,8},{8,0},{16,24},{24,16},{1,9},{9,1},{17,25},{25,17},{2,10},{10... | collective-permute-start | bytes 602120 | tf_op jit(solution)/shard_map/ppermute | solution.py:563
  283.4 25.1 %collective-permute-start.33 = (bf16[152,896]{1,0:T(8,128)(2,1)S(1)}, bf16[152,896]{1,0:T(8,128)(2,1)S(1)}, u32[]{:S(2)}, u32[]{:S(2)}) collective-permute-start(bf16[152,896]{1,0:T(8,128)(2,1)S(1)} %add_convert_fusion.16), channel_id=1, source_target_pairs={{0,16},{8,24},{16,0},{24,8},{1,17},{9,25},{17,1},{25,9},{2,18},{10... | collective-permute-start | bytes 817160 | tf_op jit(solution)/shard_map/ppermute | solution.py:563
  294.7 15.0 %collective-permute-start.32 = (bf16[56,896]{1,0:T(8,128)(2,1)S(1)}, bf16[56,896]{1,0:T(8,128)(2,1)S(1)}, u32[]{:S(2)}, u32[]{:S(2)}) collective-permute-start(bf16[56,896]{1,0:T(8,128)(2,1)S(1)} %add_convert_fusion.22), channel_id=1, source_target_pairs={{0,16},{8,24},{16,0},{24,8},{1,17},{9,25},{17,1},{25,9},{2,18},{10... | collective-permute-start | bytes 301064 | tf_op jit(solution)/shard_map/ppermute | solution.py:563
  299.2 11.5 %collective-permute-start.37 = (bf16[56,384]{1,0:T(8,128)(2,1)S(1)}, bf16[56,384]{1,0:T(8,128)(2,1)S(1)}, u32[]{:S(2)}, u32[]{:S(2)}) collective-permute-start(bf16[56,384]{1,0:T(8,128)(2,1)S(1)} %add_convert_fusion.26), channel_id=1, source_target_pairs={{0,16},{8,24},{16,0},{24,8},{1,17},{9,25},{17,1},{25,9},{2,18},{10... | collective-permute-start | bytes 129032 | tf_op jit(solution)/shard_map/ppermute | solution.py:563
  313.3 9.6 %collective-permute-start.39 = (bf16[56,2432]{1,0:T(8,128)(2,1)S(1)}, bf16[56,2432]{1,0:T(8,128)(2,1)S(1)}, u32[]{:S(2)}, u32[]{:S(2)}) collective-permute-start(bf16[56,2432]{1,0:T(8,128)(2,1)S(1)} %slice.54), channel_id=1, source_target_pairs={{0,1},{1,0},{2,3},{3,2},{4,5},{5,4},{6,7},{7,6},{8,9},{9,8},{10,11... | collective-permute-start | bytes 817160 | tf_op jit(solution)/shard_map/ppermute | solution.py:559
  (55 other events, 518.1 us)
